TPU v7x, 128 devices: a whole 4x4x4 slice. The times are simulated.
128 devices in a mesh: ka: 16 (over x, y), ta: 8 (over z, core).
Axes of the slice: x: 4, y: 4, z: 4, core: 2. Of those that a mesh axis runs over, the one named last changes fastest.
Arguments:
- green: float32 [2, 256, 512, 128], P(None, 'ka', 'ta'), may hold values from -3 to 3
- energies: float32 [256], P('ka'), may hold values from -2 to 2
- reach: int32 [512], P('ta'), may hold values from 1 to 128, as said below
Outputs:
- evolved: float32 [2, 256, 512, 128], P(None, 'ka', 'ta')
Inputs may be any that keep to these rules, and one draw needn't show every extreme that they name: `reach`: at least one time reaches 128.
All inputs are finite; a program needn't handle non-finite values.
Results may differ from a plain program's by a relative error of at most 0.0013.
Values may be sent and summed in bfloat16 or wider, within the bound.
No kernel may reach another device: no remote copies, remote signals or barrier semaphores. Data moves between devices by JAX's collectives and lax.ppermute only.
A program may use at most 128 MiB of HBM per device.

v0:
```python
import jax
import jax.numpy as jnp
import numpy as np
from jax import lax
from jax.experimental import pallas as pl
from jax.experimental.pallas import tpu as pltpu
from jax.sharding import PartitionSpec as P

K = 256
MEM = 128
ROWS = 64
OWN = 16
GROUP = 16
PART = 4
KB = 4
STEPS = OWN // KB
MIB = 2**20

quadrature = 0.0625
step_size = 0.25

F32 = jnp.float32
BF16 = jnp.bfloat16


def tables(count):
    numbers = np.arange(count)
    phase = (numbers[:, None] * numbers[None, :] % count) * (2.0 * np.pi / count)
    both = np.concatenate([np.cos(phase), np.sin(phase)], 0) / np.sqrt(count)
    return jnp.asarray(both.astype(np.float32).astype(jnp.bfloat16))


def grids():
    row = lax.broadcasted_iota(jnp.int32, (ROWS, MEM), 0)
    lane = lax.broadcasted_iota(jnp.int32, (ROWS, MEM), 1)
    return row, lane


def turn_over(block):
    row, lane = grids()
    index = (row - lane) & (MEM - 1)
    pieces = [
        jnp.take_along_axis(block[i : i + 8], index[i : i + 8], axis=1) for i in range(0, ROWS, 8)
    ]
    return jnp.concatenate(pieces, 0)


def half_turn(block):
    return pltpu.roll(block, MEM // 2, 1)


def self_energy_kernel(keep, table, x, out, y, sems):
    def save(pair):
        here = pl.ds(2 * pair, 2)
        return pltpu.make_async_copy(y.at[:, :, here], out.at[:, :, here], sems.at[pair])

    both = table[...]
    for pair in range(2):
        fields = []
        for part in range(2):
            sides = [x[:, part, 2 * pair + i].reshape(K, MEM) for i in range(2)]
            rhs = jnp.concatenate(sides, 1)
            fields.append(jnp.dot(both, rhs, preferred_element_type=F32))
        re = fields[0][:K] - fields[1][K:]
        im = fields[0][K:] + fields[1][:K]
        weight = -(re * re + im * im)
        zr = (weight * re).astype(BF16)
        zi = (weight * im).astype(BF16)
        a = jnp.dot(both, zr, preferred_element_type=F32)
        b = jnp.dot(both, zi, preferred_element_type=F32)
        sigma = (a[:K] + b[K:], b[:K] - a[K:])
        for part in range(2):
            for i in range(2):
                side = sigma[part][:, i * MEM : (i + 1) * MEM]
                kept = keep[2 * pair + i : 2 * pair + i + 1, :] > 0
                side = jnp.where(kept, side, 0.0).astype(BF16)
                y[:, part, 2 * pair + i] = side.reshape(GROUP, OWN, MEM)
        save(pair).start()
    for pair in range(2):
        save(pair).wait()


CHUNK = (GROUP, 2, PART, OWN, MEM)
STATE = (2, OWN, ROWS, MEM)
FAR = (OWN, ROWS, MEM)
HBM = pl.BlockSpec(memory_space=pltpu.HBM)
SMEM = pl.BlockSpec(memory_space=pltpu.SMEM)
VMEM = pl.BlockSpec(memory_space=pltpu.VMEM)


def params(mib):
    return pltpu.CompilerParams(vmem_limit_bytes=int(mib * MIB))


def self_energy(keep, table, spread):
    return pl.pallas_call(
        self_energy_kernel,
        in_specs=[VMEM, VMEM, VMEM],
        out_specs=HBM,
        out_shape=pltpu.HBM(CHUNK, BF16),
        scratch_shapes=[pltpu.VMEM(CHUNK, BF16), pltpu.SemaphoreType.DMA((2,))],
        compiler_params=params(12),
        name="self_energy",
    )(keep, table, spread)


def piece(ref, q):
    here = pl.ds(q * KB, KB)
    return ref.at[here] if len(ref.shape) == 3 else ref.at[:, here]


def mover(pairs, sems, first):
    def move(n, q):
        source, target = pairs[n]
        return pltpu.make_async_copy(piece(source, q), piece(target, q), sems.at[first + n, q])

    return move


def send_chunk(turned, block, chunk, sem):
    for d in range(GROUP):
        for c in range(2):
            for j in range(PART):
                t = d * PART + j
                block[d, c, j] = turned[c, t * OWN : (t + 1) * OWN, :].astype(BF16)
    copy = pltpu.make_async_copy(block, chunk, sem)
    copy.start()
    return copy


def emit(k, value, turned, near, far):
    row, lane = grids()
    causal = lane <= row
    low = []
    for c in range(2):
        turned[c, pl.ds(k, ROWS, stride=OWN), :] = value[c]
        near[c, k] = value[c].astype(BF16)
        low.append(jnp.where(causal, value[c], 0.0))
    far[k] = (low[0] + half_turn(low[1])).astype(BF16)


def prepare_kernel(x_in, out, near, far, chunk, x, y, turned, block, sems, sem):
    load = mover([(x_in, x)], sems, 0)
    pairs = [(y, out)]
    save = mover(pairs, sems, 1)
    for q in range(STEPS):
        load(0, q).start()

    def step(q, carry):
        load(0, q).wait()
        for i in range(KB):
            k = q * KB + i
            value = [turn_over(x[c, k]) for c in range(2)]
            for c in range(2):
                y[c, k] = value[c]
            emit(k, value, turned, near, far)
        return carry

    lax.fori_loop(0, STEPS, step, 0)
    last = send_chunk(turned, block, chunk, sem)
    for n in range(len(pairs)):
        for q in range(STEPS):
            save(n, q).start()
    for n in range(len(pairs)):
        for q in range(STEPS):
            save(n, q).wait()
    last.wait()


WIDE = pltpu.HBM(STATE, F32)
EMITTED = [pltpu.VMEM(STATE, BF16), pltpu.VMEM(FAR, BF16), pltpu.HBM(CHUNK, BF16)]


def emitting():
    return [
        pltpu.VMEM(STATE, BF16),
        pltpu.VMEM(FAR, BF16),
        pltpu.VMEM((2, ROWS * OWN, MEM), F32),
        pltpu.VMEM(CHUNK, BF16),
    ]


def prepare(x):
    scratch = pltpu.VMEM(STATE, F32)
    return pl.pallas_call(
        prepare_kernel,
        in_specs=[HBM],
        out_specs=[HBM, VMEM, VMEM, HBM],
        out_shape=[WIDE] + EMITTED,
        scratch_shapes=[scratch, scratch]
        + emitting()[2:]
        + [pltpu.SemaphoreType.DMA((2, STEPS)), pltpu.SemaphoreType.DMA],
        compiler_params=params(16),
        name="prepare",
    )(pltpu.with_memory_space_constraint(x, pltpu.HBM))


def stage_kernel(first, last, *refs):
    refs = list(refs)
    energies, sigma, own, own_low, near, far, base_in = refs[:7]
    if last:
        out, base, result, held, sems = refs[7:]
    else:
        out, mine, low, chunk, base, result, held, sems, turned, block, chunk_sem = refs[7:]

    loads = [(base_in, base)]
    saves = [(result, out)]
    load = mover(loads, sems, 0)
    save = mover(saves, sems, len(loads))
    for q in range(STEPS):
        for n in range(len(loads)):
            load(n, q).start()

    for d in range(GROUP):
        for c in range(2):
            for j in range(PART):
                t = d * PART + j
                held[c, t * OWN : (t + 1) * OWN, :] = sigma[d, c, j].astype(F32)

    row, lane = grids()
    causal = lane <= row
    own_side = causal | (lane >= ROWS)
    seen = lane <= row + ROWS
    lower = lane < ROWS

    def only(kept, block):
        return jnp.where(kept, block, jnp.zeros_like(block))

    def step(q, carry):
        for n in range(len(loads)):
            load(n, q).wait()
        for i in range(KB):
            k = q * KB + i
            left = []
            for c in range(2):
                memory = held[c, pl.ds(k, ROWS, stride=OWN), :]
                inner = jnp.where(own_side, memory, 0.0).astype(BF16)
                outer = jnp.where(own_side, 0.0, memory).astype(BF16)
                left.append(jnp.concatenate([inner, outer[:, :ROWS]], 1))
            left = jnp.concatenate(left, 0)
            packed = far[k]
            away = (packed, half_turn(packed))
            sides = []
            for c in range(2):
                rows = [
                    only(~causal, own[c, k]),
                    only(seen, half_turn(near[c, k])),
                    only(lower, away[c]),
                ]
                sides.append(jnp.concatenate(rows, 0))
            early = jnp.dot(left, jnp.concatenate(sides, 1), preferred_element_type=F32)
            late = jnp.dot(left[:, :ROWS], own_low[k], preferred_element_type=F32)
            collide = (
                jnp.where(
                    causal,
                    late[:ROWS] - half_turn(late[ROWS:]),
                    early[:ROWS, :MEM] - early[ROWS:, MEM:],
                ),
                jnp.where(
                    causal,
                    late[ROWS:] + half_turn(late[:ROWS]),
                    early[ROWS:, :MEM] + early[:ROWS, MEM:],
                ),
            )
            collide = [quadrature * part for part in collide]
            half = 0.5 * step_size
            if first:
                energy = energies[k]
                xr, xi = base[0, k], base[1, k]
                fr = energy * xi + collide[1]
                fi = -(energy * xr + collide[0])
                value = (xr + step_size * fr, xi + step_size * fi)
                result[0, k] = xr + half * (fr + energy * value[1])
                result[1, k] = xi + half * (fi - energy * value[0])
            else:
                value = (base[0, k] + half * collide[1], base[1, k] - half * collide[0])
                for c in range(2):
                    result[c, k] = turn_over(value[c]) if last else value[c]
            if not last:
                emit(k, value, turned, mine, low)
        for n in range(len(saves)):
            save(n, q).start()
        return carry

    lax.fori_loop(0, STEPS, step, 0)
    if not last:
        send_chunk(turned, block, chunk, chunk_sem).wait()
    for q in range(STEPS):
        for n in range(len(saves)):
            save(n, q).wait()


def stage(first, last, energies, sigma, own, own_low, near, far, base):
    state = pltpu.VMEM(STATE, F32)
    scratch = [state, state, pltpu.VMEM((2, ROWS * OWN, MEM), F32)]
    scratch += [pltpu.SemaphoreType.DMA((2, STEPS))]
    out_shape, spaces = [WIDE], [HBM]
    if not last:
        out_shape += EMITTED
        spaces += [VMEM, VMEM, HBM]
        scratch += emitting()[2:] + [pltpu.SemaphoreType.DMA]

    def kernel(*refs):
        stage_kernel(first, last, *refs)

    return pl.pallas_call(
        kernel,
        in_specs=[SMEM] + [VMEM] * 5 + [HBM],
        out_specs=spaces,
        out_shape=out_shape,
        scratch_shapes=scratch,
        compiler_params=params(16),
        name="stage",
    )(energies, sigma, own, own_low, near, far, pltpu.with_memory_space_constraint(base, pltpu.HBM))


def from_behind(block, distance):
    count = lax.axis_size("ta")
    return lax.ppermute(block, "ta", [(i - distance, i) for i in range(distance, count)])


def exchange(block):
    return lax.all_to_all(block, "ka", split_axis=0, concat_axis=0, tiled=True)


def on_device(green, energies, reach):
    table = tables(K)
    time = lax.axis_index("ka") * PART + lax.broadcasted_iota(jnp.int32, (PART, MEM), 0)
    lag = (time - lax.broadcasted_iota(jnp.int32, (PART, MEM), 1)) & (MEM - 1)
    mine = lax.dynamic_slice_in_dim(reach, lax.axis_index("ka") * PART, PART)
    keep = (lag < mine[:, None]).astype(F32)

    def inputs(own, low, chunk):
        spread = exchange(chunk)
        near, far = from_behind(own, 1), from_behind(low, 2)
        return exchange(self_energy(keep, table, spread)), own, low, near, far

    x, *rest = prepare(green)
    for last in (False, True):
        ahead, *rest = stage(True, False, energies, *inputs(*rest), x)
        x, *rest = stage(False, last, energies, *inputs(*rest), ahead)
    return x


def solution(mesh):
    in_specs = (P(None, "ka", "ta", None), P("ka"), P("ta"))
    out_specs = P(None, "ka", "ta", None)
    return jax.shard_map(
        on_device, mesh=mesh, in_specs=in_specs, out_specs=out_specs, check_vma=False
    )
```

profile of v0, /device:TPU:96, one launch (start us, length us, event | category | flops | bytes accessed | tf_op | source)
XLA Modules:
  0.0 149.5 jit_solution(3268967094342500321)
XLA Ops:
  0.0 3.5 %prepare.1 = (f32[2,16,64,128]{3,2,1,0:T(8,128)}, bf16[2,16,64,128]{3,2,1,0:T(8,128)(2,1)S(1)}, bf16[16,64,128]{2,1,0:T(8,128)(2,1)S(1)}, bf16[16,2,4,16,128]{4,3,2,1,0:T(8,128)(2,1)}) custom-call(f32[2,16,64,128]{3,2,1,0:T(8,128)} %x_in.1), custom_call_target="tpu_custom_call" | custom-call | tf_op jit(solution)/shard_map/prepare/pallas_call | solution.py:185
  3.5 0.0 copy-start
  3.6 7.2 %all-to-all-start = ((bf16[16,2,4,16,128]{4,3,2,1,0:T(8,128)(2,1)}), bf16[16,2,4,16,128]{4,3,2,1,0:T(8,128)(2,1)S(1)}, u32[]{:S(2)}, u32[]{:S(2)}) async-start(bf16[16,2,4,16,128]{4,3,2,1,0:T(8,128)(2,1)} %get-tuple-element.21), calls=%async_computation | async-start | bytes 1048576 | tf_op jit(solution)/shard_map/all_to_all | solution.py:323
  10.7 1.9 %collective-permute-start = (bf16[2,16,64,128]{3,2,1,0:T(8,128)(2,1)S(1)}, bf16[2,16,64,128]{3,2,1,0:T(8,128)(2,1)S(1)}, u32[]{:S(2)}, u32[]{:S(2)}) collective-permute-start(bf16[2,16,64,128]{3,2,1,0:T(8,128)(2,1)S(1)} %get-tuple-element.22.refs_2_), channel_id=1, source_target_pairs={{0,1},{1,2},{2,3},{3,4},{4,5},{5,6},{6,7},{8,9},{9,10},{10,11},{11... | collective-permute-start | bytes 1572872 | tf_op jit(solution)/shard_map/ppermute | solution.py:319
  12.7 0.0 copy-start.2
  12.7 0.6 copy-done.2
  13.3 0.1 dynamic_slice.3
  13.4 0.1 fusion.keep
  13.5 8.7 %all-to-all-done.x = bf16[16,2,4,16,128]{4,3,2,1,0:T(8,128)(2,1)S(1)} async-done(((bf16[16,2,4,16,128]{4,3,2,1,0:T(8,128)(2,1)}), bf16[16,2,4,16,128]{4,3,2,1,0:T(8,128)(2,1)S(1)}, u32[]{:S(2)}, u32[]{:S(2)}) %all-to-all-start) | async-done | bytes 524320 | tf_op jit(solution)/shard_map/all_to_all | solution.py:323
  22.2 0.0 copy-done
  22.2 1.8 %self_energy.4 = bf16[16,2,4,16,128]{4,3,2,1,0:T(8,128)(2,1)} custom-call(f32[4,128]{1,0:T(4,128)S(1)} %fusion.keep, bf16[512,256]{1,0:T(8,128)(2,1)S(1)} %copy-done, bf16[16,2,4,16,128]{4,3,2,1,0:T(8,128)(2,1)S(1)} %all-to-all-done.x), custom_call_target="tpu_custom_call" | custom-call | tf_op jit(solution)/shard_map/self_energy/pallas_call | solution.py:96
  24.1 3.6 %all-to-all-start.1 = ((bf16[16,2,4,16,128]{4,3,2,1,0:T(8,128)(2,1)}), bf16[16,2,4,16,128]{4,3,2,1,0:T(8,128)(2,1)S(1)}, u32[]{:S(2)}, u32[]{:S(2)}) async-start(bf16[16,2,4,16,128]{4,3,2,1,0:T(8,128)(2,1)} %self_energy.4), calls=%async_computation.1 | async-start | bytes 1048576 | tf_op jit(solution)/shard_map/all_to_all | solution.py:323
  27.7 0.0 copy-start.1
  27.7 1.3 collective-permute-start.1
  29.0 7.2 %collective-permute-done.1.refs_5_ = bf16[16,64,128]{2,1,0:T(8,128)(2,1)S(1)} collective-permute-done((bf16[16,64,128]{2,1,0:T(8,128)(2,1)S(1)}, bf16[16,64,128]{2,1,0:T(8,128)(2,1)S(1)}, u32[]{:S(2)}, u32[]{:S(2)}) %collective-permute-start.1) | collective-permute-done | bytes 262176 | tf_op jit(solution)/shard_map/ppermute | solution.py:319
  36.2 0.0 collective-permute-done.refs_4_
  36.2 1.8 %all-to-all-done.1.refs_1_ = bf16[16,2,4,16,128]{4,3,2,1,0:T(8,128)(2,1)S(1)} async-done(((bf16[16,2,4,16,128]{4,3,2,1,0:T(8,128)(2,1)}), bf16[16,2,4,16,128]{4,3,2,1,0:T(8,128)(2,1)S(1)}, u32[]{:S(2)}, u32[]{:S(2)}) %all-to-all-start.1) | async-done | bytes 524320 | tf_op jit(solution)/shard_map/all_to_all | solution.py:323
  38.0 0.0 copy-done.1
  38.0 4.8 %stage.4 = (f32[2,16,64,128]{3,2,1,0:T(8,128)}, bf16[2,16,64,128]{3,2,1,0:T(8,128)(2,1)S(1)}, bf16[16,64,128]{2,1,0:T(8,128)(2,1)S(1)}, bf16[16,2,4,16,128]{4,3,2,1,0:T(8,128)(2,1)}) custom-call(f32[16]{0:T(128)S(1)} %copy-done.1, bf16[16,2,4,16,128]{4,3,2,1,0:T(8,128)(2,1)S(1)} %all-to-all-done.1.refs_1_, ...), custom_call_target="tpu_custom_call" | custom-call | tf_op jit(solution)/shard_map/stage/pallas_call | solution.py:306
  42.8 5.1 %all-to-all-start.2 = ((bf16[16,2,4,16,128]{4,3,2,1,0:T(8,128)(2,1)}), bf16[16,2,4,16,128]{4,3,2,1,0:T(8,128)(2,1)S(1)}, u32[]{:S(2)}, u32[]{:S(2)}) async-start(bf16[16,2,4,16,128]{4,3,2,1,0:T(8,128)(2,1)} %get-tuple-element.25), calls=%async_computation.2 | async-start | bytes 1048576 | tf_op jit(solution)/shard_map/all_to_all | solution.py:323
  47.9 1.9 %collective-permute-start.2 = (bf16[2,16,64,128]{3,2,1,0:T(8,128)(2,1)S(1)}, bf16[2,16,64,128]{3,2,1,0:T(8,128)(2,1)S(1)}, u32[]{:S(2)}, u32[]{:S(2)}) collective-permute-start(bf16[2,16,64,128]{3,2,1,0:T(8,128)(2,1)S(1)} %get-tuple-element.26.refs_2_), channel_id=1, source_target_pairs={{0,1},{1,2},{2,3},{3,4},{4,5},{5,6},{6,7},{8,9},{9,10},{10,11},{11... | collective-permute-start | bytes 1572872 | tf_op jit(solution)/shard_map/ppermute | solution.py:319
  49.8 8.2 %all-to-all-done.2.x = bf16[16,2,4,16,128]{4,3,2,1,0:T(8,128)(2,1)S(1)} async-done(((bf16[16,2,4,16,128]{4,3,2,1,0:T(8,128)(2,1)}), bf16[16,2,4,16,128]{4,3,2,1,0:T(8,128)(2,1)S(1)}, u32[]{:S(2)}, u32[]{:S(2)}) %all-to-all-start.2) | async-done | bytes 524320 | tf_op jit(solution)/shard_map/all_to_all | solution.py:323
  58.0 1.8 %self_energy.5 = bf16[16,2,4,16,128]{4,3,2,1,0:T(8,128)(2,1)} custom-call(f32[4,128]{1,0:T(4,128)S(1)} %fusion.keep, bf16[512,256]{1,0:T(8,128)(2,1)S(1)} %copy-done, bf16[16,2,4,16,128]{4,3,2,1,0:T(8,128)(2,1)S(1)} %all-to-all-done.2.x), custom_call_target="tpu_custom_call" | custom-call | tf_op jit(solution)/shard_map/self_energy/pallas_call | solution.py:96
  59.8 3.6 %all-to-all-start.3 = ((bf16[16,2,4,16,128]{4,3,2,1,0:T(8,128)(2,1)}), bf16[16,2,4,16,128]{4,3,2,1,0:T(8,128)(2,1)S(1)}, u32[]{:S(2)}, u32[]{:S(2)}) async-start(bf16[16,2,4,16,128]{4,3,2,1,0:T(8,128)(2,1)} %self_energy.5), calls=%async_computation.3 | async-start | bytes 1048576 | tf_op jit(solution)/shard_map/all_to_all | solution.py:323
  63.4 1.3 collective-permute-start.3
  64.7 7.0 %collective-permute-done.3.refs_5_ = bf16[16,64,128]{2,1,0:T(8,128)(2,1)S(1)} collective-permute-done((bf16[16,64,128]{2,1,0:T(8,128)(2,1)S(1)}, bf16[16,64,128]{2,1,0:T(8,128)(2,1)S(1)}, u32[]{:S(2)}, u32[]{:S(2)}) %collective-permute-start.3) | collective-permute-done | bytes 262176 | tf_op jit(solution)/shard_map/ppermute | solution.py:319
  71.7 0.0 collective-permute-done.2.refs_4_
  71.7 1.8 %all-to-all-done.3.refs_1_ = bf16[16,2,4,16,128]{4,3,2,1,0:T(8,128)(2,1)S(1)} async-done(((bf16[16,2,4,16,128]{4,3,2,1,0:T(8,128)(2,1)}), bf16[16,2,4,16,128]{4,3,2,1,0:T(8,128)(2,1)S(1)}, u32[]{:S(2)}, u32[]{:S(2)}) %all-to-all-start.3) | async-done | bytes 524320 | tf_op jit(solution)/shard_map/all_to_all | solution.py:323
  73.5 4.7 %stage.5 = (f32[2,16,64,128]{3,2,1,0:T(8,128)}, bf16[2,16,64,128]{3,2,1,0:T(8,128)(2,1)S(1)}, bf16[16,64,128]{2,1,0:T(8,128)(2,1)S(1)}, bf16[16,2,4,16,128]{4,3,2,1,0:T(8,128)(2,1)}) custom-call(f32[16]{0:T(128)S(1)} %copy-done.1, bf16[16,2,4,16,128]{4,3,2,1,0:T(8,128)(2,1)S(1)} %all-to-all-done.3.refs_1_, ...), custom_call_target="tpu_custom_call" | custom-call | tf_op jit(solution)/shard_map/stage/pallas_call | solution.py:306
  78.1 5.4 %all-to-all-start.4 = ((bf16[16,2,4,16,128]{4,3,2,1,0:T(8,128)(2,1)}), bf16[16,2,4,16,128]{4,3,2,1,0:T(8,128)(2,1)S(1)}, u32[]{:S(2)}, u32[]{:S(2)}) async-start(bf16[16,2,4,16,128]{4,3,2,1,0:T(8,128)(2,1)} %get-tuple-element.29), calls=%async_computation.4 | async-start | bytes 1048576 | tf_op jit(solution)/shard_map/all_to_all | solution.py:323
  83.5 1.9 %collective-permute-start.4 = (bf16[2,16,64,128]{3,2,1,0:T(8,128)(2,1)S(1)}, bf16[2,16,64,128]{3,2,1,0:T(8,128)(2,1)S(1)}, u32[]{:S(2)}, u32[]{:S(2)}) collective-permute-start(bf16[2,16,64,128]{3,2,1,0:T(8,128)(2,1)S(1)} %get-tuple-element.30.refs_2_), channel_id=1, source_target_pairs={{0,1},{1,2},{2,3},{3,4},{4,5},{5,6},{6,7},{8,9},{9,10},{10,11},{11... | collective-permute-start | bytes 1572872 | tf_op jit(solution)/shard_map/ppermute | solution.py:319
  85.5 8.2 %all-to-all-done.4.x = bf16[16,2,4,16,128]{4,3,2,1,0:T(8,128)(2,1)S(1)} async-done(((bf16[16,2,4,16,128]{4,3,2,1,0:T(8,128)(2,1)}), bf16[16,2,4,16,128]{4,3,2,1,0:T(8,128)(2,1)S(1)}, u32[]{:S(2)}, u32[]{:S(2)}) %all-to-all-start.4) | async-done | bytes 524320 | tf_op jit(solution)/shard_map/all_to_all | solution.py:323
  93.6 1.8 %self_energy.6 = bf16[16,2,4,16,128]{4,3,2,1,0:T(8,128)(2,1)} custom-call(f32[4,128]{1,0:T(4,128)S(1)} %fusion.keep, bf16[512,256]{1,0:T(8,128)(2,1)S(1)} %copy-done, bf16[16,2,4,16,128]{4,3,2,1,0:T(8,128)(2,1)S(1)} %all-to-all-done.4.x), custom_call_target="tpu_custom_call" | custom-call | tf_op jit(solution)/shard_map/self_energy/pallas_call | solution.py:96
  95.5 3.6 %all-to-all-start.5 = ((bf16[16,2,4,16,128]{4,3,2,1,0:T(8,128)(2,1)}), bf16[16,2,4,16,128]{4,3,2,1,0:T(8,128)(2,1)S(1)}, u32[]{:S(2)}, u32[]{:S(2)}) async-start(bf16[16,2,4,16,128]{4,3,2,1,0:T(8,128)(2,1)} %self_energy.6), calls=%async_computation.5 | async-start | bytes 1048576 | tf_op jit(solution)/shard_map/all_to_all | solution.py:323
  99.1 1.3 collective-permute-start.5
  100.4 7.0 %collective-permute-done.5.refs_5_ = bf16[16,64,128]{2,1,0:T(8,128)(2,1)S(1)} collective-permute-done((bf16[16,64,128]{2,1,0:T(8,128)(2,1)S(1)}, bf16[16,64,128]{2,1,0:T(8,128)(2,1)S(1)}, u32[]{:S(2)}, u32[]{:S(2)}) %collective-permute-start.5) | collective-permute-done | bytes 262176 | tf_op jit(solution)/shard_map/ppermute | solution.py:319
  107.3 0.0 collective-permute-done.4.refs_4_
  107.3 1.8 %all-to-all-done.5.refs_1_ = bf16[16,2,4,16,128]{4,3,2,1,0:T(8,128)(2,1)S(1)} async-done(((bf16[16,2,4,16,128]{4,3,2,1,0:T(8,128)(2,1)}), bf16[16,2,4,16,128]{4,3,2,1,0:T(8,128)(2,1)S(1)}, u32[]{:S(2)}, u32[]{:S(2)}) %all-to-all-start.5) | async-done | bytes 524320 | tf_op jit(solution)/shard_map/all_to_all | solution.py:323
  109.1 4.8 %stage.6 = (f32[2,16,64,128]{3,2,1,0:T(8,128)}, bf16[2,16,64,128]{3,2,1,0:T(8,128)(2,1)S(1)}, bf16[16,64,128]{2,1,0:T(8,128)(2,1)S(1)}, bf16[16,2,4,16,128]{4,3,2,1,0:T(8,128)(2,1)}) custom-call(f32[16]{0:T(128)S(1)} %copy-done.1, bf16[16,2,4,16,128]{4,3,2,1,0:T(8,128)(2,1)S(1)} %all-to-all-done.5.refs_1_, ...), custom_call_target="tpu_custom_call" | custom-call | tf_op jit(solution)/shard_map/stage/pallas_call | solution.py:306
  113.9 5.4 %all-to-all-start.6 = ((bf16[16,2,4,16,128]{4,3,2,1,0:T(8,128)(2,1)}), bf16[16,2,4,16,128]{4,3,2,1,0:T(8,128)(2,1)S(1)}, u32[]{:S(2)}, u32[]{:S(2)}) async-start(bf16[16,2,4,16,128]{4,3,2,1,0:T(8,128)(2,1)} %get-tuple-element.33), calls=%async_computation.6 | async-start | bytes 1048576 | tf_op jit(solution)/shard_map/all_to_all | solution.py:323
  119.3 1.9 %collective-permute-start.6 = (bf16[2,16,64,128]{3,2,1,0:T(8,128)(2,1)S(1)}, bf16[2,16,64,128]{3,2,1,0:T(8,128)(2,1)S(1)}, u32[]{:S(2)}, u32[]{:S(2)}) collective-permute-start(bf16[2,16,64,128]{3,2,1,0:T(8,128)(2,1)S(1)} %get-tuple-element.34.refs_2_), channel_id=1, source_target_pairs={{0,1},{1,2},{2,3},{3,4},{4,5},{5,6},{6,7},{8,9},{9,10},{10,11},{11... | collective-permute-start | bytes 1572872 | tf_op jit(solution)/shard_map/ppermute | solution.py:319
  121.2 8.2 %all-to-all-done.6.x = bf16[16,2,4,16,128]{4,3,2,1,0:T(8,128)(2,1)S(1)} async-done(((bf16[16,2,4,16,128]{4,3,2,1,0:T(8,128)(2,1)}), bf16[16,2,4,16,128]{4,3,2,1,0:T(8,128)(2,1)S(1)}, u32[]{:S(2)}, u32[]{:S(2)}) %all-to-all-start.6) | async-done | bytes 524320 | tf_op jit(solution)/shard_map/all_to_all | solution.py:323
  129.4 1.8 %self_energy.7 = bf16[16,2,4,16,128]{4,3,2,1,0:T(8,128)(2,1)} custom-call(f32[4,128]{1,0:T(4,128)S(1)} %fusion.keep, bf16[512,256]{1,0:T(8,128)(2,1)S(1)} %copy-done, bf16[16,2,4,16,128]{4,3,2,1,0:T(8,128)(2,1)S(1)} %all-to-all-done.6.x), custom_call_target="tpu_custom_call" | custom-call | tf_op jit(solution)/shard_map/self_energy/pallas_call | solution.py:96
  131.2 3.6 %all-to-all-start.7 = ((bf16[16,2,4,16,128]{4,3,2,1,0:T(8,128)(2,1)}), bf16[16,2,4,16,128]{4,3,2,1,0:T(8,128)(2,1)S(1)}, u32[]{:S(2)}, u32[]{:S(2)}) async-start(bf16[16,2,4,16,128]{4,3,2,1,0:T(8,128)(2,1)} %self_energy.7), calls=%async_computation.7 | async-start | bytes 1048576 | tf_op jit(solution)/shard_map/all_to_all | solution.py:323
  134.8 1.3 collective-permute-start.7
  136.1 7.0 %collective-permute-done.7.refs_5_ = bf16[16,64,128]{2,1,0:T(8,128)(2,1)S(1)} collective-permute-done((bf16[16,64,128]{2,1,0:T(8,128)(2,1)S(1)}, bf16[16,64,128]{2,1,0:T(8,128)(2,1)S(1)}, u32[]{:S(2)}, u32[]{:S(2)}) %collective-permute-start.7) | collective-permute-done | bytes 262176 | tf_op jit(solution)/shard_map/ppermute | solution.py:319
  143.1 0.0 collective-permute-done.6.refs_4_
  143.1 1.8 %all-to-all-done.7.refs_1_ = bf16[16,2,4,16,128]{4,3,2,1,0:T(8,128)(2,1)S(1)} async-done(((bf16[16,2,4,16,128]{4,3,2,1,0:T(8,128)(2,1)}), bf16[16,2,4,16,128]{4,3,2,1,0:T(8,128)(2,1)S(1)}, u32[]{:S(2)}, u32[]{:S(2)}) %all-to-all-start.7) | async-done | bytes 524320 | tf_op jit(solution)/shard_map/all_to_all | solution.py:323
  144.8 4.6 %stage.7 = f32[2,16,64,128]{3,2,1,0:T(8,128)} custom-call(f32[16]{0:T(128)S(1)} %copy-done.1, bf16[16,2,4,16,128]{4,3,2,1,0:T(8,128)(2,1)S(1)} %all-to-all-done.7.refs_1_, bf16[2,16,64,128]{3,2,1,0:T(8,128)(2,1)S(1)} %get-tuple-element.34.refs_2_, bf16[16,64,128]{2,1,0:T(8,128)(2,1)S(1)} %get-tuple-element.35.refs_3_, ...), custom_call_target="tpu_custom_call" | custom-call | tf_op jit(solution)/shard_map/stage/pallas_call | solution.py:306
  (1 shorter events, 0.0 us)
Async XLA Ops:
  3.5 18.7 %copy-start = (bf16[512,256]{1,0:T(8,128)(2,1)S(1)}, bf16[512,256]{1,0:T(8,128)(2,1)}, u32[]{:S(2)}) copy-start(bf16[512,256]{1,0:T(8,128)(2,1)} %constant.16.clone.table) | copy-start | bytes 786436
  3.6 18.7 %all-to-all-start = ((bf16[16,2,4,16,128]{4,3,2,1,0:T(8,128)(2,1)}), bf16[16,2,4,16,128]{4,3,2,1,0:T(8,128)(2,1)S(1)}, u32[]{:S(2)}, u32[]{:S(2)}) async-start(bf16[16,2,4,16,128]{4,3,2,1,0:T(8,128)(2,1)} %get-tuple-element.21), calls=%async_computation | async-start | bytes 1048576 | tf_op jit(solution)/shard_map/all_to_all | solution.py:323
  10.7 25.5 %collective-permute-start = (bf16[2,16,64,128]{3,2,1,0:T(8,128)(2,1)S(1)}, bf16[2,16,64,128]{3,2,1,0:T(8,128)(2,1)S(1)}, u32[]{:S(2)}, u32[]{:S(2)}) collective-permute-start(bf16[2,16,64,128]{3,2,1,0:T(8,128)(2,1)S(1)} %get-tuple-element.22.refs_2_), channel_id=1, source_target_pairs={{0,1},{1,2},{2,3},{3,4},{4,5},{5,6},{6,7},{8,9},{9,10},{10,11},{11... | collective-permute-start | bytes 1572872 | tf_op jit(solution)/shard_map/ppermute | solution.py:319
  12.7 0.7 copy-start.2
  24.1 13.9 %all-to-all-start.1 = ((bf16[16,2,4,16,128]{4,3,2,1,0:T(8,128)(2,1)}), bf16[16,2,4,16,128]{4,3,2,1,0:T(8,128)(2,1)S(1)}, u32[]{:S(2)}, u32[]{:S(2)}) async-start(bf16[16,2,4,16,128]{4,3,2,1,0:T(8,128)(2,1)} %self_energy.4), calls=%async_computation.1 | async-start | bytes 1048576 | tf_op jit(solution)/shard_map/all_to_all | solution.py:323
  27.7 10.3 %copy-start.1 = (f32[16]{0:T(128)S(1)}, f32[16]{0:T(128)}, u32[]{:S(2)}) copy-start(f32[16]{0:T(128)} %refs_0_.7) | copy-start | bytes 196
  27.7 8.5 %collective-permute-start.1 = (bf16[16,64,128]{2,1,0:T(8,128)(2,1)S(1)}, bf16[16,64,128]{2,1,0:T(8,128)(2,1)S(1)}, u32[]{:S(2)}, u32[]{:S(2)}) collective-permute-start(bf16[16,64,128]{2,1,0:T(8,128)(2,1)S(1)} %get-tuple-element.23.refs_3_), channel_id=1, source_target_pairs={{0,2},{1,3},{2,4},{3,5},{4,6},{5,7},{8,10},{9,11},{10,12},{11,13},... | collective-permute-start | bytes 786440 | tf_op jit(solution)/shard_map/ppermute | solution.py:319
  42.8 15.2 %all-to-all-start.2 = ((bf16[16,2,4,16,128]{4,3,2,1,0:T(8,128)(2,1)}), bf16[16,2,4,16,128]{4,3,2,1,0:T(8,128)(2,1)S(1)}, u32[]{:S(2)}, u32[]{:S(2)}) async-start(bf16[16,2,4,16,128]{4,3,2,1,0:T(8,128)(2,1)} %get-tuple-element.25), calls=%async_computation.2 | async-start | bytes 1048576 | tf_op jit(solution)/shard_map/all_to_all | solution.py:323
  47.9 23.8 %collective-permute-start.2 = (bf16[2,16,64,128]{3,2,1,0:T(8,128)(2,1)S(1)}, bf16[2,16,64,128]{3,2,1,0:T(8,128)(2,1)S(1)}, u32[]{:S(2)}, u32[]{:S(2)}) collective-permute-start(bf16[2,16,64,128]{3,2,1,0:T(8,128)(2,1)S(1)} %get-tuple-element.26.refs_2_), channel_id=1, source_target_pairs={{0,1},{1,2},{2,3},{3,4},{4,5},{5,6},{6,7},{8,9},{9,10},{10,11},{11... | collective-permute-start | bytes 1572872 | tf_op jit(solution)/shard_map/ppermute | solution.py:319
  59.8 13.7 %all-to-all-start.3 = ((bf16[16,2,4,16,128]{4,3,2,1,0:T(8,128)(2,1)}), bf16[16,2,4,16,128]{4,3,2,1,0:T(8,128)(2,1)S(1)}, u32[]{:S(2)}, u32[]{:S(2)}) async-start(bf16[16,2,4,16,128]{4,3,2,1,0:T(8,128)(2,1)} %self_energy.5), calls=%async_computation.3 | async-start | bytes 1048576 | tf_op jit(solution)/shard_map/all_to_all | solution.py:323
  63.4 8.3 %collective-permute-start.3 = (bf16[16,64,128]{2,1,0:T(8,128)(2,1)S(1)}, bf16[16,64,128]{2,1,0:T(8,128)(2,1)S(1)}, u32[]{:S(2)}, u32[]{:S(2)}) collective-permute-start(bf16[16,64,128]{2,1,0:T(8,128)(2,1)S(1)} %get-tuple-element.27.refs_3_), channel_id=1, source_target_pairs={{0,2},{1,3},{2,4},{3,5},{4,6},{5,7},{8,10},{9,11},{10,12},{11,13},... | collective-permute-start | bytes 786440 | tf_op jit(solution)/shard_map/ppermute | solution.py:319
  78.1 15.5 %all-to-all-start.4 = ((bf16[16,2,4,16,128]{4,3,2,1,0:T(8,128)(2,1)}), bf16[16,2,4,16,128]{4,3,2,1,0:T(8,128)(2,1)S(1)}, u32[]{:S(2)}, u32[]{:S(2)}) async-start(bf16[16,2,4,16,128]{4,3,2,1,0:T(8,128)(2,1)} %get-tuple-element.29), calls=%async_computation.4 | async-start | bytes 1048576 | tf_op jit(solution)/shard_map/all_to_all | solution.py:323
  83.5 23.8 %collective-permute-start.4 = (bf16[2,16,64,128]{3,2,1,0:T(8,128)(2,1)S(1)}, bf16[2,16,64,128]{3,2,1,0:T(8,128)(2,1)S(1)}, u32[]{:S(2)}, u32[]{:S(2)}) collective-permute-start(bf16[2,16,64,128]{3,2,1,0:T(8,128)(2,1)S(1)} %get-tuple-element.30.refs_2_), channel_id=1, source_target_pairs={{0,1},{1,2},{2,3},{3,4},{4,5},{5,6},{6,7},{8,9},{9,10},{10,11},{11... | collective-permute-start | bytes 1572872 | tf_op jit(solution)/shard_map/ppermute | solution.py:319
  95.5 13.6 %all-to-all-start.5 = ((bf16[16,2,4,16,128]{4,3,2,1,0:T(8,128)(2,1)}), bf16[16,2,4,16,128]{4,3,2,1,0:T(8,128)(2,1)S(1)}, u32[]{:S(2)}, u32[]{:S(2)}) async-start(bf16[16,2,4,16,128]{4,3,2,1,0:T(8,128)(2,1)} %self_energy.6), calls=%async_computation.5 | async-start | bytes 1048576 | tf_op jit(solution)/shard_map/all_to_all | solution.py:323
  99.1 8.3 %collective-permute-start.5 = (bf16[16,64,128]{2,1,0:T(8,128)(2,1)S(1)}, bf16[16,64,128]{2,1,0:T(8,128)(2,1)S(1)}, u32[]{:S(2)}, u32[]{:S(2)}) collective-permute-start(bf16[16,64,128]{2,1,0:T(8,128)(2,1)S(1)} %get-tuple-element.31.refs_3_), channel_id=1, source_target_pairs={{0,2},{1,3},{2,4},{3,5},{4,6},{5,7},{8,10},{9,11},{10,12},{11,13},... | collective-permute-start | bytes 786440 | tf_op jit(solution)/shard_map/ppermute | solution.py:319
  113.9 15.5 %all-to-all-start.6 = ((bf16[16,2,4,16,128]{4,3,2,1,0:T(8,128)(2,1)}), bf16[16,2,4,16,128]{4,3,2,1,0:T(8,128)(2,1)S(1)}, u32[]{:S(2)}, u32[]{:S(2)}) async-start(bf16[16,2,4,16,128]{4,3,2,1,0:T(8,128)(2,1)} %get-tuple-element.33), calls=%async_computation.6 | async-start | bytes 1048576 | tf_op jit(solution)/shard_map/all_to_all | solution.py:323
  119.3 23.8 %collective-permute-start.6 = (bf16[2,16,64,128]{3,2,1,0:T(8,128)(2,1)S(1)}, bf16[2,16,64,128]{3,2,1,0:T(8,128)(2,1)S(1)}, u32[]{:S(2)}, u32[]{:S(2)}) collective-permute-start(bf16[2,16,64,128]{3,2,1,0:T(8,128)(2,1)S(1)} %get-tuple-element.34.refs_2_), channel_id=1, source_target_pairs={{0,1},{1,2},{2,3},{3,4},{4,5},{5,6},{6,7},{8,9},{9,10},{10,11},{11... | collective-permute-start | bytes 1572872 | tf_op jit(solution)/shard_map/ppermute | solution.py:319
  131.2 13.7 %all-to-all-start.7 = ((bf16[16,2,4,16,128]{4,3,2,1,0:T(8,128)(2,1)}), bf16[16,2,4,16,128]{4,3,2,1,0:T(8,128)(2,1)S(1)}, u32[]{:S(2)}, u32[]{:S(2)}) async-start(bf16[16,2,4,16,128]{4,3,2,1,0:T(8,128)(2,1)} %self_energy.7), calls=%async_computation.7 | async-start | bytes 1048576 | tf_op jit(solution)/shard_map/all_to_all | solution.py:323
  134.8 8.3 %collective-permute-start.7 = (bf16[16,64,128]{2,1,0:T(8,128)(2,1)S(1)}, bf16[16,64,128]{2,1,0:T(8,128)(2,1)S(1)}, u32[]{:S(2)}, u32[]{:S(2)}) collective-permute-start(bf16[16,64,128]{2,1,0:T(8,128)(2,1)S(1)} %get-tuple-element.35.refs_3_), channel_id=1, source_target_pairs={{0,2},{1,3},{2,4},{3,5},{4,6},{5,7},{8,10},{9,11},{10,12},{11,13},... | collective-permute-start | bytes 786440 | tf_op jit(solution)/shard_map/ppermute | solution.py:319
where the time goes:
time: 151 us; the launch traced here: 149 us
  waiting for transfers between devices  68.5 us (45%)
  starting transfers between devices  50.2 us (33%)
  Pallas kernels  29.7 us (20%)
    all_to_all x8, waiting for transfers between devices, exchange(): return lax.all_to_all(block, 'ka', split_axis=0, concat_axis=0, tiled=True)  40.4 us
    all_to_all x8, starting transfers between devices, exchange(): return lax.all_to_all(block, 'ka', split_axis=0, concat_axis=0, tiled=True)  37.4 us
    ppermute x8, waiting for transfers between devices, from_behind(): lax.ppermute(block, 'ta', [(i - distance, i) for i in range(distance, cou...  28.1 us
    pallas_call x4, Pallas kernels, stage(): pl.pallas_call(kernel, in_specs=[SMEM] + [VMEM] * 5 + [HBM], out_specs=sp...  18.8 us
    ppermute x8, starting transfers between devices, from_behind(): lax.ppermute(block, 'ta', [(i - distance, i) for i in range(distance, cou...  12.9 us
    pallas_call x4, Pallas kernels, self_energy(): pl.pallas_call(self_energy_kernel, in_specs=[VMEM, VMEM, VMEM], out_specs...  7.33 us
    pallas_call x1, Pallas kernels, prepare(): pl.pallas_call(prepare_kernel, in_specs=[HBM], out_specs=[HBM, VMEM, VMEM...  3.53 us
  transfers between devices with their start and end apart: 16, of which 12 were waited for; matrix products, arithmetic and copies ran while one was open for 0% of the time, Pallas kernels for 5%

commit v1 on v0

--- a/solution.py
+++ b/solution.py
@@ -6,14 +6,17 @@
 from jax.experimental.pallas import tpu as pltpu
 from jax.sharding import PartitionSpec as P
 
+
 K = 256
 MEM = 128
 ROWS = 64
 OWN = 16
 GROUP = 16
 PART = 4
-KB = 4
+PITCH = 17
+KB = 8
 STEPS = OWN // KB
+PIECES = 4
 MIB = 2**20
 
 quadrature = 0.0625
@@ -54,21 +57,32 @@
         here = pl.ds(2 * pair, 2)
         return pltpu.make_async_copy(y.at[:, :, here], out.at[:, :, here], sems.at[pair])
 
-    both = table[...]
+    cosines, sines = table[:K], table[K:]
+    forward = jnp.concatenate(
+        [
+            jnp.concatenate([cosines, -sines], 1),
+            jnp.concatenate([sines, cosines], 1),
+        ],
+        0,
+    )
+    inverse = jnp.concatenate(
+        [
+            jnp.concatenate([cosines, sines], 1),
+            jnp.concatenate([-sines, cosines], 1),
+        ],
+        0,
+    )
     for pair in range(2):
-        fields = []
+        rows = []
         for part in range(2):
             sides = [x[:, part, 2 * pair + i].reshape(K, MEM) for i in range(2)]
-            rhs = jnp.concatenate(sides, 1)
-            fields.append(jnp.dot(both, rhs, preferred_element_type=F32))
-        re = fields[0][:K] - fields[1][K:]
-        im = fields[0][K:] + fields[1][:K]
+            rows.append(jnp.concatenate(sides, 1))
+        field = jnp.dot(forward, jnp.concatenate(rows, 0), preferred_element_type=F32)
+        re, im = field[:K], field[K:]
         weight = -(re * re + im * im)
-        zr = (weight * re).astype(BF16)
-        zi = (weight * im).astype(BF16)
-        a = jnp.dot(both, zr, preferred_element_type=F32)
-        b = jnp.dot(both, zi, preferred_element_type=F32)
-        sigma = (a[:K] + b[K:], b[:K] - a[K:])
+        z = jnp.concatenate([(weight * re).astype(BF16), (weight * im).astype(BF16)], 0)
+        both = jnp.dot(inverse, z, preferred_element_type=F32)
+        sigma = both[:K], both[K:]
         for part in range(2):
             for i in range(2):
                 side = sigma[part][:, i * MEM : (i + 1) * MEM]
@@ -104,28 +118,32 @@
     )(keep, table, spread)
 
 
-def piece(ref, q):
-    here = pl.ds(q * KB, KB)
+def piece(ref, q, size):
+    here = pl.ds(q * size, size)
     return ref.at[here] if len(ref.shape) == 3 else ref.at[:, here]
 
 
-def mover(pairs, sems, first):
+def mover(pairs, sems, first, size=KB):
     def move(n, q):
         source, target = pairs[n]
-        return pltpu.make_async_copy(piece(source, q), piece(target, q), sems.at[first + n, q])
+        return pltpu.make_async_copy(piece(source, q, size), piece(target, q, size), sems.at[first + n, q])
 
     return move
 
 
-def send_chunk(turned, block, chunk, sem):
-    for d in range(GROUP):
-        for c in range(2):
-            for j in range(PART):
-                t = d * PART + j
-                block[d, c, j] = turned[c, t * OWN : (t + 1) * OWN, :].astype(BF16)
-    copy = pltpu.make_async_copy(block, chunk, sem)
-    copy.start()
-    return copy
+def send_chunk(turned, block, chunk, sems):
+    copies = []
+    for first in range(0, GROUP, GROUP // PIECES):
+        here = pl.ds(first, GROUP // PIECES)
+        for d in range(first, first + GROUP // PIECES):
+            for c in range(2):
+                for j in range(PART):
+                    t = (d * PART + j) * PITCH
+                    block[d, c, j] = turned[c, t : t + OWN, :].astype(BF16)
+        sem = sems.at[len(copies)]
+        copies.append(pltpu.make_async_copy(block.at[here], chunk.at[here], sem))
+        copies[-1].start()
+    return copies
 
 
 def emit(k, value, turned, near, far):
@@ -133,38 +151,39 @@
     causal = lane <= row
     low = []
     for c in range(2):
-        turned[c, pl.ds(k, ROWS, stride=OWN), :] = value[c]
+        turned[c, pl.ds(k, ROWS, stride=PITCH), :] = value[c]
         near[c, k] = value[c].astype(BF16)
         low.append(jnp.where(causal, value[c], 0.0))
     far[k] = (low[0] + half_turn(low[1])).astype(BF16)
 
 
 def prepare_kernel(x_in, out, near, far, chunk, x, y, turned, block, sems, sem):
-    load = mover([(x_in, x)], sems, 0)
+    load = mover([(x_in, x)], sems, 0, 4)
     pairs = [(y, out)]
-    save = mover(pairs, sems, 1)
-    for q in range(STEPS):
+    save = mover(pairs, sems, 1, 4)
+    for q in range(OWN // 4):
         load(0, q).start()
 
     def step(q, carry):
         load(0, q).wait()
-        for i in range(KB):
-            k = q * KB + i
+        for i in range(4):
+            k = q * 4 + i
             value = [turn_over(x[c, k]) for c in range(2)]
             for c in range(2):
                 y[c, k] = value[c]
             emit(k, value, turned, near, far)
         return carry
 
-    lax.fori_loop(0, STEPS, step, 0)
-    last = send_chunk(turned, block, chunk, sem)
+    lax.fori_loop(0, OWN // 4, step, 0)
+    copies = send_chunk(turned, block, chunk, sem)
     for n in range(len(pairs)):
-        for q in range(STEPS):
+        for q in range(OWN // 4):
             save(n, q).start()
     for n in range(len(pairs)):
-        for q in range(STEPS):
+        for q in range(OWN // 4):
             save(n, q).wait()
-    last.wait()
+    for copy in copies:
+        copy.wait()
 
 
 WIDE = pltpu.HBM(STATE, F32)
@@ -175,7 +194,7 @@
     return [
         pltpu.VMEM(STATE, BF16),
         pltpu.VMEM(FAR, BF16),
-        pltpu.VMEM((2, ROWS * OWN, MEM), F32),
+        pltpu.VMEM((2, ROWS * PITCH, MEM), F32),
         pltpu.VMEM(CHUNK, BF16),
     ]
 
@@ -189,7 +208,7 @@
         out_shape=[WIDE] + EMITTED,
         scratch_shapes=[scratch, scratch]
         + emitting()[2:]
-        + [pltpu.SemaphoreType.DMA((2, STEPS)), pltpu.SemaphoreType.DMA],
+        + [pltpu.SemaphoreType.DMA((2, OWN // 4)), pltpu.SemaphoreType.DMA((PIECES,))],
         compiler_params=params(16),
         name="prepare",
     )(pltpu.with_memory_space_constraint(x, pltpu.HBM))
@@ -215,7 +234,7 @@
         for c in range(2):
             for j in range(PART):
                 t = d * PART + j
-                held[c, t * OWN : (t + 1) * OWN, :] = sigma[d, c, j].astype(F32)
+                held[c, t * PITCH : t * PITCH + OWN, :] = sigma[d, c, j].astype(F32)
 
     row, lane = grids()
     causal = lane <= row
@@ -227,13 +246,11 @@
         return jnp.where(kept, block, jnp.zeros_like(block))
 
     def step(q, carry):
-        for n in range(len(loads)):
-            load(n, q).wait()
         for i in range(KB):
             k = q * KB + i
             left = []
             for c in range(2):
-                memory = held[c, pl.ds(k, ROWS, stride=OWN), :]
+                memory = held[c, pl.ds(k, ROWS, stride=PITCH), :]
                 inner = jnp.where(own_side, memory, 0.0).astype(BF16)
                 outer = jnp.where(own_side, 0.0, memory).astype(BF16)
                 left.append(jnp.concatenate([inner, outer[:, :ROWS]], 1))
@@ -262,7 +279,13 @@
                     early[ROWS:, :MEM] + early[:ROWS, MEM:],
                 ),
             )
-            collide = [quadrature * part for part in collide]
+            for c in range(2):
+                result[c, k] = quadrature * collide[c]
+        for n in range(len(loads)):
+            load(n, q).wait()
+        for i in range(KB):
+            k = q * KB + i
+            collide = result[0, k], result[1, k]
             half = 0.5 * step_size
             if first:
                 energy = energies[k]
@@ -284,7 +307,8 @@
 
     lax.fori_loop(0, STEPS, step, 0)
     if not last:
-        send_chunk(turned, block, chunk, chunk_sem).wait()
+        for copy in send_chunk(turned, block, chunk, chunk_sem):
+            copy.wait()
     for q in range(STEPS):
         for n in range(len(saves)):
             save(n, q).wait()
@@ -292,13 +316,13 @@
 
 def stage(first, last, energies, sigma, own, own_low, near, far, base):
     state = pltpu.VMEM(STATE, F32)
-    scratch = [state, state, pltpu.VMEM((2, ROWS * OWN, MEM), F32)]
+    scratch = [state, state, pltpu.VMEM((2, ROWS * PITCH, MEM), F32)]
     scratch += [pltpu.SemaphoreType.DMA((2, STEPS))]
     out_shape, spaces = [WIDE], [HBM]
     if not last:
         out_shape += EMITTED
         spaces += [VMEM, VMEM, HBM]
-        scratch += emitting()[2:] + [pltpu.SemaphoreType.DMA]
+        scratch += emitting()[2:] + [pltpu.SemaphoreType.DMA((PIECES,))]
 
     def kernel(*refs):
         stage_kernel(first, last, *refs)
@@ -332,12 +356,16 @@
 
     def inputs(own, low, chunk):
         spread = exchange(chunk)
-        near, far = from_behind(own, 1), from_behind(low, 2)
-        return exchange(self_energy(keep, table, spread)), own, low, near, far
+        near = from_behind(own, 1)
+        far = from_behind(low, 2)
+        sigma = self_energy(keep, table, spread)
+        sigma = exchange(sigma)
+        return sigma, own, low, near, far
 
     x, *rest = prepare(green)
-    for last in (False, True):
+    for counter in range(2):
         ahead, *rest = stage(True, False, energies, *inputs(*rest), x)
+        last = counter == 1
         x, *rest = stage(False, last, energies, *inputs(*rest), ahead)
     return x
 

time: 151 us -> 146 us (0.967)
  Pallas kernels: 29.7 us -> 25.2 us
    pallas_call x4, Pallas kernels: 18.8 us -> 14.5 us  [stage(): pl.pallas_call(kernel, in_specs=[SMEM] + [VMEM] * 5 + [HBM], out_specs=sp...]
where the time goes in v1:
time: 146 us; the launch traced here: 145 us
  waiting for transfers between devices  68.5 us (47%)
  starting transfers between devices  50.2 us (34%)
  Pallas kernels  25.2 us (17%)
    all_to_all x8, waiting for transfers between devices, exchange(): return lax.all_to_all(block, 'ka', split_axis=0, concat_axis=0, tiled=True)  40.4 us
    all_to_all x8, starting transfers between devices, exchange(): return lax.all_to_all(block, 'ka', split_axis=0, concat_axis=0, tiled=True)  37.4 us
    ppermute x8, waiting for transfers between devices, from_behind(): lax.ppermute(block, 'ta', [(i - distance, i) for i in range(distance, cou...  28.1 us
    pallas_call x4, Pallas kernels, stage(): pl.pallas_call(kernel, in_specs=[SMEM] + [VMEM] * 5 + [HBM], out_specs=sp...  14.5 us
    ppermute x8, starting transfers between devices, from_behind(): lax.ppermute(block, 'ta', [(i - distance, i) for i in range(distance, cou...  12.9 us
    pallas_call x4, Pallas kernels, self_energy(): pl.pallas_call(self_energy_kernel, in_specs=[VMEM, VMEM, VMEM], out_specs...  7.3 us
    pallas_call x1, Pallas kernels, prepare(): pl.pallas_call(prepare_kernel, in_specs=[HBM], out_specs=[HBM, VMEM, VMEM...  3.45 us
  transfers between devices with their start and end apart: 16, of which 12 were waited for; matrix products, arithmetic and copies ran while one was open for 0% of the time, Pallas kernels for 5%

profile of v1, /device:TPU:96, one launch (start us, length us, event | category | flops | bytes accessed | tf_op | source)
XLA Modules:
  0.0 145.0 jit_solution(1326987513934457289)
XLA Ops:
  0.0 3.5 %prepare.1 = (f32[2,16,64,128]{3,2,1,0:T(8,128)}, bf16[2,16,64,128]{3,2,1,0:T(8,128)(2,1)S(1)}, bf16[16,64,128]{2,1,0:T(8,128)(2,1)S(1)}, bf16[16,2,4,16,128]{4,3,2,1,0:T(8,128)(2,1)}) custom-call(f32[2,16,64,128]{3,2,1,0:T(8,128)} %x_in.1), custom_call_target="tpu_custom_call" | custom-call | tf_op jit(solution)/shard_map/prepare/pallas_call | solution.py:204
  3.5 0.0 copy-start
  3.5 7.2 %all-to-all-start = ((bf16[16,2,4,16,128]{4,3,2,1,0:T(8,128)(2,1)}), bf16[16,2,4,16,128]{4,3,2,1,0:T(8,128)(2,1)S(1)}, u32[]{:S(2)}, u32[]{:S(2)}) async-start(bf16[16,2,4,16,128]{4,3,2,1,0:T(8,128)(2,1)} %get-tuple-element.21), calls=%async_computation | async-start | bytes 1048576 | tf_op jit(solution)/shard_map/all_to_all | solution.py:347
  10.7 1.9 %collective-permute-start = (bf16[2,16,64,128]{3,2,1,0:T(8,128)(2,1)S(1)}, bf16[2,16,64,128]{3,2,1,0:T(8,128)(2,1)S(1)}, u32[]{:S(2)}, u32[]{:S(2)}) collective-permute-start(bf16[2,16,64,128]{3,2,1,0:T(8,128)(2,1)S(1)} %get-tuple-element.22.refs_2_), channel_id=1, source_target_pairs={{0,1},{1,2},{2,3},{3,4},{4,5},{5,6},{6,7},{8,9},{9,10},{10,11},{11... | collective-permute-start | bytes 1572872 | tf_op jit(solution)/shard_map/ppermute | solution.py:343
  12.6 0.0 copy-start.2
  12.6 0.6 copy-done.2
  13.3 0.1 dynamic_slice.3
  13.3 0.1 fusion.keep
  13.4 8.7 %all-to-all-done.x = bf16[16,2,4,16,128]{4,3,2,1,0:T(8,128)(2,1)S(1)} async-done(((bf16[16,2,4,16,128]{4,3,2,1,0:T(8,128)(2,1)}), bf16[16,2,4,16,128]{4,3,2,1,0:T(8,128)(2,1)S(1)}, u32[]{:S(2)}, u32[]{:S(2)}) %all-to-all-start) | async-done | bytes 524320 | tf_op jit(solution)/shard_map/all_to_all | solution.py:347
  22.1 0.0 copy-done
  22.2 1.8 %self_energy.4 = bf16[16,2,4,16,128]{4,3,2,1,0:T(8,128)(2,1)} custom-call(f32[4,128]{1,0:T(4,128)S(1)} %fusion.keep, bf16[512,256]{1,0:T(8,128)(2,1)S(1)} %copy-done, bf16[16,2,4,16,128]{4,3,2,1,0:T(8,128)(2,1)S(1)} %all-to-all-done.x), custom_call_target="tpu_custom_call" | custom-call | tf_op jit(solution)/shard_map/self_energy/pallas_call | solution.py:110
  24.0 3.6 %all-to-all-start.1 = ((bf16[16,2,4,16,128]{4,3,2,1,0:T(8,128)(2,1)}), bf16[16,2,4,16,128]{4,3,2,1,0:T(8,128)(2,1)S(1)}, u32[]{:S(2)}, u32[]{:S(2)}) async-start(bf16[16,2,4,16,128]{4,3,2,1,0:T(8,128)(2,1)} %self_energy.4), calls=%async_computation.1 | async-start | bytes 1048576 | tf_op jit(solution)/shard_map/all_to_all | solution.py:347
  27.6 0.0 copy-start.1
  27.6 1.3 collective-permute-start.1
  28.9 7.2 %collective-permute-done.1.refs_5_ = bf16[16,64,128]{2,1,0:T(8,128)(2,1)S(1)} collective-permute-done((bf16[16,64,128]{2,1,0:T(8,128)(2,1)S(1)}, bf16[16,64,128]{2,1,0:T(8,128)(2,1)S(1)}, u32[]{:S(2)}, u32[]{:S(2)}) %collective-permute-start.1) | collective-permute-done | bytes 262176 | tf_op jit(solution)/shard_map/ppermute | solution.py:343
  36.1 0.0 collective-permute-done.refs_4_
  36.1 1.8 %all-to-all-done.1.refs_1_ = bf16[16,2,4,16,128]{4,3,2,1,0:T(8,128)(2,1)S(1)} async-done(((bf16[16,2,4,16,128]{4,3,2,1,0:T(8,128)(2,1)}), bf16[16,2,4,16,128]{4,3,2,1,0:T(8,128)(2,1)S(1)}, u32[]{:S(2)}, u32[]{:S(2)}) %all-to-all-start.1) | async-done | bytes 524320 | tf_op jit(solution)/shard_map/all_to_all | solution.py:347
  37.9 0.0 copy-done.1
  37.9 3.6 %stage.4 = (f32[2,16,64,128]{3,2,1,0:T(8,128)}, bf16[2,16,64,128]{3,2,1,0:T(8,128)(2,1)S(1)}, bf16[16,64,128]{2,1,0:T(8,128)(2,1)S(1)}, bf16[16,2,4,16,128]{4,3,2,1,0:T(8,128)(2,1)}) custom-call(f32[16]{0:T(128)S(1)} %copy-done.1, bf16[16,2,4,16,128]{4,3,2,1,0:T(8,128)(2,1)S(1)} %all-to-all-done.1.refs_1_, ...), custom_call_target="tpu_custom_call" | custom-call | tf_op jit(solution)/shard_map/stage/pallas_call | solution.py:330
  41.6 5.1 %all-to-all-start.2 = ((bf16[16,2,4,16,128]{4,3,2,1,0:T(8,128)(2,1)}), bf16[16,2,4,16,128]{4,3,2,1,0:T(8,128)(2,1)S(1)}, u32[]{:S(2)}, u32[]{:S(2)}) async-start(bf16[16,2,4,16,128]{4,3,2,1,0:T(8,128)(2,1)} %get-tuple-element.25), calls=%async_computation.2 | async-start | bytes 1048576 | tf_op jit(solution)/shard_map/all_to_all | solution.py:347
  46.7 1.9 %collective-permute-start.2 = (bf16[2,16,64,128]{3,2,1,0:T(8,128)(2,1)S(1)}, bf16[2,16,64,128]{3,2,1,0:T(8,128)(2,1)S(1)}, u32[]{:S(2)}, u32[]{:S(2)}) collective-permute-start(bf16[2,16,64,128]{3,2,1,0:T(8,128)(2,1)S(1)} %get-tuple-element.26.refs_2_), channel_id=1, source_target_pairs={{0,1},{1,2},{2,3},{3,4},{4,5},{5,6},{6,7},{8,9},{9,10},{10,11},{11... | collective-permute-start | bytes 1572872 | tf_op jit(solution)/shard_map/ppermute | solution.py:343
  48.6 8.2 %all-to-all-done.2.x = bf16[16,2,4,16,128]{4,3,2,1,0:T(8,128)(2,1)S(1)} async-done(((bf16[16,2,4,16,128]{4,3,2,1,0:T(8,128)(2,1)}), bf16[16,2,4,16,128]{4,3,2,1,0:T(8,128)(2,1)S(1)}, u32[]{:S(2)}, u32[]{:S(2)}) %all-to-all-start.2) | async-done | bytes 524320 | tf_op jit(solution)/shard_map/all_to_all | solution.py:347
  56.8 1.8 %self_energy.5 = bf16[16,2,4,16,128]{4,3,2,1,0:T(8,128)(2,1)} custom-call(f32[4,128]{1,0:T(4,128)S(1)} %fusion.keep, bf16[512,256]{1,0:T(8,128)(2,1)S(1)} %copy-done, bf16[16,2,4,16,128]{4,3,2,1,0:T(8,128)(2,1)S(1)} %all-to-all-done.2.x), custom_call_target="tpu_custom_call" | custom-call | tf_op jit(solution)/shard_map/self_energy/pallas_call | solution.py:110
  58.6 3.6 %all-to-all-start.3 = ((bf16[16,2,4,16,128]{4,3,2,1,0:T(8,128)(2,1)}), bf16[16,2,4,16,128]{4,3,2,1,0:T(8,128)(2,1)S(1)}, u32[]{:S(2)}, u32[]{:S(2)}) async-start(bf16[16,2,4,16,128]{4,3,2,1,0:T(8,128)(2,1)} %self_energy.5), calls=%async_computation.3 | async-start | bytes 1048576 | tf_op jit(solution)/shard_map/all_to_all | solution.py:347
  62.2 1.3 collective-permute-start.3
  63.5 7.0 %collective-permute-done.3.refs_5_ = bf16[16,64,128]{2,1,0:T(8,128)(2,1)S(1)} collective-permute-done((bf16[16,64,128]{2,1,0:T(8,128)(2,1)S(1)}, bf16[16,64,128]{2,1,0:T(8,128)(2,1)S(1)}, u32[]{:S(2)}, u32[]{:S(2)}) %collective-permute-start.3) | collective-permute-done | bytes 262176 | tf_op jit(solution)/shard_map/ppermute | solution.py:343
  70.5 0.0 collective-permute-done.2.refs_4_
  70.5 1.8 %all-to-all-done.3.refs_1_ = bf16[16,2,4,16,128]{4,3,2,1,0:T(8,128)(2,1)S(1)} async-done(((bf16[16,2,4,16,128]{4,3,2,1,0:T(8,128)(2,1)}), bf16[16,2,4,16,128]{4,3,2,1,0:T(8,128)(2,1)S(1)}, u32[]{:S(2)}, u32[]{:S(2)}) %all-to-all-start.3) | async-done | bytes 524320 | tf_op jit(solution)/shard_map/all_to_all | solution.py:347
  72.3 3.4 %stage.5 = (f32[2,16,64,128]{3,2,1,0:T(8,128)}, bf16[2,16,64,128]{3,2,1,0:T(8,128)(2,1)S(1)}, bf16[16,64,128]{2,1,0:T(8,128)(2,1)S(1)}, bf16[16,2,4,16,128]{4,3,2,1,0:T(8,128)(2,1)}) custom-call(f32[16]{0:T(128)S(1)} %copy-done.1, bf16[16,2,4,16,128]{4,3,2,1,0:T(8,128)(2,1)S(1)} %all-to-all-done.3.refs_1_, ...), custom_call_target="tpu_custom_call" | custom-call | tf_op jit(solution)/shard_map/stage/pallas_call | solution.py:330
  75.7 5.4 %all-to-all-start.4 = ((bf16[16,2,4,16,128]{4,3,2,1,0:T(8,128)(2,1)}), bf16[16,2,4,16,128]{4,3,2,1,0:T(8,128)(2,1)S(1)}, u32[]{:S(2)}, u32[]{:S(2)}) async-start(bf16[16,2,4,16,128]{4,3,2,1,0:T(8,128)(2,1)} %get-tuple-element.29), calls=%async_computation.4 | async-start | bytes 1048576 | tf_op jit(solution)/shard_map/all_to_all | solution.py:347
  81.1 1.9 %collective-permute-start.4 = (bf16[2,16,64,128]{3,2,1,0:T(8,128)(2,1)S(1)}, bf16[2,16,64,128]{3,2,1,0:T(8,128)(2,1)S(1)}, u32[]{:S(2)}, u32[]{:S(2)}) collective-permute-start(bf16[2,16,64,128]{3,2,1,0:T(8,128)(2,1)S(1)} %get-tuple-element.30.refs_2_), channel_id=1, source_target_pairs={{0,1},{1,2},{2,3},{3,4},{4,5},{5,6},{6,7},{8,9},{9,10},{10,11},{11... | collective-permute-start | bytes 1572872 | tf_op jit(solution)/shard_map/ppermute | solution.py:343
  83.0 8.2 %all-to-all-done.4.x = bf16[16,2,4,16,128]{4,3,2,1,0:T(8,128)(2,1)S(1)} async-done(((bf16[16,2,4,16,128]{4,3,2,1,0:T(8,128)(2,1)}), bf16[16,2,4,16,128]{4,3,2,1,0:T(8,128)(2,1)S(1)}, u32[]{:S(2)}, u32[]{:S(2)}) %all-to-all-start.4) | async-done | bytes 524320 | tf_op jit(solution)/shard_map/all_to_all | solution.py:347
  91.2 1.8 %self_energy.6 = bf16[16,2,4,16,128]{4,3,2,1,0:T(8,128)(2,1)} custom-call(f32[4,128]{1,0:T(4,128)S(1)} %fusion.keep, bf16[512,256]{1,0:T(8,128)(2,1)S(1)} %copy-done, bf16[16,2,4,16,128]{4,3,2,1,0:T(8,128)(2,1)S(1)} %all-to-all-done.4.x), custom_call_target="tpu_custom_call" | custom-call | tf_op jit(solution)/shard_map/self_energy/pallas_call | solution.py:110
  93.0 3.6 %all-to-all-start.5 = ((bf16[16,2,4,16,128]{4,3,2,1,0:T(8,128)(2,1)}), bf16[16,2,4,16,128]{4,3,2,1,0:T(8,128)(2,1)S(1)}, u32[]{:S(2)}, u32[]{:S(2)}) async-start(bf16[16,2,4,16,128]{4,3,2,1,0:T(8,128)(2,1)} %self_energy.6), calls=%async_computation.5 | async-start | bytes 1048576 | tf_op jit(solution)/shard_map/all_to_all | solution.py:347
  96.6 1.3 collective-permute-start.5
  97.9 7.0 %collective-permute-done.5.refs_5_ = bf16[16,64,128]{2,1,0:T(8,128)(2,1)S(1)} collective-permute-done((bf16[16,64,128]{2,1,0:T(8,128)(2,1)S(1)}, bf16[16,64,128]{2,1,0:T(8,128)(2,1)S(1)}, u32[]{:S(2)}, u32[]{:S(2)}) %collective-permute-start.5) | collective-permute-done | bytes 262176 | tf_op jit(solution)/shard_map/ppermute | solution.py:343
  104.9 0.0 collective-permute-done.4.refs_4_
  104.9 1.8 %all-to-all-done.5.refs_1_ = bf16[16,2,4,16,128]{4,3,2,1,0:T(8,128)(2,1)S(1)} async-done(((bf16[16,2,4,16,128]{4,3,2,1,0:T(8,128)(2,1)}), bf16[16,2,4,16,128]{4,3,2,1,0:T(8,128)(2,1)S(1)}, u32[]{:S(2)}, u32[]{:S(2)}) %all-to-all-start.5) | async-done | bytes 524320 | tf_op jit(solution)/shard_map/all_to_all | solution.py:347
  106.7 3.6 %stage.6 = (f32[2,16,64,128]{3,2,1,0:T(8,128)}, bf16[2,16,64,128]{3,2,1,0:T(8,128)(2,1)S(1)}, bf16[16,64,128]{2,1,0:T(8,128)(2,1)S(1)}, bf16[16,2,4,16,128]{4,3,2,1,0:T(8,128)(2,1)}) custom-call(f32[16]{0:T(128)S(1)} %copy-done.1, bf16[16,2,4,16,128]{4,3,2,1,0:T(8,128)(2,1)S(1)} %all-to-all-done.5.refs_1_, ...), custom_call_target="tpu_custom_call" | custom-call | tf_op jit(solution)/shard_map/stage/pallas_call | solution.py:330
  110.3 5.4 %all-to-all-start.6 = ((bf16[16,2,4,16,128]{4,3,2,1,0:T(8,128)(2,1)}), bf16[16,2,4,16,128]{4,3,2,1,0:T(8,128)(2,1)S(1)}, u32[]{:S(2)}, u32[]{:S(2)}) async-start(bf16[16,2,4,16,128]{4,3,2,1,0:T(8,128)(2,1)} %get-tuple-element.33), calls=%async_computation.6 | async-start | bytes 1048576 | tf_op jit(solution)/shard_map/all_to_all | solution.py:347
  115.7 1.9 %collective-permute-start.6 = (bf16[2,16,64,128]{3,2,1,0:T(8,128)(2,1)S(1)}, bf16[2,16,64,128]{3,2,1,0:T(8,128)(2,1)S(1)}, u32[]{:S(2)}, u32[]{:S(2)}) collective-permute-start(bf16[2,16,64,128]{3,2,1,0:T(8,128)(2,1)S(1)} %get-tuple-element.34.refs_2_), channel_id=1, source_target_pairs={{0,1},{1,2},{2,3},{3,4},{4,5},{5,6},{6,7},{8,9},{9,10},{10,11},{11... | collective-permute-start | bytes 1572872 | tf_op jit(solution)/shard_map/ppermute | solution.py:343
  117.6 8.2 %all-to-all-done.6.x = bf16[16,2,4,16,128]{4,3,2,1,0:T(8,128)(2,1)S(1)} async-done(((bf16[16,2,4,16,128]{4,3,2,1,0:T(8,128)(2,1)}), bf16[16,2,4,16,128]{4,3,2,1,0:T(8,128)(2,1)S(1)}, u32[]{:S(2)}, u32[]{:S(2)}) %all-to-all-start.6) | async-done | bytes 524320 | tf_op jit(solution)/shard_map/all_to_all | solution.py:347
  125.8 1.8 %self_energy.7 = bf16[16,2,4,16,128]{4,3,2,1,0:T(8,128)(2,1)} custom-call(f32[4,128]{1,0:T(4,128)S(1)} %fusion.keep, bf16[512,256]{1,0:T(8,128)(2,1)S(1)} %copy-done, bf16[16,2,4,16,128]{4,3,2,1,0:T(8,128)(2,1)S(1)} %all-to-all-done.6.x), custom_call_target="tpu_custom_call" | custom-call | tf_op jit(solution)/shard_map/self_energy/pallas_call | solution.py:110
  127.6 3.6 %all-to-all-start.7 = ((bf16[16,2,4,16,128]{4,3,2,1,0:T(8,128)(2,1)}), bf16[16,2,4,16,128]{4,3,2,1,0:T(8,128)(2,1)S(1)}, u32[]{:S(2)}, u32[]{:S(2)}) async-start(bf16[16,2,4,16,128]{4,3,2,1,0:T(8,128)(2,1)} %self_energy.7), calls=%async_computation.7 | async-start | bytes 1048576 | tf_op jit(solution)/shard_map/all_to_all | solution.py:347
  131.2 1.3 collective-permute-start.7
  132.5 7.0 %collective-permute-done.7.refs_5_ = bf16[16,64,128]{2,1,0:T(8,128)(2,1)S(1)} collective-permute-done((bf16[16,64,128]{2,1,0:T(8,128)(2,1)S(1)}, bf16[16,64,128]{2,1,0:T(8,128)(2,1)S(1)}, u32[]{:S(2)}, u32[]{:S(2)}) %collective-permute-start.7) | collective-permute-done | bytes 262176 | tf_op jit(solution)/shard_map/ppermute | solution.py:343
  139.5 0.0 collective-permute-done.6.refs_4_
  139.5 1.8 %all-to-all-done.7.refs_1_ = bf16[16,2,4,16,128]{4,3,2,1,0:T(8,128)(2,1)S(1)} async-done(((bf16[16,2,4,16,128]{4,3,2,1,0:T(8,128)(2,1)}), bf16[16,2,4,16,128]{4,3,2,1,0:T(8,128)(2,1)S(1)}, u32[]{:S(2)}, u32[]{:S(2)}) %all-to-all-start.7) | async-done | bytes 524320 | tf_op jit(solution)/shard_map/all_to_all | solution.py:347
  141.2 3.8 %stage.7 = f32[2,16,64,128]{3,2,1,0:T(8,128)} custom-call(f32[16]{0:T(128)S(1)} %copy-done.1, bf16[16,2,4,16,128]{4,3,2,1,0:T(8,128)(2,1)S(1)} %all-to-all-done.7.refs_1_, bf16[2,16,64,128]{3,2,1,0:T(8,128)(2,1)S(1)} %get-tuple-element.34.refs_2_, bf16[16,64,128]{2,1,0:T(8,128)(2,1)S(1)} %get-tuple-element.35.refs_3_, ...), custom_call_target="tpu_custom_call" | custom-call | tf_op jit(solution)/shard_map/stage/pallas_call | solution.py:330
  (1 shorter events, 0.0 us)
Async XLA Ops:
  3.5 18.7 %copy-start = (bf16[512,256]{1,0:T(8,128)(2,1)S(1)}, bf16[512,256]{1,0:T(8,128)(2,1)}, u32[]{:S(2)}) copy-start(bf16[512,256]{1,0:T(8,128)(2,1)} %constant.16.clone.table) | copy-start | bytes 786436
  3.5 18.7 %all-to-all-start = ((bf16[16,2,4,16,128]{4,3,2,1,0:T(8,128)(2,1)}), bf16[16,2,4,16,128]{4,3,2,1,0:T(8,128)(2,1)S(1)}, u32[]{:S(2)}, u32[]{:S(2)}) async-start(bf16[16,2,4,16,128]{4,3,2,1,0:T(8,128)(2,1)} %get-tuple-element.21), calls=%async_computation | async-start | bytes 1048576 | tf_op jit(solution)/shard_map/all_to_all | solution.py:347
  10.7 25.5 %collective-permute-start = (bf16[2,16,64,128]{3,2,1,0:T(8,128)(2,1)S(1)}, bf16[2,16,64,128]{3,2,1,0:T(8,128)(2,1)S(1)}, u32[]{:S(2)}, u32[]{:S(2)}) collective-permute-start(bf16[2,16,64,128]{3,2,1,0:T(8,128)(2,1)S(1)} %get-tuple-element.22.refs_2_), channel_id=1, source_target_pairs={{0,1},{1,2},{2,3},{3,4},{4,5},{5,6},{6,7},{8,9},{9,10},{10,11},{11... | collective-permute-start | bytes 1572872 | tf_op jit(solution)/shard_map/ppermute | solution.py:343
  12.6 0.7 copy-start.2
  24.0 13.9 %all-to-all-start.1 = ((bf16[16,2,4,16,128]{4,3,2,1,0:T(8,128)(2,1)}), bf16[16,2,4,16,128]{4,3,2,1,0:T(8,128)(2,1)S(1)}, u32[]{:S(2)}, u32[]{:S(2)}) async-start(bf16[16,2,4,16,128]{4,3,2,1,0:T(8,128)(2,1)} %self_energy.4), calls=%async_computation.1 | async-start | bytes 1048576 | tf_op jit(solution)/shard_map/all_to_all | solution.py:347
  27.6 10.3 %copy-start.1 = (f32[16]{0:T(128)S(1)}, f32[16]{0:T(128)}, u32[]{:S(2)}) copy-start(f32[16]{0:T(128)} %refs_0_.7) | copy-start | bytes 196
  27.6 8.5 %collective-permute-start.1 = (bf16[16,64,128]{2,1,0:T(8,128)(2,1)S(1)}, bf16[16,64,128]{2,1,0:T(8,128)(2,1)S(1)}, u32[]{:S(2)}, u32[]{:S(2)}) collective-permute-start(bf16[16,64,128]{2,1,0:T(8,128)(2,1)S(1)} %get-tuple-element.23.refs_3_), channel_id=1, source_target_pairs={{0,2},{1,3},{2,4},{3,5},{4,6},{5,7},{8,10},{9,11},{10,12},{11,13},... | collective-permute-start | bytes 786440 | tf_op jit(solution)/shard_map/ppermute | solution.py:343
  41.6 15.2 %all-to-all-start.2 = ((bf16[16,2,4,16,128]{4,3,2,1,0:T(8,128)(2,1)}), bf16[16,2,4,16,128]{4,3,2,1,0:T(8,128)(2,1)S(1)}, u32[]{:S(2)}, u32[]{:S(2)}) async-start(bf16[16,2,4,16,128]{4,3,2,1,0:T(8,128)(2,1)} %get-tuple-element.25), calls=%async_computation.2 | async-start | bytes 1048576 | tf_op jit(solution)/shard_map/all_to_all | solution.py:347
  46.7 23.8 %collective-permute-start.2 = (bf16[2,16,64,128]{3,2,1,0:T(8,128)(2,1)S(1)}, bf16[2,16,64,128]{3,2,1,0:T(8,128)(2,1)S(1)}, u32[]{:S(2)}, u32[]{:S(2)}) collective-permute-start(bf16[2,16,64,128]{3,2,1,0:T(8,128)(2,1)S(1)} %get-tuple-element.26.refs_2_), channel_id=1, source_target_pairs={{0,1},{1,2},{2,3},{3,4},{4,5},{5,6},{6,7},{8,9},{9,10},{10,11},{11... | collective-permute-start | bytes 1572872 | tf_op jit(solution)/shard_map/ppermute | solution.py:343
  58.6 13.7 %all-to-all-start.3 = ((bf16[16,2,4,16,128]{4,3,2,1,0:T(8,128)(2,1)}), bf16[16,2,4,16,128]{4,3,2,1,0:T(8,128)(2,1)S(1)}, u32[]{:S(2)}, u32[]{:S(2)}) async-start(bf16[16,2,4,16,128]{4,3,2,1,0:T(8,128)(2,1)} %self_energy.5), calls=%async_computation.3 | async-start | bytes 1048576 | tf_op jit(solution)/shard_map/all_to_all | solution.py:347
  62.2 8.3 %collective-permute-start.3 = (bf16[16,64,128]{2,1,0:T(8,128)(2,1)S(1)}, bf16[16,64,128]{2,1,0:T(8,128)(2,1)S(1)}, u32[]{:S(2)}, u32[]{:S(2)}) collective-permute-start(bf16[16,64,128]{2,1,0:T(8,128)(2,1)S(1)} %get-tuple-element.27.refs_3_), channel_id=1, source_target_pairs={{0,2},{1,3},{2,4},{3,5},{4,6},{5,7},{8,10},{9,11},{10,12},{11,13},... | collective-permute-start | bytes 786440 | tf_op jit(solution)/shard_map/ppermute | solution.py:343
  75.7 15.5 %all-to-all-start.4 = ((bf16[16,2,4,16,128]{4,3,2,1,0:T(8,128)(2,1)}), bf16[16,2,4,16,128]{4,3,2,1,0:T(8,128)(2,1)S(1)}, u32[]{:S(2)}, u32[]{:S(2)}) async-start(bf16[16,2,4,16,128]{4,3,2,1,0:T(8,128)(2,1)} %get-tuple-element.29), calls=%async_computation.4 | async-start | bytes 1048576 | tf_op jit(solution)/shard_map/all_to_all | solution.py:347
  81.1 23.8 %collective-permute-start.4 = (bf16[2,16,64,128]{3,2,1,0:T(8,128)(2,1)S(1)}, bf16[2,16,64,128]{3,2,1,0:T(8,128)(2,1)S(1)}, u32[]{:S(2)}, u32[]{:S(2)}) collective-permute-start(bf16[2,16,64,128]{3,2,1,0:T(8,128)(2,1)S(1)} %get-tuple-element.30.refs_2_), channel_id=1, source_target_pairs={{0,1},{1,2},{2,3},{3,4},{4,5},{5,6},{6,7},{8,9},{9,10},{10,11},{11... | collective-permute-start | bytes 1572872 | tf_op jit(solution)/shard_map/ppermute | solution.py:343
  93.0 13.6 %all-to-all-start.5 = ((bf16[16,2,4,16,128]{4,3,2,1,0:T(8,128)(2,1)}), bf16[16,2,4,16,128]{4,3,2,1,0:T(8,128)(2,1)S(1)}, u32[]{:S(2)}, u32[]{:S(2)}) async-start(bf16[16,2,4,16,128]{4,3,2,1,0:T(8,128)(2,1)} %self_energy.6), calls=%async_computation.5 | async-start | bytes 1048576 | tf_op jit(solution)/shard_map/all_to_all | solution.py:347
  96.6 8.3 %collective-permute-start.5 = (bf16[16,64,128]{2,1,0:T(8,128)(2,1)S(1)}, bf16[16,64,128]{2,1,0:T(8,128)(2,1)S(1)}, u32[]{:S(2)}, u32[]{:S(2)}) collective-permute-start(bf16[16,64,128]{2,1,0:T(8,128)(2,1)S(1)} %get-tuple-element.31.refs_3_), channel_id=1, source_target_pairs={{0,2},{1,3},{2,4},{3,5},{4,6},{5,7},{8,10},{9,11},{10,12},{11,13},... | collective-permute-start | bytes 786440 | tf_op jit(solution)/shard_map/ppermute | solution.py:343
  110.3 15.5 %all-to-all-start.6 = ((bf16[16,2,4,16,128]{4,3,2,1,0:T(8,128)(2,1)}), bf16[16,2,4,16,128]{4,3,2,1,0:T(8,128)(2,1)S(1)}, u32[]{:S(2)}, u32[]{:S(2)}) async-start(bf16[16,2,4,16,128]{4,3,2,1,0:T(8,128)(2,1)} %get-tuple-element.33), calls=%async_computation.6 | async-start | bytes 1048576 | tf_op jit(solution)/shard_map/all_to_all | solution.py:347
  115.7 23.8 %collective-permute-start.6 = (bf16[2,16,64,128]{3,2,1,0:T(8,128)(2,1)S(1)}, bf16[2,16,64,128]{3,2,1,0:T(8,128)(2,1)S(1)}, u32[]{:S(2)}, u32[]{:S(2)}) collective-permute-start(bf16[2,16,64,128]{3,2,1,0:T(8,128)(2,1)S(1)} %get-tuple-element.34.refs_2_), channel_id=1, source_target_pairs={{0,1},{1,2},{2,3},{3,4},{4,5},{5,6},{6,7},{8,9},{9,10},{10,11},{11... | collective-permute-start | bytes 1572872 | tf_op jit(solution)/shard_map/ppermute | solution.py:343
  127.6 13.7 %all-to-all-start.7 = ((bf16[16,2,4,16,128]{4,3,2,1,0:T(8,128)(2,1)}), bf16[16,2,4,16,128]{4,3,2,1,0:T(8,128)(2,1)S(1)}, u32[]{:S(2)}, u32[]{:S(2)}) async-start(bf16[16,2,4,16,128]{4,3,2,1,0:T(8,128)(2,1)} %self_energy.7), calls=%async_computation.7 | async-start | bytes 1048576 | tf_op jit(solution)/shard_map/all_to_all | solution.py:347
  131.2 8.3 %collective-permute-start.7 = (bf16[16,64,128]{2,1,0:T(8,128)(2,1)S(1)}, bf16[16,64,128]{2,1,0:T(8,128)(2,1)S(1)}, u32[]{:S(2)}, u32[]{:S(2)}) collective-permute-start(bf16[16,64,128]{2,1,0:T(8,128)(2,1)S(1)} %get-tuple-element.35.refs_3_), channel_id=1, source_target_pairs={{0,2},{1,3},{2,4},{3,5},{4,6},{5,7},{8,10},{9,11},{10,12},{11,13},... | collective-permute-start | bytes 786440 | tf_op jit(solution)/shard_map/ppermute | solution.py:343

commit v2 on v1

--- a/solution.py
+++ b/solution.py
@@ -16,7 +16,6 @@
 PITCH = 17
 KB = 8
 STEPS = OWN // KB
-PIECES = 4
 MIB = 2**20
 
 quadrature = 0.0625
@@ -131,59 +130,63 @@
     return move
 
 
-def send_chunk(turned, block, chunk, sems):
-    copies = []
-    for first in range(0, GROUP, GROUP // PIECES):
-        here = pl.ds(first, GROUP // PIECES)
-        for d in range(first, first + GROUP // PIECES):
-            for c in range(2):
-                for j in range(PART):
-                    t = (d * PART + j) * PITCH
-                    block[d, c, j] = turned[c, t : t + OWN, :].astype(BF16)
-        sem = sems.at[len(copies)]
-        copies.append(pltpu.make_async_copy(block.at[here], chunk.at[here], sem))
-        copies[-1].start()
-    return copies
-
-
-def emit(k, value, turned, near, far):
+def chunk_copy(block, chunk, sems, q):
+    here = pl.ds(q * (GROUP // STEPS), GROUP // STEPS)
+    return pltpu.make_async_copy(block.at[here], chunk.at[here], sems.at[q])
+
+
+def pack_chunk(turned, block, q):
+    for d in range(q * (GROUP // STEPS), (q + 1) * (GROUP // STEPS)):
+        for c in range(2):
+            for j in range(PART):
+                t = (d * PART + j) * PITCH
+                block[d, c, j] = turned[c, t : t + OWN, :].astype(BF16)
+
+
+def emit(turned, near, far):
     row, lane = grids()
     causal = lane <= row
-    low = []
-    for c in range(2):
-        turned[c, pl.ds(k, ROWS, stride=PITCH), :] = value[c]
-        near[c, k] = value[c].astype(BF16)
-        low.append(jnp.where(causal, value[c], 0.0))
-    far[k] = (low[0] + half_turn(low[1])).astype(BF16)
+
+    def step(q, carry):
+        for i in range(4):
+            k = q * 4 + i
+            low = []
+            for c in range(2):
+                value = turned[c, pl.ds(k, ROWS, stride=PITCH), :]
+                near[c, k] = value.astype(BF16)
+                low.append(jnp.where(causal, value, 0.0))
+            far[k] = (low[0] + half_turn(low[1])).astype(BF16)
+        return carry
+
+    lax.fori_loop(0, OWN // 4, step, 0)
 
 
 def prepare_kernel(x_in, out, near, far, chunk, x, y, turned, block, sems, sem):
-    load = mover([(x_in, x)], sems, 0, 4)
-    pairs = [(y, out)]
-    save = mover(pairs, sems, 1, 4)
-    for q in range(OWN // 4):
+    load = mover([(x_in, x)], sems, 0)
+    save = mover([(y, out)], sems, 1)
+    for q in range(STEPS):
         load(0, q).start()
 
     def step(q, carry):
         load(0, q).wait()
-        for i in range(4):
-            k = q * 4 + i
-            value = [turn_over(x[c, k]) for c in range(2)]
-            for c in range(2):
-                y[c, k] = value[c]
-            emit(k, value, turned, near, far)
+        for i in range(KB):
+            k = q * KB + i
+            for c in range(2):
+                value = turn_over(x[c, k])
+                y[c, k] = value
+                turned[c, pl.ds(k, ROWS, stride=PITCH), :] = value
         return carry
 
-    lax.fori_loop(0, OWN // 4, step, 0)
-    copies = send_chunk(turned, block, chunk, sem)
-    for n in range(len(pairs)):
-        for q in range(OWN // 4):
-            save(n, q).start()
-    for n in range(len(pairs)):
-        for q in range(OWN // 4):
-            save(n, q).wait()
-    for copy in copies:
-        copy.wait()
+    lax.fori_loop(0, STEPS, step, 0)
+    for q in range(STEPS):
+        pack_chunk(turned, block, q)
+        chunk_copy(block, chunk, sem, q).start()
+    for q in range(STEPS):
+        save(0, q).start()
+    emit(turned, near, far)
+    for q in range(STEPS):
+        chunk_copy(block, chunk, sem, q).wait()
+        save(0, q).wait()
 
 
 WIDE = pltpu.HBM(STATE, F32)
@@ -194,7 +197,7 @@
     return [
         pltpu.VMEM(STATE, BF16),
         pltpu.VMEM(FAR, BF16),
-        pltpu.VMEM((2, ROWS * PITCH, MEM), F32),
+        pltpu.VMEM((2, (ROWS + 1) * PITCH, MEM), F32),
         pltpu.VMEM(CHUNK, BF16),
     ]
 
@@ -208,7 +211,7 @@
         out_shape=[WIDE] + EMITTED,
         scratch_shapes=[scratch, scratch]
         + emitting()[2:]
-        + [pltpu.SemaphoreType.DMA((2, OWN // 4)), pltpu.SemaphoreType.DMA((PIECES,))],
+        + [pltpu.SemaphoreType.DMA((2, STEPS)), pltpu.SemaphoreType.DMA((STEPS,))],
         compiler_params=params(16),
         name="prepare",
     )(pltpu.with_memory_space_constraint(x, pltpu.HBM))
@@ -281,6 +284,9 @@
             )
             for c in range(2):
                 result[c, k] = quadrature * collide[c]
+        return carry
+
+    def advance(q, carry):
         for n in range(len(loads)):
             load(n, q).wait()
         for i in range(KB):
@@ -300,15 +306,21 @@
                 for c in range(2):
                     result[c, k] = turn_over(value[c]) if last else value[c]
             if not last:
-                emit(k, value, turned, mine, low)
+                for c in range(2):
+                    turned[c, pl.ds(k, ROWS, stride=PITCH), :] = value[c]
         for n in range(len(saves)):
             save(n, q).start()
         return carry
 
     lax.fori_loop(0, STEPS, step, 0)
+    lax.fori_loop(0, STEPS, advance, 0)
     if not last:
-        for copy in send_chunk(turned, block, chunk, chunk_sem):
-            copy.wait()
+        for q in range(STEPS):
+            pack_chunk(turned, block, q)
+            chunk_copy(block, chunk, chunk_sem, q).start()
+        emit(turned, mine, low)
+        for q in range(STEPS):
+            chunk_copy(block, chunk, chunk_sem, q).wait()
     for q in range(STEPS):
         for n in range(len(saves)):
             save(n, q).wait()
@@ -316,13 +328,13 @@
 
 def stage(first, last, energies, sigma, own, own_low, near, far, base):
     state = pltpu.VMEM(STATE, F32)
-    scratch = [state, state, pltpu.VMEM((2, ROWS * PITCH, MEM), F32)]
+    scratch = [state, state, pltpu.VMEM((2, (ROWS + 1) * PITCH, MEM), F32)]
     scratch += [pltpu.SemaphoreType.DMA((2, STEPS))]
     out_shape, spaces = [WIDE], [HBM]
     if not last:
         out_shape += EMITTED
         spaces += [VMEM, VMEM, HBM]
-        scratch += emitting()[2:] + [pltpu.SemaphoreType.DMA((PIECES,))]
+        scratch += emitting()[2:] + [pltpu.SemaphoreType.DMA((STEPS,))]
 
     def kernel(*refs):
         stage_kernel(first, last, *refs)

time: 146 us -> 144 us (0.986)
  Pallas kernels: 25.2 us -> 22.8 us
    pallas_call x4, Pallas kernels: 14.5 us -> 12.4 us  [stage(): pl.pallas_call(kernel, in_specs=[SMEM] + [VMEM] * 5 + [HBM], out_specs=sp...]
where the time goes in v2:
time: 144 us; the launch traced here: 143 us
  waiting for transfers between devices  68.5 us (48%)
  starting transfers between devices  50.2 us (35%)
  Pallas kernels  22.8 us (16%)
    all_to_all x8, waiting for transfers between devices, exchange(): return lax.all_to_all(block, 'ka', split_axis=0, concat_axis=0, tiled=True)  40.4 us
    all_to_all x8, starting transfers between devices, exchange(): return lax.all_to_all(block, 'ka', split_axis=0, concat_axis=0, tiled=True)  37.4 us
    ppermute x8, waiting for transfers between devices, from_behind(): lax.ppermute(block, 'ta', [(i - distance, i) for i in range(distance, cou...  28.1 us
    ppermute x8, starting transfers between devices, from_behind(): lax.ppermute(block, 'ta', [(i - distance, i) for i in range(distance, cou...  12.9 us
    pallas_call x4, Pallas kernels, stage(): pl.pallas_call(kernel, in_specs=[SMEM] + [VMEM] * 5 + [HBM], out_specs=sp...  12.4 us
    pallas_call x4, Pallas kernels, self_energy(): pl.pallas_call(self_energy_kernel, in_specs=[VMEM, VMEM, VMEM], out_specs...  7.3 us
    pallas_call x1, Pallas kernels, prepare(): pl.pallas_call(prepare_kernel, in_specs=[HBM], out_specs=[HBM, VMEM, VMEM...  3.1 us
  transfers between devices with their start and end apart: 16, of which 12 were waited for; matrix products, arithmetic and copies ran while one was open for 0% of the time, Pallas kernels for 5%

profile of v2, /device:TPU:96, one launch (start us, length us, event | category | flops | bytes accessed | tf_op | source)
XLA Modules:
  0.0 142.6 jit_solution(421445759228910564)
XLA Ops:
  0.0 3.1 %prepare.1 = (f32[2,16,64,128]{3,2,1,0:T(8,128)}, bf16[2,16,64,128]{3,2,1,0:T(8,128)(2,1)S(1)}, bf16[16,64,128]{2,1,0:T(8,128)(2,1)S(1)}, bf16[16,2,4,16,128]{4,3,2,1,0:T(8,128)(2,1)}) custom-call(f32[2,16,64,128]{3,2,1,0:T(8,128)} %x_in.1), custom_call_target="tpu_custom_call" | custom-call | tf_op jit(solution)/shard_map/prepare/pallas_call | solution.py:207
  3.1 0.0 copy-start
  3.1 7.2 %all-to-all-start = ((bf16[16,2,4,16,128]{4,3,2,1,0:T(8,128)(2,1)}), bf16[16,2,4,16,128]{4,3,2,1,0:T(8,128)(2,1)S(1)}, u32[]{:S(2)}, u32[]{:S(2)}) async-start(bf16[16,2,4,16,128]{4,3,2,1,0:T(8,128)(2,1)} %get-tuple-element.21), calls=%async_computation | async-start | bytes 1048576 | tf_op jit(solution)/shard_map/all_to_all | solution.py:359
  10.3 1.9 %collective-permute-start = (bf16[2,16,64,128]{3,2,1,0:T(8,128)(2,1)S(1)}, bf16[2,16,64,128]{3,2,1,0:T(8,128)(2,1)S(1)}, u32[]{:S(2)}, u32[]{:S(2)}) collective-permute-start(bf16[2,16,64,128]{3,2,1,0:T(8,128)(2,1)S(1)} %get-tuple-element.22.refs_2_), channel_id=1, source_target_pairs={{0,1},{1,2},{2,3},{3,4},{4,5},{5,6},{6,7},{8,9},{9,10},{10,11},{11... | collective-permute-start | bytes 1572872 | tf_op jit(solution)/shard_map/ppermute | solution.py:355
  12.2 0.0 copy-start.2
  12.3 0.6 copy-done.2
  12.9 0.1 dynamic_slice.3
  13.0 0.1 fusion.keep
  13.1 8.7 %all-to-all-done.x = bf16[16,2,4,16,128]{4,3,2,1,0:T(8,128)(2,1)S(1)} async-done(((bf16[16,2,4,16,128]{4,3,2,1,0:T(8,128)(2,1)}), bf16[16,2,4,16,128]{4,3,2,1,0:T(8,128)(2,1)S(1)}, u32[]{:S(2)}, u32[]{:S(2)}) %all-to-all-start) | async-done | bytes 524320 | tf_op jit(solution)/shard_map/all_to_all | solution.py:359
  21.8 0.0 copy-done
  21.8 1.8 %self_energy.4 = bf16[16,2,4,16,128]{4,3,2,1,0:T(8,128)(2,1)} custom-call(f32[4,128]{1,0:T(4,128)S(1)} %fusion.keep, bf16[512,256]{1,0:T(8,128)(2,1)S(1)} %copy-done, bf16[16,2,4,16,128]{4,3,2,1,0:T(8,128)(2,1)S(1)} %all-to-all-done.x), custom_call_target="tpu_custom_call" | custom-call | tf_op jit(solution)/shard_map/self_energy/pallas_call | solution.py:109
  23.6 3.6 %all-to-all-start.1 = ((bf16[16,2,4,16,128]{4,3,2,1,0:T(8,128)(2,1)}), bf16[16,2,4,16,128]{4,3,2,1,0:T(8,128)(2,1)S(1)}, u32[]{:S(2)}, u32[]{:S(2)}) async-start(bf16[16,2,4,16,128]{4,3,2,1,0:T(8,128)(2,1)} %self_energy.4), calls=%async_computation.1 | async-start | bytes 1048576 | tf_op jit(solution)/shard_map/all_to_all | solution.py:359
  27.2 0.0 copy-start.1
  27.2 1.3 collective-permute-start.1
  28.5 7.2 %collective-permute-done.1.refs_5_ = bf16[16,64,128]{2,1,0:T(8,128)(2,1)S(1)} collective-permute-done((bf16[16,64,128]{2,1,0:T(8,128)(2,1)S(1)}, bf16[16,64,128]{2,1,0:T(8,128)(2,1)S(1)}, u32[]{:S(2)}, u32[]{:S(2)}) %collective-permute-start.1) | collective-permute-done | bytes 262176 | tf_op jit(solution)/shard_map/ppermute | solution.py:355
  35.8 0.0 collective-permute-done.refs_4_
  35.8 1.8 %all-to-all-done.1.refs_1_ = bf16[16,2,4,16,128]{4,3,2,1,0:T(8,128)(2,1)S(1)} async-done(((bf16[16,2,4,16,128]{4,3,2,1,0:T(8,128)(2,1)}), bf16[16,2,4,16,128]{4,3,2,1,0:T(8,128)(2,1)S(1)}, u32[]{:S(2)}, u32[]{:S(2)}) %all-to-all-start.1) | async-done | bytes 524320 | tf_op jit(solution)/shard_map/all_to_all | solution.py:359
  37.6 0.0 copy-done.1
  37.6 3.1 %stage.4 = (f32[2,16,64,128]{3,2,1,0:T(8,128)}, bf16[2,16,64,128]{3,2,1,0:T(8,128)(2,1)S(1)}, bf16[16,64,128]{2,1,0:T(8,128)(2,1)S(1)}, bf16[16,2,4,16,128]{4,3,2,1,0:T(8,128)(2,1)}) custom-call(f32[16]{0:T(128)S(1)} %copy-done.1, bf16[16,2,4,16,128]{4,3,2,1,0:T(8,128)(2,1)S(1)} %all-to-all-done.1.refs_1_, ...), custom_call_target="tpu_custom_call" | custom-call | tf_op jit(solution)/shard_map/stage/pallas_call | solution.py:342
  40.7 5.1 %all-to-all-start.2 = ((bf16[16,2,4,16,128]{4,3,2,1,0:T(8,128)(2,1)}), bf16[16,2,4,16,128]{4,3,2,1,0:T(8,128)(2,1)S(1)}, u32[]{:S(2)}, u32[]{:S(2)}) async-start(bf16[16,2,4,16,128]{4,3,2,1,0:T(8,128)(2,1)} %get-tuple-element.25), calls=%async_computation.2 | async-start | bytes 1048576 | tf_op jit(solution)/shard_map/all_to_all | solution.py:359
  45.8 1.9 %collective-permute-start.2 = (bf16[2,16,64,128]{3,2,1,0:T(8,128)(2,1)S(1)}, bf16[2,16,64,128]{3,2,1,0:T(8,128)(2,1)S(1)}, u32[]{:S(2)}, u32[]{:S(2)}) collective-permute-start(bf16[2,16,64,128]{3,2,1,0:T(8,128)(2,1)S(1)} %get-tuple-element.26.refs_2_), channel_id=1, source_target_pairs={{0,1},{1,2},{2,3},{3,4},{4,5},{5,6},{6,7},{8,9},{9,10},{10,11},{11... | collective-permute-start | bytes 1572872 | tf_op jit(solution)/shard_map/ppermute | solution.py:355
  47.7 8.2 %all-to-all-done.2.x = bf16[16,2,4,16,128]{4,3,2,1,0:T(8,128)(2,1)S(1)} async-done(((bf16[16,2,4,16,128]{4,3,2,1,0:T(8,128)(2,1)}), bf16[16,2,4,16,128]{4,3,2,1,0:T(8,128)(2,1)S(1)}, u32[]{:S(2)}, u32[]{:S(2)}) %all-to-all-start.2) | async-done | bytes 524320 | tf_op jit(solution)/shard_map/all_to_all | solution.py:359
  55.9 1.8 %self_energy.5 = bf16[16,2,4,16,128]{4,3,2,1,0:T(8,128)(2,1)} custom-call(f32[4,128]{1,0:T(4,128)S(1)} %fusion.keep, bf16[512,256]{1,0:T(8,128)(2,1)S(1)} %copy-done, bf16[16,2,4,16,128]{4,3,2,1,0:T(8,128)(2,1)S(1)} %all-to-all-done.2.x), custom_call_target="tpu_custom_call" | custom-call | tf_op jit(solution)/shard_map/self_energy/pallas_call | solution.py:109
  57.7 3.6 %all-to-all-start.3 = ((bf16[16,2,4,16,128]{4,3,2,1,0:T(8,128)(2,1)}), bf16[16,2,4,16,128]{4,3,2,1,0:T(8,128)(2,1)S(1)}, u32[]{:S(2)}, u32[]{:S(2)}) async-start(bf16[16,2,4,16,128]{4,3,2,1,0:T(8,128)(2,1)} %self_energy.5), calls=%async_computation.3 | async-start | bytes 1048576 | tf_op jit(solution)/shard_map/all_to_all | solution.py:359
  61.3 1.3 collective-permute-start.3
  62.6 7.0 %collective-permute-done.3.refs_5_ = bf16[16,64,128]{2,1,0:T(8,128)(2,1)S(1)} collective-permute-done((bf16[16,64,128]{2,1,0:T(8,128)(2,1)S(1)}, bf16[16,64,128]{2,1,0:T(8,128)(2,1)S(1)}, u32[]{:S(2)}, u32[]{:S(2)}) %collective-permute-start.3) | collective-permute-done | bytes 262176 | tf_op jit(solution)/shard_map/ppermute | solution.py:355
  69.6 0.0 collective-permute-done.2.refs_4_
  69.6 1.8 %all-to-all-done.3.refs_1_ = bf16[16,2,4,16,128]{4,3,2,1,0:T(8,128)(2,1)S(1)} async-done(((bf16[16,2,4,16,128]{4,3,2,1,0:T(8,128)(2,1)}), bf16[16,2,4,16,128]{4,3,2,1,0:T(8,128)(2,1)S(1)}, u32[]{:S(2)}, u32[]{:S(2)}) %all-to-all-start.3) | async-done | bytes 524320 | tf_op jit(solution)/shard_map/all_to_all | solution.py:359
  71.4 2.9 %stage.5 = (f32[2,16,64,128]{3,2,1,0:T(8,128)}, bf16[2,16,64,128]{3,2,1,0:T(8,128)(2,1)S(1)}, bf16[16,64,128]{2,1,0:T(8,128)(2,1)S(1)}, bf16[16,2,4,16,128]{4,3,2,1,0:T(8,128)(2,1)}) custom-call(f32[16]{0:T(128)S(1)} %copy-done.1, bf16[16,2,4,16,128]{4,3,2,1,0:T(8,128)(2,1)S(1)} %all-to-all-done.3.refs_1_, ...), custom_call_target="tpu_custom_call" | custom-call | tf_op jit(solution)/shard_map/stage/pallas_call | solution.py:342
  74.3 5.4 %all-to-all-start.4 = ((bf16[16,2,4,16,128]{4,3,2,1,0:T(8,128)(2,1)}), bf16[16,2,4,16,128]{4,3,2,1,0:T(8,128)(2,1)S(1)}, u32[]{:S(2)}, u32[]{:S(2)}) async-start(bf16[16,2,4,16,128]{4,3,2,1,0:T(8,128)(2,1)} %get-tuple-element.29), calls=%async_computation.4 | async-start | bytes 1048576 | tf_op jit(solution)/shard_map/all_to_all | solution.py:359
  79.7 1.9 %collective-permute-start.4 = (bf16[2,16,64,128]{3,2,1,0:T(8,128)(2,1)S(1)}, bf16[2,16,64,128]{3,2,1,0:T(8,128)(2,1)S(1)}, u32[]{:S(2)}, u32[]{:S(2)}) collective-permute-start(bf16[2,16,64,128]{3,2,1,0:T(8,128)(2,1)S(1)} %get-tuple-element.30.refs_2_), channel_id=1, source_target_pairs={{0,1},{1,2},{2,3},{3,4},{4,5},{5,6},{6,7},{8,9},{9,10},{10,11},{11... | collective-permute-start | bytes 1572872 | tf_op jit(solution)/shard_map/ppermute | solution.py:355
  81.6 8.2 %all-to-all-done.4.x = bf16[16,2,4,16,128]{4,3,2,1,0:T(8,128)(2,1)S(1)} async-done(((bf16[16,2,4,16,128]{4,3,2,1,0:T(8,128)(2,1)}), bf16[16,2,4,16,128]{4,3,2,1,0:T(8,128)(2,1)S(1)}, u32[]{:S(2)}, u32[]{:S(2)}) %all-to-all-start.4) | async-done | bytes 524320 | tf_op jit(solution)/shard_map/all_to_all | solution.py:359
  89.8 1.8 %self_energy.6 = bf16[16,2,4,16,128]{4,3,2,1,0:T(8,128)(2,1)} custom-call(f32[4,128]{1,0:T(4,128)S(1)} %fusion.keep, bf16[512,256]{1,0:T(8,128)(2,1)S(1)} %copy-done, bf16[16,2,4,16,128]{4,3,2,1,0:T(8,128)(2,1)S(1)} %all-to-all-done.4.x), custom_call_target="tpu_custom_call" | custom-call | tf_op jit(solution)/shard_map/self_energy/pallas_call | solution.py:109
  91.6 3.6 %all-to-all-start.5 = ((bf16[16,2,4,16,128]{4,3,2,1,0:T(8,128)(2,1)}), bf16[16,2,4,16,128]{4,3,2,1,0:T(8,128)(2,1)S(1)}, u32[]{:S(2)}, u32[]{:S(2)}) async-start(bf16[16,2,4,16,128]{4,3,2,1,0:T(8,128)(2,1)} %self_energy.6), calls=%async_computation.5 | async-start | bytes 1048576 | tf_op jit(solution)/shard_map/all_to_all | solution.py:359
  95.2 1.3 collective-permute-start.5
  96.5 7.0 %collective-permute-done.5.refs_5_ = bf16[16,64,128]{2,1,0:T(8,128)(2,1)S(1)} collective-permute-done((bf16[16,64,128]{2,1,0:T(8,128)(2,1)S(1)}, bf16[16,64,128]{2,1,0:T(8,128)(2,1)S(1)}, u32[]{:S(2)}, u32[]{:S(2)}) %collective-permute-start.5) | collective-permute-done | bytes 262176 | tf_op jit(solution)/shard_map/ppermute | solution.py:355
  103.5 0.0 collective-permute-done.4.refs_4_
  103.5 1.8 %all-to-all-done.5.refs_1_ = bf16[16,2,4,16,128]{4,3,2,1,0:T(8,128)(2,1)S(1)} async-done(((bf16[16,2,4,16,128]{4,3,2,1,0:T(8,128)(2,1)}), bf16[16,2,4,16,128]{4,3,2,1,0:T(8,128)(2,1)S(1)}, u32[]{:S(2)}, u32[]{:S(2)}) %all-to-all-start.5) | async-done | bytes 524320 | tf_op jit(solution)/shard_map/all_to_all | solution.py:359
  105.3 3.1 %stage.6 = (f32[2,16,64,128]{3,2,1,0:T(8,128)}, bf16[2,16,64,128]{3,2,1,0:T(8,128)(2,1)S(1)}, bf16[16,64,128]{2,1,0:T(8,128)(2,1)S(1)}, bf16[16,2,4,16,128]{4,3,2,1,0:T(8,128)(2,1)}) custom-call(f32[16]{0:T(128)S(1)} %copy-done.1, bf16[16,2,4,16,128]{4,3,2,1,0:T(8,128)(2,1)S(1)} %all-to-all-done.5.refs_1_, ...), custom_call_target="tpu_custom_call" | custom-call | tf_op jit(solution)/shard_map/stage/pallas_call | solution.py:342
  108.4 5.4 %all-to-all-start.6 = ((bf16[16,2,4,16,128]{4,3,2,1,0:T(8,128)(2,1)}), bf16[16,2,4,16,128]{4,3,2,1,0:T(8,128)(2,1)S(1)}, u32[]{:S(2)}, u32[]{:S(2)}) async-start(bf16[16,2,4,16,128]{4,3,2,1,0:T(8,128)(2,1)} %get-tuple-element.33), calls=%async_computation.6 | async-start | bytes 1048576 | tf_op jit(solution)/shard_map/all_to_all | solution.py:359
  113.7 1.9 %collective-permute-start.6 = (bf16[2,16,64,128]{3,2,1,0:T(8,128)(2,1)S(1)}, bf16[2,16,64,128]{3,2,1,0:T(8,128)(2,1)S(1)}, u32[]{:S(2)}, u32[]{:S(2)}) collective-permute-start(bf16[2,16,64,128]{3,2,1,0:T(8,128)(2,1)S(1)} %get-tuple-element.34.refs_2_), channel_id=1, source_target_pairs={{0,1},{1,2},{2,3},{3,4},{4,5},{5,6},{6,7},{8,9},{9,10},{10,11},{11... | collective-permute-start | bytes 1572872 | tf_op jit(solution)/shard_map/ppermute | solution.py:355
  115.7 8.2 %all-to-all-done.6.x = bf16[16,2,4,16,128]{4,3,2,1,0:T(8,128)(2,1)S(1)} async-done(((bf16[16,2,4,16,128]{4,3,2,1,0:T(8,128)(2,1)}), bf16[16,2,4,16,128]{4,3,2,1,0:T(8,128)(2,1)S(1)}, u32[]{:S(2)}, u32[]{:S(2)}) %all-to-all-start.6) | async-done | bytes 524320 | tf_op jit(solution)/shard_map/all_to_all | solution.py:359
  123.8 1.8 %self_energy.7 = bf16[16,2,4,16,128]{4,3,2,1,0:T(8,128)(2,1)} custom-call(f32[4,128]{1,0:T(4,128)S(1)} %fusion.keep, bf16[512,256]{1,0:T(8,128)(2,1)S(1)} %copy-done, bf16[16,2,4,16,128]{4,3,2,1,0:T(8,128)(2,1)S(1)} %all-to-all-done.6.x), custom_call_target="tpu_custom_call" | custom-call | tf_op jit(solution)/shard_map/self_energy/pallas_call | solution.py:109
  125.7 3.6 %all-to-all-start.7 = ((bf16[16,2,4,16,128]{4,3,2,1,0:T(8,128)(2,1)}), bf16[16,2,4,16,128]{4,3,2,1,0:T(8,128)(2,1)S(1)}, u32[]{:S(2)}, u32[]{:S(2)}) async-start(bf16[16,2,4,16,128]{4,3,2,1,0:T(8,128)(2,1)} %self_energy.7), calls=%async_computation.7 | async-start | bytes 1048576 | tf_op jit(solution)/shard_map/all_to_all | solution.py:359
  129.2 1.3 collective-permute-start.7
  130.5 7.0 %collective-permute-done.7.refs_5_ = bf16[16,64,128]{2,1,0:T(8,128)(2,1)S(1)} collective-permute-done((bf16[16,64,128]{2,1,0:T(8,128)(2,1)S(1)}, bf16[16,64,128]{2,1,0:T(8,128)(2,1)S(1)}, u32[]{:S(2)}, u32[]{:S(2)}) %collective-permute-start.7) | collective-permute-done | bytes 262176 | tf_op jit(solution)/shard_map/ppermute | solution.py:355
  137.5 0.0 collective-permute-done.6.refs_4_
  137.5 1.8 %all-to-all-done.7.refs_1_ = bf16[16,2,4,16,128]{4,3,2,1,0:T(8,128)(2,1)S(1)} async-done(((bf16[16,2,4,16,128]{4,3,2,1,0:T(8,128)(2,1)}), bf16[16,2,4,16,128]{4,3,2,1,0:T(8,128)(2,1)S(1)}, u32[]{:S(2)}, u32[]{:S(2)}) %all-to-all-start.7) | async-done | bytes 524320 | tf_op jit(solution)/shard_map/all_to_all | solution.py:359
  139.3 3.3 %stage.7 = f32[2,16,64,128]{3,2,1,0:T(8,128)} custom-call(f32[16]{0:T(128)S(1)} %copy-done.1, bf16[16,2,4,16,128]{4,3,2,1,0:T(8,128)(2,1)S(1)} %all-to-all-done.7.refs_1_, bf16[2,16,64,128]{3,2,1,0:T(8,128)(2,1)S(1)} %get-tuple-element.34.refs_2_, bf16[16,64,128]{2,1,0:T(8,128)(2,1)S(1)} %get-tuple-element.35.refs_3_, ...), custom_call_target="tpu_custom_call" | custom-call | tf_op jit(solution)/shard_map/stage/pallas_call | solution.py:342
  (1 shorter events, 0.0 us)
Async XLA Ops:
  3.1 18.7 %copy-start = (bf16[512,256]{1,0:T(8,128)(2,1)S(1)}, bf16[512,256]{1,0:T(8,128)(2,1)}, u32[]{:S(2)}) copy-start(bf16[512,256]{1,0:T(8,128)(2,1)} %constant.16.clone.table) | copy-start | bytes 786436
  3.1 18.7 %all-to-all-start = ((bf16[16,2,4,16,128]{4,3,2,1,0:T(8,128)(2,1)}), bf16[16,2,4,16,128]{4,3,2,1,0:T(8,128)(2,1)S(1)}, u32[]{:S(2)}, u32[]{:S(2)}) async-start(bf16[16,2,4,16,128]{4,3,2,1,0:T(8,128)(2,1)} %get-tuple-element.21), calls=%async_computation | async-start | bytes 1048576 | tf_op jit(solution)/shard_map/all_to_all | solution.py:359
  10.3 25.5 %collective-permute-start = (bf16[2,16,64,128]{3,2,1,0:T(8,128)(2,1)S(1)}, bf16[2,16,64,128]{3,2,1,0:T(8,128)(2,1)S(1)}, u32[]{:S(2)}, u32[]{:S(2)}) collective-permute-start(bf16[2,16,64,128]{3,2,1,0:T(8,128)(2,1)S(1)} %get-tuple-element.22.refs_2_), channel_id=1, source_target_pairs={{0,1},{1,2},{2,3},{3,4},{4,5},{5,6},{6,7},{8,9},{9,10},{10,11},{11... | collective-permute-start | bytes 1572872 | tf_op jit(solution)/shard_map/ppermute | solution.py:355
  12.2 0.7 copy-start.2
  23.6 13.9 %all-to-all-start.1 = ((bf16[16,2,4,16,128]{4,3,2,1,0:T(8,128)(2,1)}), bf16[16,2,4,16,128]{4,3,2,1,0:T(8,128)(2,1)S(1)}, u32[]{:S(2)}, u32[]{:S(2)}) async-start(bf16[16,2,4,16,128]{4,3,2,1,0:T(8,128)(2,1)} %self_energy.4), calls=%async_computation.1 | async-start | bytes 1048576 | tf_op jit(solution)/shard_map/all_to_all | solution.py:359
  27.2 10.3 %copy-start.1 = (f32[16]{0:T(128)S(1)}, f32[16]{0:T(128)}, u32[]{:S(2)}) copy-start(f32[16]{0:T(128)} %refs_0_.7) | copy-start | bytes 196
  27.2 8.5 %collective-permute-start.1 = (bf16[16,64,128]{2,1,0:T(8,128)(2,1)S(1)}, bf16[16,64,128]{2,1,0:T(8,128)(2,1)S(1)}, u32[]{:S(2)}, u32[]{:S(2)}) collective-permute-start(bf16[16,64,128]{2,1,0:T(8,128)(2,1)S(1)} %get-tuple-element.23.refs_3_), channel_id=1, source_target_pairs={{0,2},{1,3},{2,4},{3,5},{4,6},{5,7},{8,10},{9,11},{10,12},{11,13},... | collective-permute-start | bytes 786440 | tf_op jit(solution)/shard_map/ppermute | solution.py:355
  40.7 15.2 %all-to-all-start.2 = ((bf16[16,2,4,16,128]{4,3,2,1,0:T(8,128)(2,1)}), bf16[16,2,4,16,128]{4,3,2,1,0:T(8,128)(2,1)S(1)}, u32[]{:S(2)}, u32[]{:S(2)}) async-start(bf16[16,2,4,16,128]{4,3,2,1,0:T(8,128)(2,1)} %get-tuple-element.25), calls=%async_computation.2 | async-start | bytes 1048576 | tf_op jit(solution)/shard_map/all_to_all | solution.py:359
  45.8 23.8 %collective-permute-start.2 = (bf16[2,16,64,128]{3,2,1,0:T(8,128)(2,1)S(1)}, bf16[2,16,64,128]{3,2,1,0:T(8,128)(2,1)S(1)}, u32[]{:S(2)}, u32[]{:S(2)}) collective-permute-start(bf16[2,16,64,128]{3,2,1,0:T(8,128)(2,1)S(1)} %get-tuple-element.26.refs_2_), channel_id=1, source_target_pairs={{0,1},{1,2},{2,3},{3,4},{4,5},{5,6},{6,7},{8,9},{9,10},{10,11},{11... | collective-permute-start | bytes 1572872 | tf_op jit(solution)/shard_map/ppermute | solution.py:355
  57.7 13.7 %all-to-all-start.3 = ((bf16[16,2,4,16,128]{4,3,2,1,0:T(8,128)(2,1)}), bf16[16,2,4,16,128]{4,3,2,1,0:T(8,128)(2,1)S(1)}, u32[]{:S(2)}, u32[]{:S(2)}) async-start(bf16[16,2,4,16,128]{4,3,2,1,0:T(8,128)(2,1)} %self_energy.5), calls=%async_computation.3 | async-start | bytes 1048576 | tf_op jit(solution)/shard_map/all_to_all | solution.py:359
  61.3 8.3 %collective-permute-start.3 = (bf16[16,64,128]{2,1,0:T(8,128)(2,1)S(1)}, bf16[16,64,128]{2,1,0:T(8,128)(2,1)S(1)}, u32[]{:S(2)}, u32[]{:S(2)}) collective-permute-start(bf16[16,64,128]{2,1,0:T(8,128)(2,1)S(1)} %get-tuple-element.27.refs_3_), channel_id=1, source_target_pairs={{0,2},{1,3},{2,4},{3,5},{4,6},{5,7},{8,10},{9,11},{10,12},{11,13},... | collective-permute-start | bytes 786440 | tf_op jit(solution)/shard_map/ppermute | solution.py:355
  74.3 15.5 %all-to-all-start.4 = ((bf16[16,2,4,16,128]{4,3,2,1,0:T(8,128)(2,1)}), bf16[16,2,4,16,128]{4,3,2,1,0:T(8,128)(2,1)S(1)}, u32[]{:S(2)}, u32[]{:S(2)}) async-start(bf16[16,2,4,16,128]{4,3,2,1,0:T(8,128)(2,1)} %get-tuple-element.29), calls=%async_computation.4 | async-start | bytes 1048576 | tf_op jit(solution)/shard_map/all_to_all | solution.py:359
  79.7 23.8 %collective-permute-start.4 = (bf16[2,16,64,128]{3,2,1,0:T(8,128)(2,1)S(1)}, bf16[2,16,64,128]{3,2,1,0:T(8,128)(2,1)S(1)}, u32[]{:S(2)}, u32[]{:S(2)}) collective-permute-start(bf16[2,16,64,128]{3,2,1,0:T(8,128)(2,1)S(1)} %get-tuple-element.30.refs_2_), channel_id=1, source_target_pairs={{0,1},{1,2},{2,3},{3,4},{4,5},{5,6},{6,7},{8,9},{9,10},{10,11},{11... | collective-permute-start | bytes 1572872 | tf_op jit(solution)/shard_map/ppermute | solution.py:355
  91.6 13.6 %all-to-all-start.5 = ((bf16[16,2,4,16,128]{4,3,2,1,0:T(8,128)(2,1)}), bf16[16,2,4,16,128]{4,3,2,1,0:T(8,128)(2,1)S(1)}, u32[]{:S(2)}, u32[]{:S(2)}) async-start(bf16[16,2,4,16,128]{4,3,2,1,0:T(8,128)(2,1)} %self_energy.6), calls=%async_computation.5 | async-start | bytes 1048576 | tf_op jit(solution)/shard_map/all_to_all | solution.py:359
  95.2 8.3 %collective-permute-start.5 = (bf16[16,64,128]{2,1,0:T(8,128)(2,1)S(1)}, bf16[16,64,128]{2,1,0:T(8,128)(2,1)S(1)}, u32[]{:S(2)}, u32[]{:S(2)}) collective-permute-start(bf16[16,64,128]{2,1,0:T(8,128)(2,1)S(1)} %get-tuple-element.31.refs_3_), channel_id=1, source_target_pairs={{0,2},{1,3},{2,4},{3,5},{4,6},{5,7},{8,10},{9,11},{10,12},{11,13},... | collective-permute-start | bytes 786440 | tf_op jit(solution)/shard_map/ppermute | solution.py:355
  108.4 15.5 %all-to-all-start.6 = ((bf16[16,2,4,16,128]{4,3,2,1,0:T(8,128)(2,1)}), bf16[16,2,4,16,128]{4,3,2,1,0:T(8,128)(2,1)S(1)}, u32[]{:S(2)}, u32[]{:S(2)}) async-start(bf16[16,2,4,16,128]{4,3,2,1,0:T(8,128)(2,1)} %get-tuple-element.33), calls=%async_computation.6 | async-start | bytes 1048576 | tf_op jit(solution)/shard_map/all_to_all | solution.py:359
  113.7 23.8 %collective-permute-start.6 = (bf16[2,16,64,128]{3,2,1,0:T(8,128)(2,1)S(1)}, bf16[2,16,64,128]{3,2,1,0:T(8,128)(2,1)S(1)}, u32[]{:S(2)}, u32[]{:S(2)}) collective-permute-start(bf16[2,16,64,128]{3,2,1,0:T(8,128)(2,1)S(1)} %get-tuple-element.34.refs_2_), channel_id=1, source_target_pairs={{0,1},{1,2},{2,3},{3,4},{4,5},{5,6},{6,7},{8,9},{9,10},{10,11},{11... | collective-permute-start | bytes 1572872 | tf_op jit(solution)/shard_map/ppermute | solution.py:355
  125.7 13.7 %all-to-all-start.7 = ((bf16[16,2,4,16,128]{4,3,2,1,0:T(8,128)(2,1)}), bf16[16,2,4,16,128]{4,3,2,1,0:T(8,128)(2,1)S(1)}, u32[]{:S(2)}, u32[]{:S(2)}) async-start(bf16[16,2,4,16,128]{4,3,2,1,0:T(8,128)(2,1)} %self_energy.7), calls=%async_computation.7 | async-start | bytes 1048576 | tf_op jit(solution)/shard_map/all_to_all | solution.py:359
  129.2 8.3 %collective-permute-start.7 = (bf16[16,64,128]{2,1,0:T(8,128)(2,1)S(1)}, bf16[16,64,128]{2,1,0:T(8,128)(2,1)S(1)}, u32[]{:S(2)}, u32[]{:S(2)}) collective-permute-start(bf16[16,64,128]{2,1,0:T(8,128)(2,1)S(1)} %get-tuple-element.35.refs_3_), channel_id=1, source_target_pairs={{0,2},{1,3},{2,4},{3,5},{4,6},{5,7},{8,10},{9,11},{10,12},{11,13},... | collective-permute-start | bytes 786440 | tf_op jit(solution)/shard_map/ppermute | solution.py:355

commit v3 on v2

--- a/solution.py
+++ b/solution.py
@@ -97,7 +97,6 @@
 STATE = (2, OWN, ROWS, MEM)
 FAR = (OWN, ROWS, MEM)
 HBM = pl.BlockSpec(memory_space=pltpu.HBM)
-SMEM = pl.BlockSpec(memory_space=pltpu.SMEM)
 VMEM = pl.BlockSpec(memory_space=pltpu.VMEM)
 
 
@@ -219,11 +218,13 @@
 
 def stage_kernel(first, last, *refs):
     refs = list(refs)
-    energies, sigma, own, own_low, near, far, base_in = refs[:7]
+    sigma, own, own_low, near, far, base_in = refs[:6]
+    refs = refs[6:]
+    energies = refs.pop(0) if first else None
     if last:
-        out, base, result, held, sems = refs[7:]
+        out, base, result, held, sems = refs
     else:
-        out, mine, low, chunk, base, result, held, sems, turned, block, chunk_sem = refs[7:]
+        out, mine, low, chunk, base, result, held, sems, turned, block, chunk_sem = refs
 
     loads = [(base_in, base)]
     saves = [(result, out)]
@@ -294,7 +295,7 @@
             collide = result[0, k], result[1, k]
             half = 0.5 * step_size
             if first:
-                energy = energies[k]
+                energy = energies[pl.ds(k, 1), :]
                 xr, xi = base[0, k], base[1, k]
                 fr = energy * xi + collide[1]
                 fi = -(energy * xr + collide[0])
@@ -339,15 +340,20 @@
     def kernel(*refs):
         stage_kernel(first, last, *refs)
 
+    operands = [sigma, own, own_low, near, far, pltpu.with_memory_space_constraint(base, pltpu.HBM)]
+    in_specs = [VMEM] * 5 + [HBM]
+    if first:
+        operands.append(energies)
+        in_specs.append(VMEM)
     return pl.pallas_call(
         kernel,
-        in_specs=[SMEM] + [VMEM] * 5 + [HBM],
+        in_specs=in_specs,
         out_specs=spaces,
         out_shape=out_shape,
         scratch_shapes=scratch,
         compiler_params=params(16),
         name="stage",
-    )(energies, sigma, own, own_low, near, far, pltpu.with_memory_space_constraint(base, pltpu.HBM))
+    )(*operands)
 
 
 def from_behind(block, distance):
@@ -365,6 +371,8 @@
     lag = (time - lax.broadcasted_iota(jnp.int32, (PART, MEM), 1)) & (MEM - 1)
     mine = lax.dynamic_slice_in_dim(reach, lax.axis_index("ka") * PART, PART)
     keep = (lag < mine[:, None]).astype(F32)
+
+    energies = jnp.broadcast_to(energies[:, None], (OWN, MEM))
 
     def inputs(own, low, chunk):
         spread = exchange(chunk)

time: 144 us -> 142 us (0.986)
  Pallas kernels: 22.8 us -> 20.7 us
    pallas_call x4, Pallas kernels: 12.4 us -> 10.2 us  [stage(): pl.pallas_call(kernel, in_specs=in_specs, out_specs=spaces, out_shape=out...]
where the time goes in v3:
time: 142 us; the launch traced here: 141 us
  waiting for transfers between devices  68.5 us (48%)
  starting transfers between devices  50.2 us (35%)
  Pallas kernels  20.7 us (15%)
    all_to_all x8, waiting for transfers between devices, exchange(): return lax.all_to_all(block, 'ka', split_axis=0, concat_axis=0, tiled=True)  40.4 us
    all_to_all x8, starting transfers between devices, exchange(): return lax.all_to_all(block, 'ka', split_axis=0, concat_axis=0, tiled=True)  37.4 us
    ppermute x8, waiting for transfers between devices, from_behind(): lax.ppermute(block, 'ta', [(i - distance, i) for i in range(distance, cou...  28.1 us
    ppermute x8, starting transfers between devices, from_behind(): lax.ppermute(block, 'ta', [(i - distance, i) for i in range(distance, cou...  12.9 us
    pallas_call x4, Pallas kernels, stage(): pl.pallas_call(kernel, in_specs=in_specs, out_specs=spaces, out_shape=out...  10.2 us
    pallas_call x4, Pallas kernels, self_energy(): pl.pallas_call(self_energy_kernel, in_specs=[VMEM, VMEM, VMEM], out_specs...  7.3 us
    pallas_call x1, Pallas kernels, prepare(): pl.pallas_call(prepare_kernel, in_specs=[HBM], out_specs=[HBM, VMEM, VMEM...  3.1 us
  transfers between devices with their start and end apart: 16, of which 12 were waited for; matrix products, arithmetic and copies ran while one was open for 0% of the time, Pallas kernels for 5%

profile of v3, /device:TPU:96, one launch (start us, length us, event | category | flops | bytes accessed | tf_op | source)
XLA Modules:
  0.0 140.5 jit_solution(4484014481940510760)
XLA Ops:
  0.0 3.1 %prepare.1 = (f32[2,16,64,128]{3,2,1,0:T(8,128)}, bf16[2,16,64,128]{3,2,1,0:T(8,128)(2,1)S(1)}, bf16[16,64,128]{2,1,0:T(8,128)(2,1)S(1)}, bf16[16,2,4,16,128]{4,3,2,1,0:T(8,128)(2,1)}) custom-call(f32[2,16,64,128]{3,2,1,0:T(8,128)} %x_in.1), custom_call_target="tpu_custom_call" | custom-call | tf_op jit(solution)/shard_map/prepare/pallas_call | solution.py:206
  3.1 0.0 copy-start
  3.1 7.2 %all-to-all-start = ((bf16[16,2,4,16,128]{4,3,2,1,0:T(8,128)(2,1)}), bf16[16,2,4,16,128]{4,3,2,1,0:T(8,128)(2,1)S(1)}, u32[]{:S(2)}, u32[]{:S(2)}) async-start(bf16[16,2,4,16,128]{4,3,2,1,0:T(8,128)(2,1)} %get-tuple-element.21), calls=%async_computation | async-start | bytes 1048576 | tf_op jit(solution)/shard_map/all_to_all | solution.py:365
  10.3 1.9 %collective-permute-start = (bf16[2,16,64,128]{3,2,1,0:T(8,128)(2,1)S(1)}, bf16[2,16,64,128]{3,2,1,0:T(8,128)(2,1)S(1)}, u32[]{:S(2)}, u32[]{:S(2)}) collective-permute-start(bf16[2,16,64,128]{3,2,1,0:T(8,128)(2,1)S(1)} %get-tuple-element.22.refs_1_), channel_id=1, source_target_pairs={{0,1},{1,2},{2,3},{3,4},{4,5},{5,6},{6,7},{8,9},{9,10},{10,11},{11... | collective-permute-start | bytes 1572872 | tf_op jit(solution)/shard_map/ppermute | solution.py:361
  12.2 0.0 copy-start.2
  12.3 0.6 copy-done.2
  12.9 0.1 dynamic_slice.3
  13.0 0.1 fusion.keep
  13.1 8.7 %all-to-all-done.x = bf16[16,2,4,16,128]{4,3,2,1,0:T(8,128)(2,1)S(1)} async-done(((bf16[16,2,4,16,128]{4,3,2,1,0:T(8,128)(2,1)}), bf16[16,2,4,16,128]{4,3,2,1,0:T(8,128)(2,1)S(1)}, u32[]{:S(2)}, u32[]{:S(2)}) %all-to-all-start) | async-done | bytes 524320 | tf_op jit(solution)/shard_map/all_to_all | solution.py:365
  21.8 0.0 copy-done
  21.8 1.8 %self_energy.4 = bf16[16,2,4,16,128]{4,3,2,1,0:T(8,128)(2,1)} custom-call(f32[4,128]{1,0:T(4,128)S(1)} %fusion.keep, bf16[512,256]{1,0:T(8,128)(2,1)S(1)} %copy-done, bf16[16,2,4,16,128]{4,3,2,1,0:T(8,128)(2,1)S(1)} %all-to-all-done.x), custom_call_target="tpu_custom_call" | custom-call | tf_op jit(solution)/shard_map/self_energy/pallas_call | solution.py:108
  23.6 3.6 %all-to-all-start.1 = ((bf16[16,2,4,16,128]{4,3,2,1,0:T(8,128)(2,1)}), bf16[16,2,4,16,128]{4,3,2,1,0:T(8,128)(2,1)S(1)}, u32[]{:S(2)}, u32[]{:S(2)}) async-start(bf16[16,2,4,16,128]{4,3,2,1,0:T(8,128)(2,1)} %self_energy.4), calls=%async_computation.1 | async-start | bytes 1048576 | tf_op jit(solution)/shard_map/all_to_all | solution.py:365
  27.2 0.0 copy-start.1
  27.2 1.3 collective-permute-start.1
  28.5 7.2 %collective-permute-done.1.refs_4_ = bf16[16,64,128]{2,1,0:T(8,128)(2,1)S(1)} collective-permute-done((bf16[16,64,128]{2,1,0:T(8,128)(2,1)S(1)}, bf16[16,64,128]{2,1,0:T(8,128)(2,1)S(1)}, u32[]{:S(2)}, u32[]{:S(2)}) %collective-permute-start.1) | collective-permute-done | bytes 262176 | tf_op jit(solution)/shard_map/ppermute | solution.py:361
  35.8 0.0 collective-permute-done.refs_3_
  35.8 1.8 %all-to-all-done.1.refs_0_ = bf16[16,2,4,16,128]{4,3,2,1,0:T(8,128)(2,1)S(1)} async-done(((bf16[16,2,4,16,128]{4,3,2,1,0:T(8,128)(2,1)}), bf16[16,2,4,16,128]{4,3,2,1,0:T(8,128)(2,1)S(1)}, u32[]{:S(2)}, u32[]{:S(2)}) %all-to-all-start.1) | async-done | bytes 524320 | tf_op jit(solution)/shard_map/all_to_all | solution.py:365
  37.6 0.0 copy-done.1
  37.6 0.1 broadcast_in_dim.2.refs_6_
  37.6 2.5 %stage.4 = (f32[2,16,64,128]{3,2,1,0:T(8,128)}, bf16[2,16,64,128]{3,2,1,0:T(8,128)(2,1)S(1)}, bf16[16,64,128]{2,1,0:T(8,128)(2,1)S(1)}, bf16[16,2,4,16,128]{4,3,2,1,0:T(8,128)(2,1)}) custom-call(bf16[16,2,4,16,128]{4,3,2,1,0:T(8,128)(2,1)S(1)} %all-to-all-done.1.refs_0_, bf16[2,16,64,128]{3,2,1,0:T(8,128)(2,1)S(1)} %get-tuple-element.22.refs_1_, ...), custom_call_target="tpu_custom_call" | custom-call | tf_op jit(solution)/shard_map/stage/pallas_call | solution.py:348
  40.2 5.1 %all-to-all-start.2 = ((bf16[16,2,4,16,128]{4,3,2,1,0:T(8,128)(2,1)}), bf16[16,2,4,16,128]{4,3,2,1,0:T(8,128)(2,1)S(1)}, u32[]{:S(2)}, u32[]{:S(2)}) async-start(bf16[16,2,4,16,128]{4,3,2,1,0:T(8,128)(2,1)} %get-tuple-element.25), calls=%async_computation.2 | async-start | bytes 1048576 | tf_op jit(solution)/shard_map/all_to_all | solution.py:365
  45.3 1.9 %collective-permute-start.2 = (bf16[2,16,64,128]{3,2,1,0:T(8,128)(2,1)S(1)}, bf16[2,16,64,128]{3,2,1,0:T(8,128)(2,1)S(1)}, u32[]{:S(2)}, u32[]{:S(2)}) collective-permute-start(bf16[2,16,64,128]{3,2,1,0:T(8,128)(2,1)S(1)} %get-tuple-element.26.refs_1_), channel_id=1, source_target_pairs={{0,1},{1,2},{2,3},{3,4},{4,5},{5,6},{6,7},{8,9},{9,10},{10,11},{11... | collective-permute-start | bytes 1572872 | tf_op jit(solution)/shard_map/ppermute | solution.py:361
  47.2 8.2 %all-to-all-done.2.x = bf16[16,2,4,16,128]{4,3,2,1,0:T(8,128)(2,1)S(1)} async-done(((bf16[16,2,4,16,128]{4,3,2,1,0:T(8,128)(2,1)}), bf16[16,2,4,16,128]{4,3,2,1,0:T(8,128)(2,1)S(1)}, u32[]{:S(2)}, u32[]{:S(2)}) %all-to-all-start.2) | async-done | bytes 524320 | tf_op jit(solution)/shard_map/all_to_all | solution.py:365
  55.4 1.8 %self_energy.5 = bf16[16,2,4,16,128]{4,3,2,1,0:T(8,128)(2,1)} custom-call(f32[4,128]{1,0:T(4,128)S(1)} %fusion.keep, bf16[512,256]{1,0:T(8,128)(2,1)S(1)} %copy-done, bf16[16,2,4,16,128]{4,3,2,1,0:T(8,128)(2,1)S(1)} %all-to-all-done.2.x), custom_call_target="tpu_custom_call" | custom-call | tf_op jit(solution)/shard_map/self_energy/pallas_call | solution.py:108
  57.2 3.6 %all-to-all-start.3 = ((bf16[16,2,4,16,128]{4,3,2,1,0:T(8,128)(2,1)}), bf16[16,2,4,16,128]{4,3,2,1,0:T(8,128)(2,1)S(1)}, u32[]{:S(2)}, u32[]{:S(2)}) async-start(bf16[16,2,4,16,128]{4,3,2,1,0:T(8,128)(2,1)} %self_energy.5), calls=%async_computation.3 | async-start | bytes 1048576 | tf_op jit(solution)/shard_map/all_to_all | solution.py:365
  60.8 1.3 collective-permute-start.3
  62.1 7.0 %collective-permute-done.3.refs_4_ = bf16[16,64,128]{2,1,0:T(8,128)(2,1)S(1)} collective-permute-done((bf16[16,64,128]{2,1,0:T(8,128)(2,1)S(1)}, bf16[16,64,128]{2,1,0:T(8,128)(2,1)S(1)}, u32[]{:S(2)}, u32[]{:S(2)}) %collective-permute-start.3) | collective-permute-done | bytes 262176 | tf_op jit(solution)/shard_map/ppermute | solution.py:361
  69.1 0.0 collective-permute-done.2.refs_3_
  69.1 1.8 %all-to-all-done.3.refs_0_ = bf16[16,2,4,16,128]{4,3,2,1,0:T(8,128)(2,1)S(1)} async-done(((bf16[16,2,4,16,128]{4,3,2,1,0:T(8,128)(2,1)}), bf16[16,2,4,16,128]{4,3,2,1,0:T(8,128)(2,1)S(1)}, u32[]{:S(2)}, u32[]{:S(2)}) %all-to-all-start.3) | async-done | bytes 524320 | tf_op jit(solution)/shard_map/all_to_all | solution.py:365
  70.9 2.4 %stage.5 = (f32[2,16,64,128]{3,2,1,0:T(8,128)}, bf16[2,16,64,128]{3,2,1,0:T(8,128)(2,1)S(1)}, bf16[16,64,128]{2,1,0:T(8,128)(2,1)S(1)}, bf16[16,2,4,16,128]{4,3,2,1,0:T(8,128)(2,1)}) custom-call(bf16[16,2,4,16,128]{4,3,2,1,0:T(8,128)(2,1)S(1)} %all-to-all-done.3.refs_0_, bf16[2,16,64,128]{3,2,1,0:T(8,128)(2,1)S(1)} %get-tuple-element.26.refs_1_, ...), custom_call_target="tpu_custom_call" | custom-call | tf_op jit(solution)/shard_map/stage/pallas_call | solution.py:348
  73.3 5.4 %all-to-all-start.4 = ((bf16[16,2,4,16,128]{4,3,2,1,0:T(8,128)(2,1)}), bf16[16,2,4,16,128]{4,3,2,1,0:T(8,128)(2,1)S(1)}, u32[]{:S(2)}, u32[]{:S(2)}) async-start(bf16[16,2,4,16,128]{4,3,2,1,0:T(8,128)(2,1)} %get-tuple-element.29), calls=%async_computation.4 | async-start | bytes 1048576 | tf_op jit(solution)/shard_map/all_to_all | solution.py:365
  78.6 1.9 %collective-permute-start.4 = (bf16[2,16,64,128]{3,2,1,0:T(8,128)(2,1)S(1)}, bf16[2,16,64,128]{3,2,1,0:T(8,128)(2,1)S(1)}, u32[]{:S(2)}, u32[]{:S(2)}) collective-permute-start(bf16[2,16,64,128]{3,2,1,0:T(8,128)(2,1)S(1)} %get-tuple-element.30.refs_1_), channel_id=1, source_target_pairs={{0,1},{1,2},{2,3},{3,4},{4,5},{5,6},{6,7},{8,9},{9,10},{10,11},{11... | collective-permute-start | bytes 1572872 | tf_op jit(solution)/shard_map/ppermute | solution.py:361
  80.6 8.2 %all-to-all-done.4.x = bf16[16,2,4,16,128]{4,3,2,1,0:T(8,128)(2,1)S(1)} async-done(((bf16[16,2,4,16,128]{4,3,2,1,0:T(8,128)(2,1)}), bf16[16,2,4,16,128]{4,3,2,1,0:T(8,128)(2,1)S(1)}, u32[]{:S(2)}, u32[]{:S(2)}) %all-to-all-start.4) | async-done | bytes 524320 | tf_op jit(solution)/shard_map/all_to_all | solution.py:365
  88.7 1.8 %self_energy.6 = bf16[16,2,4,16,128]{4,3,2,1,0:T(8,128)(2,1)} custom-call(f32[4,128]{1,0:T(4,128)S(1)} %fusion.keep, bf16[512,256]{1,0:T(8,128)(2,1)S(1)} %copy-done, bf16[16,2,4,16,128]{4,3,2,1,0:T(8,128)(2,1)S(1)} %all-to-all-done.4.x), custom_call_target="tpu_custom_call" | custom-call | tf_op jit(solution)/shard_map/self_energy/pallas_call | solution.py:108
  90.6 3.6 %all-to-all-start.5 = ((bf16[16,2,4,16,128]{4,3,2,1,0:T(8,128)(2,1)}), bf16[16,2,4,16,128]{4,3,2,1,0:T(8,128)(2,1)S(1)}, u32[]{:S(2)}, u32[]{:S(2)}) async-start(bf16[16,2,4,16,128]{4,3,2,1,0:T(8,128)(2,1)} %self_energy.6), calls=%async_computation.5 | async-start | bytes 1048576 | tf_op jit(solution)/shard_map/all_to_all | solution.py:365
  94.2 1.3 collective-permute-start.5
  95.5 7.0 %collective-permute-done.5.refs_4_ = bf16[16,64,128]{2,1,0:T(8,128)(2,1)S(1)} collective-permute-done((bf16[16,64,128]{2,1,0:T(8,128)(2,1)S(1)}, bf16[16,64,128]{2,1,0:T(8,128)(2,1)S(1)}, u32[]{:S(2)}, u32[]{:S(2)}) %collective-permute-start.5) | collective-permute-done | bytes 262176 | tf_op jit(solution)/shard_map/ppermute | solution.py:361
  102.4 0.0 collective-permute-done.4.refs_3_
  102.4 1.8 %all-to-all-done.5.refs_0_ = bf16[16,2,4,16,128]{4,3,2,1,0:T(8,128)(2,1)S(1)} async-done(((bf16[16,2,4,16,128]{4,3,2,1,0:T(8,128)(2,1)}), bf16[16,2,4,16,128]{4,3,2,1,0:T(8,128)(2,1)S(1)}, u32[]{:S(2)}, u32[]{:S(2)}) %all-to-all-start.5) | async-done | bytes 524320 | tf_op jit(solution)/shard_map/all_to_all | solution.py:365
  104.2 2.5 %stage.6 = (f32[2,16,64,128]{3,2,1,0:T(8,128)}, bf16[2,16,64,128]{3,2,1,0:T(8,128)(2,1)S(1)}, bf16[16,64,128]{2,1,0:T(8,128)(2,1)S(1)}, bf16[16,2,4,16,128]{4,3,2,1,0:T(8,128)(2,1)}) custom-call(bf16[16,2,4,16,128]{4,3,2,1,0:T(8,128)(2,1)S(1)} %all-to-all-done.5.refs_0_, bf16[2,16,64,128]{3,2,1,0:T(8,128)(2,1)S(1)} %get-tuple-element.30.refs_1_, ...), custom_call_target="tpu_custom_call" | custom-call | tf_op jit(solution)/shard_map/stage/pallas_call | solution.py:348
  106.8 5.4 %all-to-all-start.6 = ((bf16[16,2,4,16,128]{4,3,2,1,0:T(8,128)(2,1)}), bf16[16,2,4,16,128]{4,3,2,1,0:T(8,128)(2,1)S(1)}, u32[]{:S(2)}, u32[]{:S(2)}) async-start(bf16[16,2,4,16,128]{4,3,2,1,0:T(8,128)(2,1)} %get-tuple-element.33), calls=%async_computation.6 | async-start | bytes 1048576 | tf_op jit(solution)/shard_map/all_to_all | solution.py:365
  112.2 1.9 %collective-permute-start.6 = (bf16[2,16,64,128]{3,2,1,0:T(8,128)(2,1)S(1)}, bf16[2,16,64,128]{3,2,1,0:T(8,128)(2,1)S(1)}, u32[]{:S(2)}, u32[]{:S(2)}) collective-permute-start(bf16[2,16,64,128]{3,2,1,0:T(8,128)(2,1)S(1)} %get-tuple-element.34.refs_1_), channel_id=1, source_target_pairs={{0,1},{1,2},{2,3},{3,4},{4,5},{5,6},{6,7},{8,9},{9,10},{10,11},{11... | collective-permute-start | bytes 1572872 | tf_op jit(solution)/shard_map/ppermute | solution.py:361
  114.1 8.2 %all-to-all-done.6.x = bf16[16,2,4,16,128]{4,3,2,1,0:T(8,128)(2,1)S(1)} async-done(((bf16[16,2,4,16,128]{4,3,2,1,0:T(8,128)(2,1)}), bf16[16,2,4,16,128]{4,3,2,1,0:T(8,128)(2,1)S(1)}, u32[]{:S(2)}, u32[]{:S(2)}) %all-to-all-start.6) | async-done | bytes 524320 | tf_op jit(solution)/shard_map/all_to_all | solution.py:365
  122.3 1.8 %self_energy.7 = bf16[16,2,4,16,128]{4,3,2,1,0:T(8,128)(2,1)} custom-call(f32[4,128]{1,0:T(4,128)S(1)} %fusion.keep, bf16[512,256]{1,0:T(8,128)(2,1)S(1)} %copy-done, bf16[16,2,4,16,128]{4,3,2,1,0:T(8,128)(2,1)S(1)} %all-to-all-done.6.x), custom_call_target="tpu_custom_call" | custom-call | tf_op jit(solution)/shard_map/self_energy/pallas_call | solution.py:108
  124.1 3.6 %all-to-all-start.7 = ((bf16[16,2,4,16,128]{4,3,2,1,0:T(8,128)(2,1)}), bf16[16,2,4,16,128]{4,3,2,1,0:T(8,128)(2,1)S(1)}, u32[]{:S(2)}, u32[]{:S(2)}) async-start(bf16[16,2,4,16,128]{4,3,2,1,0:T(8,128)(2,1)} %self_energy.7), calls=%async_computation.7 | async-start | bytes 1048576 | tf_op jit(solution)/shard_map/all_to_all | solution.py:365
  127.7 1.3 collective-permute-start.7
  129.0 7.0 %collective-permute-done.7.refs_4_ = bf16[16,64,128]{2,1,0:T(8,128)(2,1)S(1)} collective-permute-done((bf16[16,64,128]{2,1,0:T(8,128)(2,1)S(1)}, bf16[16,64,128]{2,1,0:T(8,128)(2,1)S(1)}, u32[]{:S(2)}, u32[]{:S(2)}) %collective-permute-start.7) | collective-permute-done | bytes 262176 | tf_op jit(solution)/shard_map/ppermute | solution.py:361
  135.9 0.0 collective-permute-done.6.refs_3_
  135.9 1.8 %all-to-all-done.7.refs_0_ = bf16[16,2,4,16,128]{4,3,2,1,0:T(8,128)(2,1)S(1)} async-done(((bf16[16,2,4,16,128]{4,3,2,1,0:T(8,128)(2,1)}), bf16[16,2,4,16,128]{4,3,2,1,0:T(8,128)(2,1)S(1)}, u32[]{:S(2)}, u32[]{:S(2)}) %all-to-all-start.7) | async-done | bytes 524320 | tf_op jit(solution)/shard_map/all_to_all | solution.py:365
  137.7 2.8 %stage.7 = f32[2,16,64,128]{3,2,1,0:T(8,128)} custom-call(bf16[16,2,4,16,128]{4,3,2,1,0:T(8,128)(2,1)S(1)} %all-to-all-done.7.refs_0_, bf16[2,16,64,128]{3,2,1,0:T(8,128)(2,1)S(1)} %get-tuple-element.34.refs_1_, bf16[16,64,128]{2,1,0:T(8,128)(2,1)S(1)} %get-tuple-element.35.refs_2_, bf16[2,16,64,128]{3,2,1,0:T(8,128)(2,1)S(1)} %collective-permute-done.6.refs_3_, ...), custom_call_target="tpu_custom_call" | custom-call | tf_op jit(solution)/shard_map/stage/pallas_call | solution.py:348
  (1 shorter events, 0.0 us)
Async XLA Ops:
  3.1 18.7 %copy-start = (bf16[512,256]{1,0:T(8,128)(2,1)S(1)}, bf16[512,256]{1,0:T(8,128)(2,1)}, u32[]{:S(2)}) copy-start(bf16[512,256]{1,0:T(8,128)(2,1)} %constant.16.clone.table) | copy-start | bytes 786436
  3.1 18.7 %all-to-all-start = ((bf16[16,2,4,16,128]{4,3,2,1,0:T(8,128)(2,1)}), bf16[16,2,4,16,128]{4,3,2,1,0:T(8,128)(2,1)S(1)}, u32[]{:S(2)}, u32[]{:S(2)}) async-start(bf16[16,2,4,16,128]{4,3,2,1,0:T(8,128)(2,1)} %get-tuple-element.21), calls=%async_computation | async-start | bytes 1048576 | tf_op jit(solution)/shard_map/all_to_all | solution.py:365
  10.3 25.5 %collective-permute-start = (bf16[2,16,64,128]{3,2,1,0:T(8,128)(2,1)S(1)}, bf16[2,16,64,128]{3,2,1,0:T(8,128)(2,1)S(1)}, u32[]{:S(2)}, u32[]{:S(2)}) collective-permute-start(bf16[2,16,64,128]{3,2,1,0:T(8,128)(2,1)S(1)} %get-tuple-element.22.refs_1_), channel_id=1, source_target_pairs={{0,1},{1,2},{2,3},{3,4},{4,5},{5,6},{6,7},{8,9},{9,10},{10,11},{11... | collective-permute-start | bytes 1572872 | tf_op jit(solution)/shard_map/ppermute | solution.py:361
  12.2 0.7 copy-start.2
  23.6 13.9 %all-to-all-start.1 = ((bf16[16,2,4,16,128]{4,3,2,1,0:T(8,128)(2,1)}), bf16[16,2,4,16,128]{4,3,2,1,0:T(8,128)(2,1)S(1)}, u32[]{:S(2)}, u32[]{:S(2)}) async-start(bf16[16,2,4,16,128]{4,3,2,1,0:T(8,128)(2,1)} %self_energy.4), calls=%async_computation.1 | async-start | bytes 1048576 | tf_op jit(solution)/shard_map/all_to_all | solution.py:365
  27.2 10.3 %copy-start.1 = (f32[16]{0:T(128)S(1)}, f32[16]{0:T(128)}, u32[]{:S(2)}) copy-start(f32[16]{0:T(128)} %param.5) | copy-start | bytes 196
  27.2 8.5 %collective-permute-start.1 = (bf16[16,64,128]{2,1,0:T(8,128)(2,1)S(1)}, bf16[16,64,128]{2,1,0:T(8,128)(2,1)S(1)}, u32[]{:S(2)}, u32[]{:S(2)}) collective-permute-start(bf16[16,64,128]{2,1,0:T(8,128)(2,1)S(1)} %get-tuple-element.23.refs_2_), channel_id=1, source_target_pairs={{0,2},{1,3},{2,4},{3,5},{4,6},{5,7},{8,10},{9,11},{10,12},{11,13},... | collective-permute-start | bytes 786440 | tf_op jit(solution)/shard_map/ppermute | solution.py:361
  40.2 15.2 %all-to-all-start.2 = ((bf16[16,2,4,16,128]{4,3,2,1,0:T(8,128)(2,1)}), bf16[16,2,4,16,128]{4,3,2,1,0:T(8,128)(2,1)S(1)}, u32[]{:S(2)}, u32[]{:S(2)}) async-start(bf16[16,2,4,16,128]{4,3,2,1,0:T(8,128)(2,1)} %get-tuple-element.25), calls=%async_computation.2 | async-start | bytes 1048576 | tf_op jit(solution)/shard_map/all_to_all | solution.py:365
  45.3 23.8 %collective-permute-start.2 = (bf16[2,16,64,128]{3,2,1,0:T(8,128)(2,1)S(1)}, bf16[2,16,64,128]{3,2,1,0:T(8,128)(2,1)S(1)}, u32[]{:S(2)}, u32[]{:S(2)}) collective-permute-start(bf16[2,16,64,128]{3,2,1,0:T(8,128)(2,1)S(1)} %get-tuple-element.26.refs_1_), channel_id=1, source_target_pairs={{0,1},{1,2},{2,3},{3,4},{4,5},{5,6},{6,7},{8,9},{9,10},{10,11},{11... | collective-permute-start | bytes 1572872 | tf_op jit(solution)/shard_map/ppermute | solution.py:361
  57.2 13.7 %all-to-all-start.3 = ((bf16[16,2,4,16,128]{4,3,2,1,0:T(8,128)(2,1)}), bf16[16,2,4,16,128]{4,3,2,1,0:T(8,128)(2,1)S(1)}, u32[]{:S(2)}, u32[]{:S(2)}) async-start(bf16[16,2,4,16,128]{4,3,2,1,0:T(8,128)(2,1)} %self_energy.5), calls=%async_computation.3 | async-start | bytes 1048576 | tf_op jit(solution)/shard_map/all_to_all | solution.py:365
  60.8 8.3 %collective-permute-start.3 = (bf16[16,64,128]{2,1,0:T(8,128)(2,1)S(1)}, bf16[16,64,128]{2,1,0:T(8,128)(2,1)S(1)}, u32[]{:S(2)}, u32[]{:S(2)}) collective-permute-start(bf16[16,64,128]{2,1,0:T(8,128)(2,1)S(1)} %get-tuple-element.27.refs_2_), channel_id=1, source_target_pairs={{0,2},{1,3},{2,4},{3,5},{4,6},{5,7},{8,10},{9,11},{10,12},{11,13},... | collective-permute-start | bytes 786440 | tf_op jit(solution)/shard_map/ppermute | solution.py:361
  73.3 15.5 %all-to-all-start.4 = ((bf16[16,2,4,16,128]{4,3,2,1,0:T(8,128)(2,1)}), bf16[16,2,4,16,128]{4,3,2,1,0:T(8,128)(2,1)S(1)}, u32[]{:S(2)}, u32[]{:S(2)}) async-start(bf16[16,2,4,16,128]{4,3,2,1,0:T(8,128)(2,1)} %get-tuple-element.29), calls=%async_computation.4 | async-start | bytes 1048576 | tf_op jit(solution)/shard_map/all_to_all | solution.py:365
  78.6 23.8 %collective-permute-start.4 = (bf16[2,16,64,128]{3,2,1,0:T(8,128)(2,1)S(1)}, bf16[2,16,64,128]{3,2,1,0:T(8,128)(2,1)S(1)}, u32[]{:S(2)}, u32[]{:S(2)}) collective-permute-start(bf16[2,16,64,128]{3,2,1,0:T(8,128)(2,1)S(1)} %get-tuple-element.30.refs_1_), channel_id=1, source_target_pairs={{0,1},{1,2},{2,3},{3,4},{4,5},{5,6},{6,7},{8,9},{9,10},{10,11},{11... | collective-permute-start | bytes 1572872 | tf_op jit(solution)/shard_map/ppermute | solution.py:361
  90.6 13.6 %all-to-all-start.5 = ((bf16[16,2,4,16,128]{4,3,2,1,0:T(8,128)(2,1)}), bf16[16,2,4,16,128]{4,3,2,1,0:T(8,128)(2,1)S(1)}, u32[]{:S(2)}, u32[]{:S(2)}) async-start(bf16[16,2,4,16,128]{4,3,2,1,0:T(8,128)(2,1)} %self_energy.6), calls=%async_computation.5 | async-start | bytes 1048576 | tf_op jit(solution)/shard_map/all_to_all | solution.py:365
  94.2 8.3 %collective-permute-start.5 = (bf16[16,64,128]{2,1,0:T(8,128)(2,1)S(1)}, bf16[16,64,128]{2,1,0:T(8,128)(2,1)S(1)}, u32[]{:S(2)}, u32[]{:S(2)}) collective-permute-start(bf16[16,64,128]{2,1,0:T(8,128)(2,1)S(1)} %get-tuple-element.31.refs_2_), channel_id=1, source_target_pairs={{0,2},{1,3},{2,4},{3,5},{4,6},{5,7},{8,10},{9,11},{10,12},{11,13},... | collective-permute-start | bytes 786440 | tf_op jit(solution)/shard_map/ppermute | solution.py:361
  106.8 15.5 %all-to-all-start.6 = ((bf16[16,2,4,16,128]{4,3,2,1,0:T(8,128)(2,1)}), bf16[16,2,4,16,128]{4,3,2,1,0:T(8,128)(2,1)S(1)}, u32[]{:S(2)}, u32[]{:S(2)}) async-start(bf16[16,2,4,16,128]{4,3,2,1,0:T(8,128)(2,1)} %get-tuple-element.33), calls=%async_computation.6 | async-start | bytes 1048576 | tf_op jit(solution)/shard_map/all_to_all | solution.py:365
  112.2 23.8 %collective-permute-start.6 = (bf16[2,16,64,128]{3,2,1,0:T(8,128)(2,1)S(1)}, bf16[2,16,64,128]{3,2,1,0:T(8,128)(2,1)S(1)}, u32[]{:S(2)}, u32[]{:S(2)}) collective-permute-start(bf16[2,16,64,128]{3,2,1,0:T(8,128)(2,1)S(1)} %get-tuple-element.34.refs_1_), channel_id=1, source_target_pairs={{0,1},{1,2},{2,3},{3,4},{4,5},{5,6},{6,7},{8,9},{9,10},{10,11},{11... | collective-permute-start | bytes 1572872 | tf_op jit(solution)/shard_map/ppermute | solution.py:361
  124.1 13.7 %all-to-all-start.7 = ((bf16[16,2,4,16,128]{4,3,2,1,0:T(8,128)(2,1)}), bf16[16,2,4,16,128]{4,3,2,1,0:T(8,128)(2,1)S(1)}, u32[]{:S(2)}, u32[]{:S(2)}) async-start(bf16[16,2,4,16,128]{4,3,2,1,0:T(8,128)(2,1)} %self_energy.7), calls=%async_computation.7 | async-start | bytes 1048576 | tf_op jit(solution)/shard_map/all_to_all | solution.py:365
  127.7 8.3 %collective-permute-start.7 = (bf16[16,64,128]{2,1,0:T(8,128)(2,1)S(1)}, bf16[16,64,128]{2,1,0:T(8,128)(2,1)S(1)}, u32[]{:S(2)}, u32[]{:S(2)}) collective-permute-start(bf16[16,64,128]{2,1,0:T(8,128)(2,1)S(1)} %get-tuple-element.35.refs_2_), channel_id=1, source_target_pairs={{0,2},{1,3},{2,4},{3,5},{4,6},{5,7},{8,10},{9,11},{10,12},{11,13},... | collective-permute-start | bytes 786440 | tf_op jit(solution)/shard_map/ppermute | solution.py:361

commit v4 on v3

--- a/solution.py
+++ b/solution.py
@@ -174,14 +174,13 @@
                 value = turn_over(x[c, k])
                 y[c, k] = value
                 turned[c, pl.ds(k, ROWS, stride=PITCH), :] = value
+        save(0, q).start()
         return carry
 
     lax.fori_loop(0, STEPS, step, 0)
     for q in range(STEPS):
         pack_chunk(turned, block, q)
         chunk_copy(block, chunk, sem, q).start()
-    for q in range(STEPS):
-        save(0, q).start()
     emit(turned, near, far)
     for q in range(STEPS):
         chunk_copy(block, chunk, sem, q).wait()
@@ -254,9 +253,9 @@
             k = q * KB + i
             left = []
             for c in range(2):
-                memory = held[c, pl.ds(k, ROWS, stride=PITCH), :]
-                inner = jnp.where(own_side, memory, 0.0).astype(BF16)
-                outer = jnp.where(own_side, 0.0, memory).astype(BF16)
+                memory = held[c, pl.ds(k, ROWS, stride=PITCH), :].astype(BF16)
+                inner = only(own_side, memory)
+                outer = only(~own_side, memory)
                 left.append(jnp.concatenate([inner, outer[:, :ROWS]], 1))
             left = jnp.concatenate(left, 0)
             packed = far[k]

time: 142 us -> 142 us (level)
  no operation moved by 1% of the time
where the time goes in v4:
time: 142 us; the launch traced here: 140 us
  waiting for transfers between devices  68.5 us (48%)
  starting transfers between devices  50.2 us (35%)
  Pallas kernels  20.5 us (14%)
    all_to_all x8, waiting for transfers between devices, exchange(): return lax.all_to_all(block, 'ka', split_axis=0, concat_axis=0, tiled=True)  40.4 us
    all_to_all x8, starting transfers between devices, exchange(): return lax.all_to_all(block, 'ka', split_axis=0, concat_axis=0, tiled=True)  37.4 us
    ppermute x8, waiting for transfers between devices, from_behind(): lax.ppermute(block, 'ta', [(i - distance, i) for i in range(distance, cou...  28.1 us
    ppermute x8, starting transfers between devices, from_behind(): lax.ppermute(block, 'ta', [(i - distance, i) for i in range(distance, cou...  12.9 us
    pallas_call x4, Pallas kernels, stage(): pl.pallas_call(kernel, in_specs=in_specs, out_specs=spaces, out_shape=out...  10.2 us
    pallas_call x4, Pallas kernels, self_energy(): pl.pallas_call(self_energy_kernel, in_specs=[VMEM, VMEM, VMEM], out_specs...  7.3 us
    pallas_call x1, Pallas kernels, prepare(): pl.pallas_call(prepare_kernel, in_specs=[HBM], out_specs=[HBM, VMEM, VMEM...  2.93 us
  transfers between devices with their start and end apart: 16, of which 12 were waited for; matrix products, arithmetic and copies ran while one was open for 0% of the time, Pallas kernels for 5%

profile of v4, /device:TPU:96, one launch (start us, length us, event | category | flops | bytes accessed | tf_op | source)
XLA Modules:
  0.0 140.3 jit_solution(13881695165143477280)
XLA Ops:
  0.0 2.9 %prepare.1 = (f32[2,16,64,128]{3,2,1,0:T(8,128)}, bf16[2,16,64,128]{3,2,1,0:T(8,128)(2,1)S(1)}, bf16[16,64,128]{2,1,0:T(8,128)(2,1)S(1)}, bf16[16,2,4,16,128]{4,3,2,1,0:T(8,128)(2,1)}) custom-call(f32[2,16,64,128]{3,2,1,0:T(8,128)} %x_in.1), custom_call_target="tpu_custom_call" | custom-call | tf_op jit(solution)/shard_map/prepare/pallas_call | solution.py:205
  2.9 0.0 copy-start
  2.9 7.2 %all-to-all-start = ((bf16[16,2,4,16,128]{4,3,2,1,0:T(8,128)(2,1)}), bf16[16,2,4,16,128]{4,3,2,1,0:T(8,128)(2,1)S(1)}, u32[]{:S(2)}, u32[]{:S(2)}) async-start(bf16[16,2,4,16,128]{4,3,2,1,0:T(8,128)(2,1)} %get-tuple-element.21), calls=%async_computation | async-start | bytes 1048576 | tf_op jit(solution)/shard_map/all_to_all | solution.py:364
  10.1 1.9 %collective-permute-start = (bf16[2,16,64,128]{3,2,1,0:T(8,128)(2,1)S(1)}, bf16[2,16,64,128]{3,2,1,0:T(8,128)(2,1)S(1)}, u32[]{:S(2)}, u32[]{:S(2)}) collective-permute-start(bf16[2,16,64,128]{3,2,1,0:T(8,128)(2,1)S(1)} %get-tuple-element.22.refs_1_), channel_id=1, source_target_pairs={{0,1},{1,2},{2,3},{3,4},{4,5},{5,6},{6,7},{8,9},{9,10},{10,11},{11... | collective-permute-start | bytes 1572872 | tf_op jit(solution)/shard_map/ppermute | solution.py:360
  12.1 0.0 copy-start.2
  12.1 0.6 copy-done.2
  12.7 0.1 dynamic_slice.3
  12.8 0.1 fusion.keep
  12.9 8.7 %all-to-all-done.x = bf16[16,2,4,16,128]{4,3,2,1,0:T(8,128)(2,1)S(1)} async-done(((bf16[16,2,4,16,128]{4,3,2,1,0:T(8,128)(2,1)}), bf16[16,2,4,16,128]{4,3,2,1,0:T(8,128)(2,1)S(1)}, u32[]{:S(2)}, u32[]{:S(2)}) %all-to-all-start) | async-done | bytes 524320 | tf_op jit(solution)/shard_map/all_to_all | solution.py:364
  21.6 0.0 copy-done
  21.6 1.8 %self_energy.4 = bf16[16,2,4,16,128]{4,3,2,1,0:T(8,128)(2,1)} custom-call(f32[4,128]{1,0:T(4,128)S(1)} %fusion.keep, bf16[512,256]{1,0:T(8,128)(2,1)S(1)} %copy-done, bf16[16,2,4,16,128]{4,3,2,1,0:T(8,128)(2,1)S(1)} %all-to-all-done.x), custom_call_target="tpu_custom_call" | custom-call | tf_op jit(solution)/shard_map/self_energy/pallas_call | solution.py:108
  23.5 3.6 %all-to-all-start.1 = ((bf16[16,2,4,16,128]{4,3,2,1,0:T(8,128)(2,1)}), bf16[16,2,4,16,128]{4,3,2,1,0:T(8,128)(2,1)S(1)}, u32[]{:S(2)}, u32[]{:S(2)}) async-start(bf16[16,2,4,16,128]{4,3,2,1,0:T(8,128)(2,1)} %self_energy.4), calls=%async_computation.1 | async-start | bytes 1048576 | tf_op jit(solution)/shard_map/all_to_all | solution.py:364
  27.1 0.0 copy-start.1
  27.1 1.3 collective-permute-start.1
  28.4 7.2 %collective-permute-done.1.refs_4_ = bf16[16,64,128]{2,1,0:T(8,128)(2,1)S(1)} collective-permute-done((bf16[16,64,128]{2,1,0:T(8,128)(2,1)S(1)}, bf16[16,64,128]{2,1,0:T(8,128)(2,1)S(1)}, u32[]{:S(2)}, u32[]{:S(2)}) %collective-permute-start.1) | collective-permute-done | bytes 262176 | tf_op jit(solution)/shard_map/ppermute | solution.py:360
  35.6 0.0 collective-permute-done.refs_3_
  35.6 1.8 %all-to-all-done.1.refs_0_ = bf16[16,2,4,16,128]{4,3,2,1,0:T(8,128)(2,1)S(1)} async-done(((bf16[16,2,4,16,128]{4,3,2,1,0:T(8,128)(2,1)}), bf16[16,2,4,16,128]{4,3,2,1,0:T(8,128)(2,1)S(1)}, u32[]{:S(2)}, u32[]{:S(2)}) %all-to-all-start.1) | async-done | bytes 524320 | tf_op jit(solution)/shard_map/all_to_all | solution.py:364
  37.4 0.0 copy-done.1
  37.4 0.1 broadcast_in_dim.2.refs_6_
  37.5 2.5 %stage.4 = (f32[2,16,64,128]{3,2,1,0:T(8,128)}, bf16[2,16,64,128]{3,2,1,0:T(8,128)(2,1)S(1)}, bf16[16,64,128]{2,1,0:T(8,128)(2,1)S(1)}, bf16[16,2,4,16,128]{4,3,2,1,0:T(8,128)(2,1)}) custom-call(bf16[16,2,4,16,128]{4,3,2,1,0:T(8,128)(2,1)S(1)} %all-to-all-done.1.refs_0_, bf16[2,16,64,128]{3,2,1,0:T(8,128)(2,1)S(1)} %get-tuple-element.22.refs_1_, ...), custom_call_target="tpu_custom_call" | custom-call | tf_op jit(solution)/shard_map/stage/pallas_call | solution.py:347
  40.0 5.1 %all-to-all-start.2 = ((bf16[16,2,4,16,128]{4,3,2,1,0:T(8,128)(2,1)}), bf16[16,2,4,16,128]{4,3,2,1,0:T(8,128)(2,1)S(1)}, u32[]{:S(2)}, u32[]{:S(2)}) async-start(bf16[16,2,4,16,128]{4,3,2,1,0:T(8,128)(2,1)} %get-tuple-element.25), calls=%async_computation.2 | async-start | bytes 1048576 | tf_op jit(solution)/shard_map/all_to_all | solution.py:364
  45.1 1.9 %collective-permute-start.2 = (bf16[2,16,64,128]{3,2,1,0:T(8,128)(2,1)S(1)}, bf16[2,16,64,128]{3,2,1,0:T(8,128)(2,1)S(1)}, u32[]{:S(2)}, u32[]{:S(2)}) collective-permute-start(bf16[2,16,64,128]{3,2,1,0:T(8,128)(2,1)S(1)} %get-tuple-element.26.refs_1_), channel_id=1, source_target_pairs={{0,1},{1,2},{2,3},{3,4},{4,5},{5,6},{6,7},{8,9},{9,10},{10,11},{11... | collective-permute-start | bytes 1572872 | tf_op jit(solution)/shard_map/ppermute | solution.py:360
  47.1 8.2 %all-to-all-done.2.x = bf16[16,2,4,16,128]{4,3,2,1,0:T(8,128)(2,1)S(1)} async-done(((bf16[16,2,4,16,128]{4,3,2,1,0:T(8,128)(2,1)}), bf16[16,2,4,16,128]{4,3,2,1,0:T(8,128)(2,1)S(1)}, u32[]{:S(2)}, u32[]{:S(2)}) %all-to-all-start.2) | async-done | bytes 524320 | tf_op jit(solution)/shard_map/all_to_all | solution.py:364
  55.2 1.8 %self_energy.5 = bf16[16,2,4,16,128]{4,3,2,1,0:T(8,128)(2,1)} custom-call(f32[4,128]{1,0:T(4,128)S(1)} %fusion.keep, bf16[512,256]{1,0:T(8,128)(2,1)S(1)} %copy-done, bf16[16,2,4,16,128]{4,3,2,1,0:T(8,128)(2,1)S(1)} %all-to-all-done.2.x), custom_call_target="tpu_custom_call" | custom-call | tf_op jit(solution)/shard_map/self_energy/pallas_call | solution.py:108
  57.1 3.6 %all-to-all-start.3 = ((bf16[16,2,4,16,128]{4,3,2,1,0:T(8,128)(2,1)}), bf16[16,2,4,16,128]{4,3,2,1,0:T(8,128)(2,1)S(1)}, u32[]{:S(2)}, u32[]{:S(2)}) async-start(bf16[16,2,4,16,128]{4,3,2,1,0:T(8,128)(2,1)} %self_energy.5), calls=%async_computation.3 | async-start | bytes 1048576 | tf_op jit(solution)/shard_map/all_to_all | solution.py:364
  60.7 1.3 collective-permute-start.3
  62.0 7.0 %collective-permute-done.3.refs_4_ = bf16[16,64,128]{2,1,0:T(8,128)(2,1)S(1)} collective-permute-done((bf16[16,64,128]{2,1,0:T(8,128)(2,1)S(1)}, bf16[16,64,128]{2,1,0:T(8,128)(2,1)S(1)}, u32[]{:S(2)}, u32[]{:S(2)}) %collective-permute-start.3) | collective-permute-done | bytes 262176 | tf_op jit(solution)/shard_map/ppermute | solution.py:360
  68.9 0.0 collective-permute-done.2.refs_3_
  68.9 1.8 %all-to-all-done.3.refs_0_ = bf16[16,2,4,16,128]{4,3,2,1,0:T(8,128)(2,1)S(1)} async-done(((bf16[16,2,4,16,128]{4,3,2,1,0:T(8,128)(2,1)}), bf16[16,2,4,16,128]{4,3,2,1,0:T(8,128)(2,1)S(1)}, u32[]{:S(2)}, u32[]{:S(2)}) %all-to-all-start.3) | async-done | bytes 524320 | tf_op jit(solution)/shard_map/all_to_all | solution.py:364
  70.7 2.4 %stage.5 = (f32[2,16,64,128]{3,2,1,0:T(8,128)}, bf16[2,16,64,128]{3,2,1,0:T(8,128)(2,1)S(1)}, bf16[16,64,128]{2,1,0:T(8,128)(2,1)S(1)}, bf16[16,2,4,16,128]{4,3,2,1,0:T(8,128)(2,1)}) custom-call(bf16[16,2,4,16,128]{4,3,2,1,0:T(8,128)(2,1)S(1)} %all-to-all-done.3.refs_0_, bf16[2,16,64,128]{3,2,1,0:T(8,128)(2,1)S(1)} %get-tuple-element.26.refs_1_, ...), custom_call_target="tpu_custom_call" | custom-call | tf_op jit(solution)/shard_map/stage/pallas_call | solution.py:347
  73.1 5.4 %all-to-all-start.4 = ((bf16[16,2,4,16,128]{4,3,2,1,0:T(8,128)(2,1)}), bf16[16,2,4,16,128]{4,3,2,1,0:T(8,128)(2,1)S(1)}, u32[]{:S(2)}, u32[]{:S(2)}) async-start(bf16[16,2,4,16,128]{4,3,2,1,0:T(8,128)(2,1)} %get-tuple-element.29), calls=%async_computation.4 | async-start | bytes 1048576 | tf_op jit(solution)/shard_map/all_to_all | solution.py:364
  78.5 1.9 %collective-permute-start.4 = (bf16[2,16,64,128]{3,2,1,0:T(8,128)(2,1)S(1)}, bf16[2,16,64,128]{3,2,1,0:T(8,128)(2,1)S(1)}, u32[]{:S(2)}, u32[]{:S(2)}) collective-permute-start(bf16[2,16,64,128]{3,2,1,0:T(8,128)(2,1)S(1)} %get-tuple-element.30.refs_1_), channel_id=1, source_target_pairs={{0,1},{1,2},{2,3},{3,4},{4,5},{5,6},{6,7},{8,9},{9,10},{10,11},{11... | collective-permute-start | bytes 1572872 | tf_op jit(solution)/shard_map/ppermute | solution.py:360
  80.4 8.2 %all-to-all-done.4.x = bf16[16,2,4,16,128]{4,3,2,1,0:T(8,128)(2,1)S(1)} async-done(((bf16[16,2,4,16,128]{4,3,2,1,0:T(8,128)(2,1)}), bf16[16,2,4,16,128]{4,3,2,1,0:T(8,128)(2,1)S(1)}, u32[]{:S(2)}, u32[]{:S(2)}) %all-to-all-start.4) | async-done | bytes 524320 | tf_op jit(solution)/shard_map/all_to_all | solution.py:364
  88.6 1.8 %self_energy.6 = bf16[16,2,4,16,128]{4,3,2,1,0:T(8,128)(2,1)} custom-call(f32[4,128]{1,0:T(4,128)S(1)} %fusion.keep, bf16[512,256]{1,0:T(8,128)(2,1)S(1)} %copy-done, bf16[16,2,4,16,128]{4,3,2,1,0:T(8,128)(2,1)S(1)} %all-to-all-done.4.x), custom_call_target="tpu_custom_call" | custom-call | tf_op jit(solution)/shard_map/self_energy/pallas_call | solution.py:108
  90.4 3.6 %all-to-all-start.5 = ((bf16[16,2,4,16,128]{4,3,2,1,0:T(8,128)(2,1)}), bf16[16,2,4,16,128]{4,3,2,1,0:T(8,128)(2,1)S(1)}, u32[]{:S(2)}, u32[]{:S(2)}) async-start(bf16[16,2,4,16,128]{4,3,2,1,0:T(8,128)(2,1)} %self_energy.6), calls=%async_computation.5 | async-start | bytes 1048576 | tf_op jit(solution)/shard_map/all_to_all | solution.py:364
  94.0 1.3 collective-permute-start.5
  95.3 7.0 %collective-permute-done.5.refs_4_ = bf16[16,64,128]{2,1,0:T(8,128)(2,1)S(1)} collective-permute-done((bf16[16,64,128]{2,1,0:T(8,128)(2,1)S(1)}, bf16[16,64,128]{2,1,0:T(8,128)(2,1)S(1)}, u32[]{:S(2)}, u32[]{:S(2)}) %collective-permute-start.5) | collective-permute-done | bytes 262176 | tf_op jit(solution)/shard_map/ppermute | solution.py:360
  102.3 0.0 collective-permute-done.4.refs_3_
  102.3 1.8 %all-to-all-done.5.refs_0_ = bf16[16,2,4,16,128]{4,3,2,1,0:T(8,128)(2,1)S(1)} async-done(((bf16[16,2,4,16,128]{4,3,2,1,0:T(8,128)(2,1)}), bf16[16,2,4,16,128]{4,3,2,1,0:T(8,128)(2,1)S(1)}, u32[]{:S(2)}, u32[]{:S(2)}) %all-to-all-start.5) | async-done | bytes 524320 | tf_op jit(solution)/shard_map/all_to_all | solution.py:364
  104.1 2.5 %stage.6 = (f32[2,16,64,128]{3,2,1,0:T(8,128)}, bf16[2,16,64,128]{3,2,1,0:T(8,128)(2,1)S(1)}, bf16[16,64,128]{2,1,0:T(8,128)(2,1)S(1)}, bf16[16,2,4,16,128]{4,3,2,1,0:T(8,128)(2,1)}) custom-call(bf16[16,2,4,16,128]{4,3,2,1,0:T(8,128)(2,1)S(1)} %all-to-all-done.5.refs_0_, bf16[2,16,64,128]{3,2,1,0:T(8,128)(2,1)S(1)} %get-tuple-element.30.refs_1_, ...), custom_call_target="tpu_custom_call" | custom-call | tf_op jit(solution)/shard_map/stage/pallas_call | solution.py:347
  106.6 5.4 %all-to-all-start.6 = ((bf16[16,2,4,16,128]{4,3,2,1,0:T(8,128)(2,1)}), bf16[16,2,4,16,128]{4,3,2,1,0:T(8,128)(2,1)S(1)}, u32[]{:S(2)}, u32[]{:S(2)}) async-start(bf16[16,2,4,16,128]{4,3,2,1,0:T(8,128)(2,1)} %get-tuple-element.33), calls=%async_computation.6 | async-start | bytes 1048576 | tf_op jit(solution)/shard_map/all_to_all | solution.py:364
  112.0 1.9 %collective-permute-start.6 = (bf16[2,16,64,128]{3,2,1,0:T(8,128)(2,1)S(1)}, bf16[2,16,64,128]{3,2,1,0:T(8,128)(2,1)S(1)}, u32[]{:S(2)}, u32[]{:S(2)}) collective-permute-start(bf16[2,16,64,128]{3,2,1,0:T(8,128)(2,1)S(1)} %get-tuple-element.34.refs_1_), channel_id=1, source_target_pairs={{0,1},{1,2},{2,3},{3,4},{4,5},{5,6},{6,7},{8,9},{9,10},{10,11},{11... | collective-permute-start | bytes 1572872 | tf_op jit(solution)/shard_map/ppermute | solution.py:360
  113.9 8.2 %all-to-all-done.6.x = bf16[16,2,4,16,128]{4,3,2,1,0:T(8,128)(2,1)S(1)} async-done(((bf16[16,2,4,16,128]{4,3,2,1,0:T(8,128)(2,1)}), bf16[16,2,4,16,128]{4,3,2,1,0:T(8,128)(2,1)S(1)}, u32[]{:S(2)}, u32[]{:S(2)}) %all-to-all-start.6) | async-done | bytes 524320 | tf_op jit(solution)/shard_map/all_to_all | solution.py:364
  122.1 1.8 %self_energy.7 = bf16[16,2,4,16,128]{4,3,2,1,0:T(8,128)(2,1)} custom-call(f32[4,128]{1,0:T(4,128)S(1)} %fusion.keep, bf16[512,256]{1,0:T(8,128)(2,1)S(1)} %copy-done, bf16[16,2,4,16,128]{4,3,2,1,0:T(8,128)(2,1)S(1)} %all-to-all-done.6.x), custom_call_target="tpu_custom_call" | custom-call | tf_op jit(solution)/shard_map/self_energy/pallas_call | solution.py:108
  123.9 3.6 %all-to-all-start.7 = ((bf16[16,2,4,16,128]{4,3,2,1,0:T(8,128)(2,1)}), bf16[16,2,4,16,128]{4,3,2,1,0:T(8,128)(2,1)S(1)}, u32[]{:S(2)}, u32[]{:S(2)}) async-start(bf16[16,2,4,16,128]{4,3,2,1,0:T(8,128)(2,1)} %self_energy.7), calls=%async_computation.7 | async-start | bytes 1048576 | tf_op jit(solution)/shard_map/all_to_all | solution.py:364
  127.5 1.3 collective-permute-start.7
  128.8 7.0 %collective-permute-done.7.refs_4_ = bf16[16,64,128]{2,1,0:T(8,128)(2,1)S(1)} collective-permute-done((bf16[16,64,128]{2,1,0:T(8,128)(2,1)S(1)}, bf16[16,64,128]{2,1,0:T(8,128)(2,1)S(1)}, u32[]{:S(2)}, u32[]{:S(2)}) %collective-permute-start.7) | collective-permute-done | bytes 262176 | tf_op jit(solution)/shard_map/ppermute | solution.py:360
  135.8 0.0 collective-permute-done.6.refs_3_
  135.8 1.8 %all-to-all-done.7.refs_0_ = bf16[16,2,4,16,128]{4,3,2,1,0:T(8,128)(2,1)S(1)} async-done(((bf16[16,2,4,16,128]{4,3,2,1,0:T(8,128)(2,1)}), bf16[16,2,4,16,128]{4,3,2,1,0:T(8,128)(2,1)S(1)}, u32[]{:S(2)}, u32[]{:S(2)}) %all-to-all-start.7) | async-done | bytes 524320 | tf_op jit(solution)/shard_map/all_to_all | solution.py:364
  137.6 2.8 %stage.7 = f32[2,16,64,128]{3,2,1,0:T(8,128)} custom-call(bf16[16,2,4,16,128]{4,3,2,1,0:T(8,128)(2,1)S(1)} %all-to-all-done.7.refs_0_, bf16[2,16,64,128]{3,2,1,0:T(8,128)(2,1)S(1)} %get-tuple-element.34.refs_1_, bf16[16,64,128]{2,1,0:T(8,128)(2,1)S(1)} %get-tuple-element.35.refs_2_, bf16[2,16,64,128]{3,2,1,0:T(8,128)(2,1)S(1)} %collective-permute-done.6.refs_3_, ...), custom_call_target="tpu_custom_call" | custom-call | tf_op jit(solution)/shard_map/stage/pallas_call | solution.py:347
  (1 shorter events, 0.0 us)
Async XLA Ops:
  2.9 18.7 %copy-start = (bf16[512,256]{1,0:T(8,128)(2,1)S(1)}, bf16[512,256]{1,0:T(8,128)(2,1)}, u32[]{:S(2)}) copy-start(bf16[512,256]{1,0:T(8,128)(2,1)} %constant.16.clone.table) | copy-start | bytes 786436
  2.9 18.7 %all-to-all-start = ((bf16[16,2,4,16,128]{4,3,2,1,0:T(8,128)(2,1)}), bf16[16,2,4,16,128]{4,3,2,1,0:T(8,128)(2,1)S(1)}, u32[]{:S(2)}, u32[]{:S(2)}) async-start(bf16[16,2,4,16,128]{4,3,2,1,0:T(8,128)(2,1)} %get-tuple-element.21), calls=%async_computation | async-start | bytes 1048576 | tf_op jit(solution)/shard_map/all_to_all | solution.py:364
  10.1 25.5 %collective-permute-start = (bf16[2,16,64,128]{3,2,1,0:T(8,128)(2,1)S(1)}, bf16[2,16,64,128]{3,2,1,0:T(8,128)(2,1)S(1)}, u32[]{:S(2)}, u32[]{:S(2)}) collective-permute-start(bf16[2,16,64,128]{3,2,1,0:T(8,128)(2,1)S(1)} %get-tuple-element.22.refs_1_), channel_id=1, source_target_pairs={{0,1},{1,2},{2,3},{3,4},{4,5},{5,6},{6,7},{8,9},{9,10},{10,11},{11... | collective-permute-start | bytes 1572872 | tf_op jit(solution)/shard_map/ppermute | solution.py:360
  12.1 0.7 copy-start.2
  23.5 13.9 %all-to-all-start.1 = ((bf16[16,2,4,16,128]{4,3,2,1,0:T(8,128)(2,1)}), bf16[16,2,4,16,128]{4,3,2,1,0:T(8,128)(2,1)S(1)}, u32[]{:S(2)}, u32[]{:S(2)}) async-start(bf16[16,2,4,16,128]{4,3,2,1,0:T(8,128)(2,1)} %self_energy.4), calls=%async_computation.1 | async-start | bytes 1048576 | tf_op jit(solution)/shard_map/all_to_all | solution.py:364
  27.1 10.3 %copy-start.1 = (f32[16]{0:T(128)S(1)}, f32[16]{0:T(128)}, u32[]{:S(2)}) copy-start(f32[16]{0:T(128)} %param.5) | copy-start | bytes 196
  27.1 8.5 %collective-permute-start.1 = (bf16[16,64,128]{2,1,0:T(8,128)(2,1)S(1)}, bf16[16,64,128]{2,1,0:T(8,128)(2,1)S(1)}, u32[]{:S(2)}, u32[]{:S(2)}) collective-permute-start(bf16[16,64,128]{2,1,0:T(8,128)(2,1)S(1)} %get-tuple-element.23.refs_2_), channel_id=1, source_target_pairs={{0,2},{1,3},{2,4},{3,5},{4,6},{5,7},{8,10},{9,11},{10,12},{11,13},... | collective-permute-start | bytes 786440 | tf_op jit(solution)/shard_map/ppermute | solution.py:360
  40.0 15.2 %all-to-all-start.2 = ((bf16[16,2,4,16,128]{4,3,2,1,0:T(8,128)(2,1)}), bf16[16,2,4,16,128]{4,3,2,1,0:T(8,128)(2,1)S(1)}, u32[]{:S(2)}, u32[]{:S(2)}) async-start(bf16[16,2,4,16,128]{4,3,2,1,0:T(8,128)(2,1)} %get-tuple-element.25), calls=%async_computation.2 | async-start | bytes 1048576 | tf_op jit(solution)/shard_map/all_to_all | solution.py:364
  45.1 23.8 %collective-permute-start.2 = (bf16[2,16,64,128]{3,2,1,0:T(8,128)(2,1)S(1)}, bf16[2,16,64,128]{3,2,1,0:T(8,128)(2,1)S(1)}, u32[]{:S(2)}, u32[]{:S(2)}) collective-permute-start(bf16[2,16,64,128]{3,2,1,0:T(8,128)(2,1)S(1)} %get-tuple-element.26.refs_1_), channel_id=1, source_target_pairs={{0,1},{1,2},{2,3},{3,4},{4,5},{5,6},{6,7},{8,9},{9,10},{10,11},{11... | collective-permute-start | bytes 1572872 | tf_op jit(solution)/shard_map/ppermute | solution.py:360
  57.1 13.7 %all-to-all-start.3 = ((bf16[16,2,4,16,128]{4,3,2,1,0:T(8,128)(2,1)}), bf16[16,2,4,16,128]{4,3,2,1,0:T(8,128)(2,1)S(1)}, u32[]{:S(2)}, u32[]{:S(2)}) async-start(bf16[16,2,4,16,128]{4,3,2,1,0:T(8,128)(2,1)} %self_energy.5), calls=%async_computation.3 | async-start | bytes 1048576 | tf_op jit(solution)/shard_map/all_to_all | solution.py:364
  60.7 8.3 %collective-permute-start.3 = (bf16[16,64,128]{2,1,0:T(8,128)(2,1)S(1)}, bf16[16,64,128]{2,1,0:T(8,128)(2,1)S(1)}, u32[]{:S(2)}, u32[]{:S(2)}) collective-permute-start(bf16[16,64,128]{2,1,0:T(8,128)(2,1)S(1)} %get-tuple-element.27.refs_2_), channel_id=1, source_target_pairs={{0,2},{1,3},{2,4},{3,5},{4,6},{5,7},{8,10},{9,11},{10,12},{11,13},... | collective-permute-start | bytes 786440 | tf_op jit(solution)/shard_map/ppermute | solution.py:360
  73.1 15.5 %all-to-all-start.4 = ((bf16[16,2,4,16,128]{4,3,2,1,0:T(8,128)(2,1)}), bf16[16,2,4,16,128]{4,3,2,1,0:T(8,128)(2,1)S(1)}, u32[]{:S(2)}, u32[]{:S(2)}) async-start(bf16[16,2,4,16,128]{4,3,2,1,0:T(8,128)(2,1)} %get-tuple-element.29), calls=%async_computation.4 | async-start | bytes 1048576 | tf_op jit(solution)/shard_map/all_to_all | solution.py:364
  78.5 23.8 %collective-permute-start.4 = (bf16[2,16,64,128]{3,2,1,0:T(8,128)(2,1)S(1)}, bf16[2,16,64,128]{3,2,1,0:T(8,128)(2,1)S(1)}, u32[]{:S(2)}, u32[]{:S(2)}) collective-permute-start(bf16[2,16,64,128]{3,2,1,0:T(8,128)(2,1)S(1)} %get-tuple-element.30.refs_1_), channel_id=1, source_target_pairs={{0,1},{1,2},{2,3},{3,4},{4,5},{5,6},{6,7},{8,9},{9,10},{10,11},{11... | collective-permute-start | bytes 1572872 | tf_op jit(solution)/shard_map/ppermute | solution.py:360
  90.4 13.6 %all-to-all-start.5 = ((bf16[16,2,4,16,128]{4,3,2,1,0:T(8,128)(2,1)}), bf16[16,2,4,16,128]{4,3,2,1,0:T(8,128)(2,1)S(1)}, u32[]{:S(2)}, u32[]{:S(2)}) async-start(bf16[16,2,4,16,128]{4,3,2,1,0:T(8,128)(2,1)} %self_energy.6), calls=%async_computation.5 | async-start | bytes 1048576 | tf_op jit(solution)/shard_map/all_to_all | solution.py:364
  94.0 8.3 %collective-permute-start.5 = (bf16[16,64,128]{2,1,0:T(8,128)(2,1)S(1)}, bf16[16,64,128]{2,1,0:T(8,128)(2,1)S(1)}, u32[]{:S(2)}, u32[]{:S(2)}) collective-permute-start(bf16[16,64,128]{2,1,0:T(8,128)(2,1)S(1)} %get-tuple-element.31.refs_2_), channel_id=1, source_target_pairs={{0,2},{1,3},{2,4},{3,5},{4,6},{5,7},{8,10},{9,11},{10,12},{11,13},... | collective-permute-start | bytes 786440 | tf_op jit(solution)/shard_map/ppermute | solution.py:360
  106.6 15.5 %all-to-all-start.6 = ((bf16[16,2,4,16,128]{4,3,2,1,0:T(8,128)(2,1)}), bf16[16,2,4,16,128]{4,3,2,1,0:T(8,128)(2,1)S(1)}, u32[]{:S(2)}, u32[]{:S(2)}) async-start(bf16[16,2,4,16,128]{4,3,2,1,0:T(8,128)(2,1)} %get-tuple-element.33), calls=%async_computation.6 | async-start | bytes 1048576 | tf_op jit(solution)/shard_map/all_to_all | solution.py:364
  112.0 23.8 %collective-permute-start.6 = (bf16[2,16,64,128]{3,2,1,0:T(8,128)(2,1)S(1)}, bf16[2,16,64,128]{3,2,1,0:T(8,128)(2,1)S(1)}, u32[]{:S(2)}, u32[]{:S(2)}) collective-permute-start(bf16[2,16,64,128]{3,2,1,0:T(8,128)(2,1)S(1)} %get-tuple-element.34.refs_1_), channel_id=1, source_target_pairs={{0,1},{1,2},{2,3},{3,4},{4,5},{5,6},{6,7},{8,9},{9,10},{10,11},{11... | collective-permute-start | bytes 1572872 | tf_op jit(solution)/shard_map/ppermute | solution.py:360
  123.9 13.7 %all-to-all-start.7 = ((bf16[16,2,4,16,128]{4,3,2,1,0:T(8,128)(2,1)}), bf16[16,2,4,16,128]{4,3,2,1,0:T(8,128)(2,1)S(1)}, u32[]{:S(2)}, u32[]{:S(2)}) async-start(bf16[16,2,4,16,128]{4,3,2,1,0:T(8,128)(2,1)} %self_energy.7), calls=%async_computation.7 | async-start | bytes 1048576 | tf_op jit(solution)/shard_map/all_to_all | solution.py:364
  127.5 8.3 %collective-permute-start.7 = (bf16[16,64,128]{2,1,0:T(8,128)(2,1)S(1)}, bf16[16,64,128]{2,1,0:T(8,128)(2,1)S(1)}, u32[]{:S(2)}, u32[]{:S(2)}) collective-permute-start(bf16[16,64,128]{2,1,0:T(8,128)(2,1)S(1)} %get-tuple-element.35.refs_2_), channel_id=1, source_target_pairs={{0,2},{1,3},{2,4},{3,5},{4,6},{5,7},{8,10},{9,11},{10,12},{11,13},... | collective-permute-start | bytes 786440 | tf_op jit(solution)/shard_map/ppermute | solution.py:360

commit v5 on v4

--- a/solution.py
+++ b/solution.py
@@ -151,10 +151,10 @@
             k = q * 4 + i
             low = []
             for c in range(2):
-                value = turned[c, pl.ds(k, ROWS, stride=PITCH), :]
-                near[c, k] = value.astype(BF16)
-                low.append(jnp.where(causal, value, 0.0))
-            far[k] = (low[0] + half_turn(low[1])).astype(BF16)
+                value = turned[c, pl.ds(k, ROWS, stride=PITCH), :].astype(BF16)
+                near[c, k] = value
+                low.append(jnp.where(causal, value, jnp.zeros_like(value)))
+            far[k] = jnp.where(lane < ROWS, low[0], half_turn(low[1]))
         return carry
 
     lax.fori_loop(0, OWN // 4, step, 0)

time: 142 us -> 142 us (level)
  no operation moved by 1% of the time
where the time goes in v5:
time: 142 us; the launch traced here: 140 us
  waiting for transfers between devices  68.5 us (48%)
  starting transfers between devices  50.2 us (35%)
  Pallas kernels  20.5 us (14%)
    all_to_all x8, waiting for transfers between devices, exchange(): return lax.all_to_all(block, 'ka', split_axis=0, concat_axis=0, tiled=True)  40.4 us
    all_to_all x8, starting transfers between devices, exchange(): return lax.all_to_all(block, 'ka', split_axis=0, concat_axis=0, tiled=True)  37.4 us
    ppermute x8, waiting for transfers between devices, from_behind(): lax.ppermute(block, 'ta', [(i - distance, i) for i in range(distance, cou...  28.1 us
    ppermute x8, starting transfers between devices, from_behind(): lax.ppermute(block, 'ta', [(i - distance, i) for i in range(distance, cou...  12.9 us
    pallas_call x4, Pallas kernels, stage(): pl.pallas_call(kernel, in_specs=in_specs, out_specs=spaces, out_shape=out...  10.2 us
    pallas_call x4, Pallas kernels, self_energy(): pl.pallas_call(self_energy_kernel, in_specs=[VMEM, VMEM, VMEM], out_specs...  7.3 us
    pallas_call x1, Pallas kernels, prepare(): pl.pallas_call(prepare_kernel, in_specs=[HBM], out_specs=[HBM, VMEM, VMEM...  2.93 us
  transfers between devices with their start and end apart: 16, of which 12 were waited for; matrix products, arithmetic and copies ran while one was open for 0% of the time, Pallas kernels for 5%

profile of v5, /device:TPU:96, one launch (start us, length us, event | category | flops | bytes accessed | tf_op | source)
XLA Modules:
  0.0 140.3 jit_solution(13388335930702382776)
XLA Ops:
  0.0 2.9 %prepare.1 = (f32[2,16,64,128]{3,2,1,0:T(8,128)}, bf16[2,16,64,128]{3,2,1,0:T(8,128)(2,1)S(1)}, bf16[16,64,128]{2,1,0:T(8,128)(2,1)S(1)}, bf16[16,2,4,16,128]{4,3,2,1,0:T(8,128)(2,1)}) custom-call(f32[2,16,64,128]{3,2,1,0:T(8,128)} %x_in.1), custom_call_target="tpu_custom_call" | custom-call | tf_op jit(solution)/shard_map/prepare/pallas_call | solution.py:205
  2.9 0.0 copy-start
  2.9 7.2 %all-to-all-start = ((bf16[16,2,4,16,128]{4,3,2,1,0:T(8,128)(2,1)}), bf16[16,2,4,16,128]{4,3,2,1,0:T(8,128)(2,1)S(1)}, u32[]{:S(2)}, u32[]{:S(2)}) async-start(bf16[16,2,4,16,128]{4,3,2,1,0:T(8,128)(2,1)} %get-tuple-element.21), calls=%async_computation | async-start | bytes 1048576 | tf_op jit(solution)/shard_map/all_to_all | solution.py:364
  10.1 1.9 %collective-permute-start = (bf16[2,16,64,128]{3,2,1,0:T(8,128)(2,1)S(1)}, bf16[2,16,64,128]{3,2,1,0:T(8,128)(2,1)S(1)}, u32[]{:S(2)}, u32[]{:S(2)}) collective-permute-start(bf16[2,16,64,128]{3,2,1,0:T(8,128)(2,1)S(1)} %get-tuple-element.22.refs_1_), channel_id=1, source_target_pairs={{0,1},{1,2},{2,3},{3,4},{4,5},{5,6},{6,7},{8,9},{9,10},{10,11},{11... | collective-permute-start | bytes 1572872 | tf_op jit(solution)/shard_map/ppermute | solution.py:360
  12.1 0.0 copy-start.2
  12.1 0.6 copy-done.2
  12.7 0.1 dynamic_slice.3
  12.8 0.1 fusion.keep
  12.9 8.7 %all-to-all-done.x = bf16[16,2,4,16,128]{4,3,2,1,0:T(8,128)(2,1)S(1)} async-done(((bf16[16,2,4,16,128]{4,3,2,1,0:T(8,128)(2,1)}), bf16[16,2,4,16,128]{4,3,2,1,0:T(8,128)(2,1)S(1)}, u32[]{:S(2)}, u32[]{:S(2)}) %all-to-all-start) | async-done | bytes 524320 | tf_op jit(solution)/shard_map/all_to_all | solution.py:364
  21.6 0.0 copy-done
  21.6 1.8 %self_energy.4 = bf16[16,2,4,16,128]{4,3,2,1,0:T(8,128)(2,1)} custom-call(f32[4,128]{1,0:T(4,128)S(1)} %fusion.keep, bf16[512,256]{1,0:T(8,128)(2,1)S(1)} %copy-done, bf16[16,2,4,16,128]{4,3,2,1,0:T(8,128)(2,1)S(1)} %all-to-all-done.x), custom_call_target="tpu_custom_call" | custom-call | tf_op jit(solution)/shard_map/self_energy/pallas_call | solution.py:108
  23.5 3.6 %all-to-all-start.1 = ((bf16[16,2,4,16,128]{4,3,2,1,0:T(8,128)(2,1)}), bf16[16,2,4,16,128]{4,3,2,1,0:T(8,128)(2,1)S(1)}, u32[]{:S(2)}, u32[]{:S(2)}) async-start(bf16[16,2,4,16,128]{4,3,2,1,0:T(8,128)(2,1)} %self_energy.4), calls=%async_computation.1 | async-start | bytes 1048576 | tf_op jit(solution)/shard_map/all_to_all | solution.py:364
  27.1 0.0 copy-start.1
  27.1 1.3 collective-permute-start.1
  28.4 7.2 %collective-permute-done.1.refs_4_ = bf16[16,64,128]{2,1,0:T(8,128)(2,1)S(1)} collective-permute-done((bf16[16,64,128]{2,1,0:T(8,128)(2,1)S(1)}, bf16[16,64,128]{2,1,0:T(8,128)(2,1)S(1)}, u32[]{:S(2)}, u32[]{:S(2)}) %collective-permute-start.1) | collective-permute-done | bytes 262176 | tf_op jit(solution)/shard_map/ppermute | solution.py:360
  35.6 0.0 collective-permute-done.refs_3_
  35.6 1.8 %all-to-all-done.1.refs_0_ = bf16[16,2,4,16,128]{4,3,2,1,0:T(8,128)(2,1)S(1)} async-done(((bf16[16,2,4,16,128]{4,3,2,1,0:T(8,128)(2,1)}), bf16[16,2,4,16,128]{4,3,2,1,0:T(8,128)(2,1)S(1)}, u32[]{:S(2)}, u32[]{:S(2)}) %all-to-all-start.1) | async-done | bytes 524320 | tf_op jit(solution)/shard_map/all_to_all | solution.py:364
  37.4 0.0 copy-done.1
  37.4 0.1 broadcast_in_dim.2.refs_6_
  37.5 2.5 %stage.4 = (f32[2,16,64,128]{3,2,1,0:T(8,128)}, bf16[2,16,64,128]{3,2,1,0:T(8,128)(2,1)S(1)}, bf16[16,64,128]{2,1,0:T(8,128)(2,1)S(1)}, bf16[16,2,4,16,128]{4,3,2,1,0:T(8,128)(2,1)}) custom-call(bf16[16,2,4,16,128]{4,3,2,1,0:T(8,128)(2,1)S(1)} %all-to-all-done.1.refs_0_, bf16[2,16,64,128]{3,2,1,0:T(8,128)(2,1)S(1)} %get-tuple-element.22.refs_1_, ...), custom_call_target="tpu_custom_call" | custom-call | tf_op jit(solution)/shard_map/stage/pallas_call | solution.py:347
  40.0 5.1 %all-to-all-start.2 = ((bf16[16,2,4,16,128]{4,3,2,1,0:T(8,128)(2,1)}), bf16[16,2,4,16,128]{4,3,2,1,0:T(8,128)(2,1)S(1)}, u32[]{:S(2)}, u32[]{:S(2)}) async-start(bf16[16,2,4,16,128]{4,3,2,1,0:T(8,128)(2,1)} %get-tuple-element.25), calls=%async_computation.2 | async-start | bytes 1048576 | tf_op jit(solution)/shard_map/all_to_all | solution.py:364
  45.1 1.9 %collective-permute-start.2 = (bf16[2,16,64,128]{3,2,1,0:T(8,128)(2,1)S(1)}, bf16[2,16,64,128]{3,2,1,0:T(8,128)(2,1)S(1)}, u32[]{:S(2)}, u32[]{:S(2)}) collective-permute-start(bf16[2,16,64,128]{3,2,1,0:T(8,128)(2,1)S(1)} %get-tuple-element.26.refs_1_), channel_id=1, source_target_pairs={{0,1},{1,2},{2,3},{3,4},{4,5},{5,6},{6,7},{8,9},{9,10},{10,11},{11... | collective-permute-start | bytes 1572872 | tf_op jit(solution)/shard_map/ppermute | solution.py:360
  47.1 8.2 %all-to-all-done.2.x = bf16[16,2,4,16,128]{4,3,2,1,0:T(8,128)(2,1)S(1)} async-done(((bf16[16,2,4,16,128]{4,3,2,1,0:T(8,128)(2,1)}), bf16[16,2,4,16,128]{4,3,2,1,0:T(8,128)(2,1)S(1)}, u32[]{:S(2)}, u32[]{:S(2)}) %all-to-all-start.2) | async-done | bytes 524320 | tf_op jit(solution)/shard_map/all_to_all | solution.py:364
  55.2 1.8 %self_energy.5 = bf16[16,2,4,16,128]{4,3,2,1,0:T(8,128)(2,1)} custom-call(f32[4,128]{1,0:T(4,128)S(1)} %fusion.keep, bf16[512,256]{1,0:T(8,128)(2,1)S(1)} %copy-done, bf16[16,2,4,16,128]{4,3,2,1,0:T(8,128)(2,1)S(1)} %all-to-all-done.2.x), custom_call_target="tpu_custom_call" | custom-call | tf_op jit(solution)/shard_map/self_energy/pallas_call | solution.py:108
  57.1 3.6 %all-to-all-start.3 = ((bf16[16,2,4,16,128]{4,3,2,1,0:T(8,128)(2,1)}), bf16[16,2,4,16,128]{4,3,2,1,0:T(8,128)(2,1)S(1)}, u32[]{:S(2)}, u32[]{:S(2)}) async-start(bf16[16,2,4,16,128]{4,3,2,1,0:T(8,128)(2,1)} %self_energy.5), calls=%async_computation.3 | async-start | bytes 1048576 | tf_op jit(solution)/shard_map/all_to_all | solution.py:364
  60.6 1.3 collective-permute-start.3
  61.9 7.0 %collective-permute-done.3.refs_4_ = bf16[16,64,128]{2,1,0:T(8,128)(2,1)S(1)} collective-permute-done((bf16[16,64,128]{2,1,0:T(8,128)(2,1)S(1)}, bf16[16,64,128]{2,1,0:T(8,128)(2,1)S(1)}, u32[]{:S(2)}, u32[]{:S(2)}) %collective-permute-start.3) | collective-permute-done | bytes 262176 | tf_op jit(solution)/shard_map/ppermute | solution.py:360
  68.9 0.0 collective-permute-done.2.refs_3_
  68.9 1.8 %all-to-all-done.3.refs_0_ = bf16[16,2,4,16,128]{4,3,2,1,0:T(8,128)(2,1)S(1)} async-done(((bf16[16,2,4,16,128]{4,3,2,1,0:T(8,128)(2,1)}), bf16[16,2,4,16,128]{4,3,2,1,0:T(8,128)(2,1)S(1)}, u32[]{:S(2)}, u32[]{:S(2)}) %all-to-all-start.3) | async-done | bytes 524320 | tf_op jit(solution)/shard_map/all_to_all | solution.py:364
  70.7 2.4 %stage.5 = (f32[2,16,64,128]{3,2,1,0:T(8,128)}, bf16[2,16,64,128]{3,2,1,0:T(8,128)(2,1)S(1)}, bf16[16,64,128]{2,1,0:T(8,128)(2,1)S(1)}, bf16[16,2,4,16,128]{4,3,2,1,0:T(8,128)(2,1)}) custom-call(bf16[16,2,4,16,128]{4,3,2,1,0:T(8,128)(2,1)S(1)} %all-to-all-done.3.refs_0_, bf16[2,16,64,128]{3,2,1,0:T(8,128)(2,1)S(1)} %get-tuple-element.26.refs_1_, ...), custom_call_target="tpu_custom_call" | custom-call | tf_op jit(solution)/shard_map/stage/pallas_call | solution.py:347
  73.1 5.4 %all-to-all-start.4 = ((bf16[16,2,4,16,128]{4,3,2,1,0:T(8,128)(2,1)}), bf16[16,2,4,16,128]{4,3,2,1,0:T(8,128)(2,1)S(1)}, u32[]{:S(2)}, u32[]{:S(2)}) async-start(bf16[16,2,4,16,128]{4,3,2,1,0:T(8,128)(2,1)} %get-tuple-element.29), calls=%async_computation.4 | async-start | bytes 1048576 | tf_op jit(solution)/shard_map/all_to_all | solution.py:364
  78.5 1.9 %collective-permute-start.4 = (bf16[2,16,64,128]{3,2,1,0:T(8,128)(2,1)S(1)}, bf16[2,16,64,128]{3,2,1,0:T(8,128)(2,1)S(1)}, u32[]{:S(2)}, u32[]{:S(2)}) collective-permute-start(bf16[2,16,64,128]{3,2,1,0:T(8,128)(2,1)S(1)} %get-tuple-element.30.refs_1_), channel_id=1, source_target_pairs={{0,1},{1,2},{2,3},{3,4},{4,5},{5,6},{6,7},{8,9},{9,10},{10,11},{11... | collective-permute-start | bytes 1572872 | tf_op jit(solution)/shard_map/ppermute | solution.py:360
  80.4 8.2 %all-to-all-done.4.x = bf16[16,2,4,16,128]{4,3,2,1,0:T(8,128)(2,1)S(1)} async-done(((bf16[16,2,4,16,128]{4,3,2,1,0:T(8,128)(2,1)}), bf16[16,2,4,16,128]{4,3,2,1,0:T(8,128)(2,1)S(1)}, u32[]{:S(2)}, u32[]{:S(2)}) %all-to-all-start.4) | async-done | bytes 524320 | tf_op jit(solution)/shard_map/all_to_all | solution.py:364
  88.6 1.8 %self_energy.6 = bf16[16,2,4,16,128]{4,3,2,1,0:T(8,128)(2,1)} custom-call(f32[4,128]{1,0:T(4,128)S(1)} %fusion.keep, bf16[512,256]{1,0:T(8,128)(2,1)S(1)} %copy-done, bf16[16,2,4,16,128]{4,3,2,1,0:T(8,128)(2,1)S(1)} %all-to-all-done.4.x), custom_call_target="tpu_custom_call" | custom-call | tf_op jit(solution)/shard_map/self_energy/pallas_call | solution.py:108
  90.4 3.6 %all-to-all-start.5 = ((bf16[16,2,4,16,128]{4,3,2,1,0:T(8,128)(2,1)}), bf16[16,2,4,16,128]{4,3,2,1,0:T(8,128)(2,1)S(1)}, u32[]{:S(2)}, u32[]{:S(2)}) async-start(bf16[16,2,4,16,128]{4,3,2,1,0:T(8,128)(2,1)} %self_energy.6), calls=%async_computation.5 | async-start | bytes 1048576 | tf_op jit(solution)/shard_map/all_to_all | solution.py:364
  94.0 1.3 collective-permute-start.5
  95.3 7.0 %collective-permute-done.5.refs_4_ = bf16[16,64,128]{2,1,0:T(8,128)(2,1)S(1)} collective-permute-done((bf16[16,64,128]{2,1,0:T(8,128)(2,1)S(1)}, bf16[16,64,128]{2,1,0:T(8,128)(2,1)S(1)}, u32[]{:S(2)}, u32[]{:S(2)}) %collective-permute-start.5) | collective-permute-done | bytes 262176 | tf_op jit(solution)/shard_map/ppermute | solution.py:360
  102.3 0.0 collective-permute-done.4.refs_3_
  102.3 1.8 %all-to-all-done.5.refs_0_ = bf16[16,2,4,16,128]{4,3,2,1,0:T(8,128)(2,1)S(1)} async-done(((bf16[16,2,4,16,128]{4,3,2,1,0:T(8,128)(2,1)}), bf16[16,2,4,16,128]{4,3,2,1,0:T(8,128)(2,1)S(1)}, u32[]{:S(2)}, u32[]{:S(2)}) %all-to-all-start.5) | async-done | bytes 524320 | tf_op jit(solution)/shard_map/all_to_all | solution.py:364
  104.1 2.5 %stage.6 = (f32[2,16,64,128]{3,2,1,0:T(8,128)}, bf16[2,16,64,128]{3,2,1,0:T(8,128)(2,1)S(1)}, bf16[16,64,128]{2,1,0:T(8,128)(2,1)S(1)}, bf16[16,2,4,16,128]{4,3,2,1,0:T(8,128)(2,1)}) custom-call(bf16[16,2,4,16,128]{4,3,2,1,0:T(8,128)(2,1)S(1)} %all-to-all-done.5.refs_0_, bf16[2,16,64,128]{3,2,1,0:T(8,128)(2,1)S(1)} %get-tuple-element.30.refs_1_, ...), custom_call_target="tpu_custom_call" | custom-call | tf_op jit(solution)/shard_map/stage/pallas_call | solution.py:347
  106.6 5.4 %all-to-all-start.6 = ((bf16[16,2,4,16,128]{4,3,2,1,0:T(8,128)(2,1)}), bf16[16,2,4,16,128]{4,3,2,1,0:T(8,128)(2,1)S(1)}, u32[]{:S(2)}, u32[]{:S(2)}) async-start(bf16[16,2,4,16,128]{4,3,2,1,0:T(8,128)(2,1)} %get-tuple-element.33), calls=%async_computation.6 | async-start | bytes 1048576 | tf_op jit(solution)/shard_map/all_to_all | solution.py:364
  112.0 1.9 %collective-permute-start.6 = (bf16[2,16,64,128]{3,2,1,0:T(8,128)(2,1)S(1)}, bf16[2,16,64,128]{3,2,1,0:T(8,128)(2,1)S(1)}, u32[]{:S(2)}, u32[]{:S(2)}) collective-permute-start(bf16[2,16,64,128]{3,2,1,0:T(8,128)(2,1)S(1)} %get-tuple-element.34.refs_1_), channel_id=1, source_target_pairs={{0,1},{1,2},{2,3},{3,4},{4,5},{5,6},{6,7},{8,9},{9,10},{10,11},{11... | collective-permute-start | bytes 1572872 | tf_op jit(solution)/shard_map/ppermute | solution.py:360
  113.9 8.2 %all-to-all-done.6.x = bf16[16,2,4,16,128]{4,3,2,1,0:T(8,128)(2,1)S(1)} async-done(((bf16[16,2,4,16,128]{4,3,2,1,0:T(8,128)(2,1)}), bf16[16,2,4,16,128]{4,3,2,1,0:T(8,128)(2,1)S(1)}, u32[]{:S(2)}, u32[]{:S(2)}) %all-to-all-start.6) | async-done | bytes 524320 | tf_op jit(solution)/shard_map/all_to_all | solution.py:364
  122.1 1.8 %self_energy.7 = bf16[16,2,4,16,128]{4,3,2,1,0:T(8,128)(2,1)} custom-call(f32[4,128]{1,0:T(4,128)S(1)} %fusion.keep, bf16[512,256]{1,0:T(8,128)(2,1)S(1)} %copy-done, bf16[16,2,4,16,128]{4,3,2,1,0:T(8,128)(2,1)S(1)} %all-to-all-done.6.x), custom_call_target="tpu_custom_call" | custom-call | tf_op jit(solution)/shard_map/self_energy/pallas_call | solution.py:108
  123.9 3.6 %all-to-all-start.7 = ((bf16[16,2,4,16,128]{4,3,2,1,0:T(8,128)(2,1)}), bf16[16,2,4,16,128]{4,3,2,1,0:T(8,128)(2,1)S(1)}, u32[]{:S(2)}, u32[]{:S(2)}) async-start(bf16[16,2,4,16,128]{4,3,2,1,0:T(8,128)(2,1)} %self_energy.7), calls=%async_computation.7 | async-start | bytes 1048576 | tf_op jit(solution)/shard_map/all_to_all | solution.py:364
  127.5 1.3 collective-permute-start.7
  128.8 7.0 %collective-permute-done.7.refs_4_ = bf16[16,64,128]{2,1,0:T(8,128)(2,1)S(1)} collective-permute-done((bf16[16,64,128]{2,1,0:T(8,128)(2,1)S(1)}, bf16[16,64,128]{2,1,0:T(8,128)(2,1)S(1)}, u32[]{:S(2)}, u32[]{:S(2)}) %collective-permute-start.7) | collective-permute-done | bytes 262176 | tf_op jit(solution)/shard_map/ppermute | solution.py:360
  135.8 0.0 collective-permute-done.6.refs_3_
  135.8 1.8 %all-to-all-done.7.refs_0_ = bf16[16,2,4,16,128]{4,3,2,1,0:T(8,128)(2,1)S(1)} async-done(((bf16[16,2,4,16,128]{4,3,2,1,0:T(8,128)(2,1)}), bf16[16,2,4,16,128]{4,3,2,1,0:T(8,128)(2,1)S(1)}, u32[]{:S(2)}, u32[]{:S(2)}) %all-to-all-start.7) | async-done | bytes 524320 | tf_op jit(solution)/shard_map/all_to_all | solution.py:364
  137.5 2.8 %stage.7 = f32[2,16,64,128]{3,2,1,0:T(8,128)} custom-call(bf16[16,2,4,16,128]{4,3,2,1,0:T(8,128)(2,1)S(1)} %all-to-all-done.7.refs_0_, bf16[2,16,64,128]{3,2,1,0:T(8,128)(2,1)S(1)} %get-tuple-element.34.refs_1_, bf16[16,64,128]{2,1,0:T(8,128)(2,1)S(1)} %get-tuple-element.35.refs_2_, bf16[2,16,64,128]{3,2,1,0:T(8,128)(2,1)S(1)} %collective-permute-done.6.refs_3_, ...), custom_call_target="tpu_custom_call" | custom-call | tf_op jit(solution)/shard_map/stage/pallas_call | solution.py:347
  (1 shorter events, 0.0 us)
Async XLA Ops:
  2.9 18.7 %copy-start = (bf16[512,256]{1,0:T(8,128)(2,1)S(1)}, bf16[512,256]{1,0:T(8,128)(2,1)}, u32[]{:S(2)}) copy-start(bf16[512,256]{1,0:T(8,128)(2,1)} %constant.16.clone.table) | copy-start | bytes 786436
  2.9 18.7 %all-to-all-start = ((bf16[16,2,4,16,128]{4,3,2,1,0:T(8,128)(2,1)}), bf16[16,2,4,16,128]{4,3,2,1,0:T(8,128)(2,1)S(1)}, u32[]{:S(2)}, u32[]{:S(2)}) async-start(bf16[16,2,4,16,128]{4,3,2,1,0:T(8,128)(2,1)} %get-tuple-element.21), calls=%async_computation | async-start | bytes 1048576 | tf_op jit(solution)/shard_map/all_to_all | solution.py:364
  10.1 25.5 %collective-permute-start = (bf16[2,16,64,128]{3,2,1,0:T(8,128)(2,1)S(1)}, bf16[2,16,64,128]{3,2,1,0:T(8,128)(2,1)S(1)}, u32[]{:S(2)}, u32[]{:S(2)}) collective-permute-start(bf16[2,16,64,128]{3,2,1,0:T(8,128)(2,1)S(1)} %get-tuple-element.22.refs_1_), channel_id=1, source_target_pairs={{0,1},{1,2},{2,3},{3,4},{4,5},{5,6},{6,7},{8,9},{9,10},{10,11},{11... | collective-permute-start | bytes 1572872 | tf_op jit(solution)/shard_map/ppermute | solution.py:360
  12.1 0.7 copy-start.2
  23.5 13.9 %all-to-all-start.1 = ((bf16[16,2,4,16,128]{4,3,2,1,0:T(8,128)(2,1)}), bf16[16,2,4,16,128]{4,3,2,1,0:T(8,128)(2,1)S(1)}, u32[]{:S(2)}, u32[]{:S(2)}) async-start(bf16[16,2,4,16,128]{4,3,2,1,0:T(8,128)(2,1)} %self_energy.4), calls=%async_computation.1 | async-start | bytes 1048576 | tf_op jit(solution)/shard_map/all_to_all | solution.py:364
  27.1 10.3 %copy-start.1 = (f32[16]{0:T(128)S(1)}, f32[16]{0:T(128)}, u32[]{:S(2)}) copy-start(f32[16]{0:T(128)} %param.5) | copy-start | bytes 196
  27.1 8.5 %collective-permute-start.1 = (bf16[16,64,128]{2,1,0:T(8,128)(2,1)S(1)}, bf16[16,64,128]{2,1,0:T(8,128)(2,1)S(1)}, u32[]{:S(2)}, u32[]{:S(2)}) collective-permute-start(bf16[16,64,128]{2,1,0:T(8,128)(2,1)S(1)} %get-tuple-element.23.refs_2_), channel_id=1, source_target_pairs={{0,2},{1,3},{2,4},{3,5},{4,6},{5,7},{8,10},{9,11},{10,12},{11,13},... | collective-permute-start | bytes 786440 | tf_op jit(solution)/shard_map/ppermute | solution.py:360
  40.0 15.2 %all-to-all-start.2 = ((bf16[16,2,4,16,128]{4,3,2,1,0:T(8,128)(2,1)}), bf16[16,2,4,16,128]{4,3,2,1,0:T(8,128)(2,1)S(1)}, u32[]{:S(2)}, u32[]{:S(2)}) async-start(bf16[16,2,4,16,128]{4,3,2,1,0:T(8,128)(2,1)} %get-tuple-element.25), calls=%async_computation.2 | async-start | bytes 1048576 | tf_op jit(solution)/shard_map/all_to_all | solution.py:364
  45.1 23.8 %collective-permute-start.2 = (bf16[2,16,64,128]{3,2,1,0:T(8,128)(2,1)S(1)}, bf16[2,16,64,128]{3,2,1,0:T(8,128)(2,1)S(1)}, u32[]{:S(2)}, u32[]{:S(2)}) collective-permute-start(bf16[2,16,64,128]{3,2,1,0:T(8,128)(2,1)S(1)} %get-tuple-element.26.refs_1_), channel_id=1, source_target_pairs={{0,1},{1,2},{2,3},{3,4},{4,5},{5,6},{6,7},{8,9},{9,10},{10,11},{11... | collective-permute-start | bytes 1572872 | tf_op jit(solution)/shard_map/ppermute | solution.py:360
  57.1 13.7 %all-to-all-start.3 = ((bf16[16,2,4,16,128]{4,3,2,1,0:T(8,128)(2,1)}), bf16[16,2,4,16,128]{4,3,2,1,0:T(8,128)(2,1)S(1)}, u32[]{:S(2)}, u32[]{:S(2)}) async-start(bf16[16,2,4,16,128]{4,3,2,1,0:T(8,128)(2,1)} %self_energy.5), calls=%async_computation.3 | async-start | bytes 1048576 | tf_op jit(solution)/shard_map/all_to_all | solution.py:364
  60.6 8.3 %collective-permute-start.3 = (bf16[16,64,128]{2,1,0:T(8,128)(2,1)S(1)}, bf16[16,64,128]{2,1,0:T(8,128)(2,1)S(1)}, u32[]{:S(2)}, u32[]{:S(2)}) collective-permute-start(bf16[16,64,128]{2,1,0:T(8,128)(2,1)S(1)} %get-tuple-element.27.refs_2_), channel_id=1, source_target_pairs={{0,2},{1,3},{2,4},{3,5},{4,6},{5,7},{8,10},{9,11},{10,12},{11,13},... | collective-permute-start | bytes 786440 | tf_op jit(solution)/shard_map/ppermute | solution.py:360
  73.1 15.5 %all-to-all-start.4 = ((bf16[16,2,4,16,128]{4,3,2,1,0:T(8,128)(2,1)}), bf16[16,2,4,16,128]{4,3,2,1,0:T(8,128)(2,1)S(1)}, u32[]{:S(2)}, u32[]{:S(2)}) async-start(bf16[16,2,4,16,128]{4,3,2,1,0:T(8,128)(2,1)} %get-tuple-element.29), calls=%async_computation.4 | async-start | bytes 1048576 | tf_op jit(solution)/shard_map/all_to_all | solution.py:364
  78.5 23.8 %collective-permute-start.4 = (bf16[2,16,64,128]{3,2,1,0:T(8,128)(2,1)S(1)}, bf16[2,16,64,128]{3,2,1,0:T(8,128)(2,1)S(1)}, u32[]{:S(2)}, u32[]{:S(2)}) collective-permute-start(bf16[2,16,64,128]{3,2,1,0:T(8,128)(2,1)S(1)} %get-tuple-element.30.refs_1_), channel_id=1, source_target_pairs={{0,1},{1,2},{2,3},{3,4},{4,5},{5,6},{6,7},{8,9},{9,10},{10,11},{11... | collective-permute-start | bytes 1572872 | tf_op jit(solution)/shard_map/ppermute | solution.py:360
  90.4 13.6 %all-to-all-start.5 = ((bf16[16,2,4,16,128]{4,3,2,1,0:T(8,128)(2,1)}), bf16[16,2,4,16,128]{4,3,2,1,0:T(8,128)(2,1)S(1)}, u32[]{:S(2)}, u32[]{:S(2)}) async-start(bf16[16,2,4,16,128]{4,3,2,1,0:T(8,128)(2,1)} %self_energy.6), calls=%async_computation.5 | async-start | bytes 1048576 | tf_op jit(solution)/shard_map/all_to_all | solution.py:364
  94.0 8.3 %collective-permute-start.5 = (bf16[16,64,128]{2,1,0:T(8,128)(2,1)S(1)}, bf16[16,64,128]{2,1,0:T(8,128)(2,1)S(1)}, u32[]{:S(2)}, u32[]{:S(2)}) collective-permute-start(bf16[16,64,128]{2,1,0:T(8,128)(2,1)S(1)} %get-tuple-element.31.refs_2_), channel_id=1, source_target_pairs={{0,2},{1,3},{2,4},{3,5},{4,6},{5,7},{8,10},{9,11},{10,12},{11,13},... | collective-permute-start | bytes 786440 | tf_op jit(solution)/shard_map/ppermute | solution.py:360
  106.6 15.5 %all-to-all-start.6 = ((bf16[16,2,4,16,128]{4,3,2,1,0:T(8,128)(2,1)}), bf16[16,2,4,16,128]{4,3,2,1,0:T(8,128)(2,1)S(1)}, u32[]{:S(2)}, u32[]{:S(2)}) async-start(bf16[16,2,4,16,128]{4,3,2,1,0:T(8,128)(2,1)} %get-tuple-element.33), calls=%async_computation.6 | async-start | bytes 1048576 | tf_op jit(solution)/shard_map/all_to_all | solution.py:364
  112.0 23.8 %collective-permute-start.6 = (bf16[2,16,64,128]{3,2,1,0:T(8,128)(2,1)S(1)}, bf16[2,16,64,128]{3,2,1,0:T(8,128)(2,1)S(1)}, u32[]{:S(2)}, u32[]{:S(2)}) collective-permute-start(bf16[2,16,64,128]{3,2,1,0:T(8,128)(2,1)S(1)} %get-tuple-element.34.refs_1_), channel_id=1, source_target_pairs={{0,1},{1,2},{2,3},{3,4},{4,5},{5,6},{6,7},{8,9},{9,10},{10,11},{11... | collective-permute-start | bytes 1572872 | tf_op jit(solution)/shard_map/ppermute | solution.py:360
  123.9 13.7 %all-to-all-start.7 = ((bf16[16,2,4,16,128]{4,3,2,1,0:T(8,128)(2,1)}), bf16[16,2,4,16,128]{4,3,2,1,0:T(8,128)(2,1)S(1)}, u32[]{:S(2)}, u32[]{:S(2)}) async-start(bf16[16,2,4,16,128]{4,3,2,1,0:T(8,128)(2,1)} %self_energy.7), calls=%async_computation.7 | async-start | bytes 1048576 | tf_op jit(solution)/shard_map/all_to_all | solution.py:364
  127.5 8.3 %collective-permute-start.7 = (bf16[16,64,128]{2,1,0:T(8,128)(2,1)S(1)}, bf16[16,64,128]{2,1,0:T(8,128)(2,1)S(1)}, u32[]{:S(2)}, u32[]{:S(2)}) collective-permute-start(bf16[16,64,128]{2,1,0:T(8,128)(2,1)S(1)} %get-tuple-element.35.refs_2_), channel_id=1, source_target_pairs={{0,2},{1,3},{2,4},{3,5},{4,6},{5,7},{8,10},{9,11},{10,12},{11,13},... | collective-permute-start | bytes 786440 | tf_op jit(solution)/shard_map/ppermute | solution.py:360
